TPU v7x, 128 devices: a whole 4x4x4 slice. The times are simulated.
128 devices in a mesh: seq: 64 (over x, z, y), mp: 2 (over core).
Axes of the slice: x: 4, y: 4, z: 4, core: 2. Of those that a mesh axis runs over, the one named last changes fastest.
Arguments:
- tokens: bfloat16 [8192, 2688], P('seq'), may hold values from -16 to 16
- tangent: bfloat16 [8192, 2688], P('seq'), may hold values from -6 to 6
- w_query: bfloat16 [2688, 2048], P(None, 'mp'), may hold values from -0.078116071 to 0.078116071
- w_key: bfloat16 [2688, 1024], P(None, 'mp'), may hold values from -0.078116071 to 0.078116071
- value_weight: bfloat16 [2688, 1024], P(None, 'mp'), may hold values from -0.125 to 0.125
- w_out: bfloat16 [2048, 2688], P('mp'), may hold values from -0.125 to 0.125
Outputs:
- input_grad: bfloat16 [8192, 2688], P('seq', 'mp')
- weight_grad: float32 [2688, 2, 1024], P('seq', None, 'mp')
All inputs are finite; a program needn't handle non-finite values.
Results may differ from a plain program's by a relative error of at most 0.011.
Values may be sent and summed in bfloat16 or wider, within the bound.
No kernel may reach another device: no remote copies, remote signals or barrier semaphores. Data moves between devices by JAX's collectives and lax.ppermute only.
A program may use at most 128 MiB of HBM per device.

v0:
```python
import math

import jax
import jax.numpy as jnp
from jax import lax
from jax.experimental import pallas as pl
from jax.experimental.pallas import tpu as pltpu
from jax.sharding import PartitionSpec as P

BF = jnp.bfloat16
F32 = jnp.float32
HEAD = 128
SCALE = 168.0 ** (-0.5)
SCALE2 = SCALE * math.log2(math.e)
PIECE = 42


NT = (((1,), (1,)), ((), ()))
TN = (((0,), (0,)), ((), ()))
NN = (((1,), (0,)), ((), ()))


def mm(a, b, dims=NN):
    return lax.dot_general(a, b, dims, preferred_element_type=F32)


def ring_y(x, d):
    return lax.ppermute(x, "seq", [(i, i // 4 * 4 + (i + d) % 4) for i in range(64)])


def ring_z(x, d):
    return lax.ppermute(
        x, "seq", [(i, i // 16 * 16 + (i // 4 + d) % 4 * 4 + i % 4) for i in range(64)]
    )


def ring_x(x, d):
    return lax.ppermute(x, "seq", [(i, (i // 16 + d) % 4 * 16 + i % 16) for i in range(64)])


def lines_on(x, d):
    return lax.ppermute(x, "seq", [(i, i + 4 * d) for i in range(64) if 0 <= i + 4 * d < 64])


def exchange(ring, chunks):
    got = {d: ring(chunks[d], d) for d in (1, 3, 2)}
    return [chunks[0], got[1], got[2], got[3]]


def other_core(x):
    return lax.ppermute(x, "mp", [(0, 1), (1, 0)])


def call(kernel, grid, ins, outs, scratch=(), flops=0, moved=0, limit=20):
    specs_in, values = zip(*ins[1:])
    specs_out, shapes = zip(*outs)
    return pl.pallas_call(
        kernel,
        grid_spec=pltpu.PrefetchScalarGridSpec(
            num_scalar_prefetch=1,
            grid=grid,
            in_specs=list(specs_in),
            out_specs=list(specs_out),
            scratch_shapes=list(scratch),
        ),
        out_shape=list(shapes),
        compiler_params=pltpu.CompilerParams(
            dimension_semantics=("arbitrary",) * len(grid), vmem_limit_bytes=limit << 20
        ),
        cost_estimate=pl.CostEstimate(flops=flops, bytes_accessed=moved, transcendentals=0),
    )(ins[0], *values)


def flat_call(kernel, ins, outs, scratch=(), flops=0, moved=0, limit=20):
    specs_in, values = zip(*ins[1:])
    _, shapes = zip(*outs)
    return pl.pallas_call(
        kernel,
        in_specs=[pl.BlockSpec(memory_space=pltpu.SMEM)] + list(specs_in),
        out_specs=[pl.BlockSpec(memory_space=pltpu.VMEM)] * len(shapes),
        scratch_shapes=list(scratch),
        out_shape=list(shapes),
        compiler_params=pltpu.CompilerParams(vmem_limit_bytes=limit << 20),
        cost_estimate=pl.CostEstimate(flops=flops, bytes_accessed=moved, transcendentals=0),
    )(ins[0], *values)


def whole(shape):
    return pl.BlockSpec(shape, lambda *_: (0,) * len(shape))


def hbm():
    return pl.BlockSpec(memory_space=pl.ANY)


def far_memory():
    return pl.BlockSpec(memory_space=pltpu.HBM)


def vmem():
    return pl.BlockSpec(memory_space=pltpu.VMEM)


def out(shape, dtype):
    return whole(shape), jax.ShapeDtypeStruct(shape, dtype)


def load_inputs(tok, tan, both, sem):
    rows = tok.shape[0]
    return [
        pltpu.make_async_copy(tok, both.at[pl.ds(0, rows)], sem.at[0]),
        pltpu.make_async_copy(tan, both.at[pl.ds(rows, rows)], sem.at[1]),
    ]


def key_value_kernel(pos, tok, tan, wk, wv, *refs):
    outs, (both, w, sem) = refs[:4], refs[4:]
    rows = tok.shape[0]
    copies = load_inputs(tok, tan, both, sem)
    for d in range(4):
        cols = pl.ds(pl.multiple_of(lax.rem(pos[2] + d, 4) * HEAD, HEAD), HEAD)
        for j, src in enumerate((wk, wv)):
            copies.append(
                pltpu.make_async_copy(
                    src.at[:, cols], w.at[d, :, pl.ds(j * HEAD, HEAD)], sem.at[2 + 2 * d + j]
                )
            )
    for c in copies[:6]:
        c.start()
    copies[0].wait()
    copies[1].wait()
    for d in range(4):
        copies[2 + 2 * d].wait()
        copies[3 + 2 * d].wait()
        for c in copies[6 + 2 * d : 8 + 2 * d]:
            c.start()
        res = mm(both[...], w[d]).astype(BF)
        outs[d][0] = res[:rows, :HEAD]
        outs[d][1] = res[rows:, :HEAD]
        outs[d][2] = res[:rows, HEAD:]
        outs[d][3] = res[rows:, HEAD:]


def query_kernel(pos, tok, tan, w, *refs):
    outs, both = refs[:4], refs[4]
    rows = tok.shape[0]
    both[:rows] = tok[...]
    both[rows:] = tan[...]
    for d in range(4):
        cols = pl.ds(pl.multiple_of(lax.rem(pos[2] + d, 4) * 256, 256), 256)
        res = mm(both[...], w[:, cols]).astype(BF)
        outs[d][0] = res[:rows]
        outs[d][1] = res[rows:]


def join_kernel(pos, a, b, c, e, res):
    res[0] = a[...]
    res[1] = b[...]
    res[2] = c[...]
    res[3] = e[...]


def two_heads(block):
    return jnp.concatenate([block[:, :HEAD], block[:, HEAD:]], axis=0)


def forward_kernel(pos, *refs):
    lines = refs[:3]
    q_refs = refs[3:7]
    o0, o1, o2, o3, k_all, v_all, q_all, p_all, kkd, vvd, qbuf, sems = refs[-12:]
    outs = (o0, o1, o2, o3)
    b = pl.program_id(0)
    y = pos[2]

    @pl.when(b == 0)
    def _():
        copies = []
        for line in range(3):
            for d in range(4):
                row = pl.multiple_of((lax.rem(y + 4 - d, 4) + 4 * line) * HEAD, HEAD)
                src = lines[line].at[d]
                for part in range(4):
                    dst = kkd if part < 2 else vvd
                    copies.append(
                        pltpu.make_async_copy(
                            src.at[part],
                            dst.at[pl.ds(row, HEAD), pl.ds(part % 2 * HEAD, HEAD)],
                            sems.at[line * 16 + d * 4 + part],
                        )
                    )
        for d in range(4):
            copies.append(
                pltpu.make_async_copy(
                    q_refs[d], qbuf.at[lax.rem(y + 4 - d, 4)], sems.at[48 + d]
                )
            )
        for c in copies:
            c.start()
        for c in copies:
            c.wait()
        k_all[...] = kkd[:, :HEAD]
        v_all[...] = vvd[:, :HEAD]

    rows = pl.ds(pl.multiple_of(b * HEAD, HEAD), 9 * HEAD)
    q = two_heads(qbuf[b, 0])
    qd = two_heads(qbuf[b, 1])
    q_all[0] = q
    keys = kkd[rows, :]
    s = mm(keys[:, :HEAD], q, NT)
    u = lax.broadcasted_iota(jnp.int32, s.shape, 0)
    t = lax.rem(lax.broadcasted_iota(jnp.int32, (1, s.shape[1]), 1), HEAD)
    first = 1024 - b * HEAD - 512 * (4 * pos[0] + pos[1])
    allowed = (u >= jnp.maximum(t + 1, first)) & (u <= t + 1024)
    s = jnp.where(allowed, s, -1e30)
    e = jnp.exp2((s - jnp.max(s, axis=0, keepdims=True)) * SCALE2)
    inv = 1.0 / jnp.sum(e, axis=0, keepdims=True)
    sd = mm(keys, jnp.concatenate([qd, q], axis=1), NT)
    mean = jnp.sum(e * sd, axis=0, keepdims=True) * inv
    p_b = (e * inv).astype(BF)
    pd_b = (e * ((sd - mean) * (inv * SCALE))).astype(BF)
    p_all[0] = p_b
    values = vvd[rows, :]
    mixed = mm(values[:, :HEAD], pd_b, TN) + mm(values[:, HEAD:], p_b, TN)
    mixed = jnp.concatenate([mixed[:, :HEAD].T, mixed[:, HEAD:].T], axis=1).astype(BF)
    target = lax.rem(b + 4 - y, 4)
    for d in range(4):

        @pl.when(target == d)
        def _():
            outs[d][...] = mixed


def place_heads(pos, chunks, buf, size):
    for d, c in enumerate(chunks):
        head = lax.rem(pos[2] + 4 - d, 4)
        buf[:, pl.ds(pl.multiple_of(head * size, size), size)] = c


def out_kernel(pos, o0, o1, o2, o3, w, total, sent, buf):
    place_heads(pos, (o0[...], o1[...], o2[...], o3[...]), buf, 256)
    full = mm(buf[...], w[...])
    total[...] = full
    sent[...] = full.astype(BF)


def gradient_kernel(pos, total, other, w, g0, g1, g2, g3, buf):
    ct = (total[...] + other[...].astype(F32)).astype(BF)
    buf[...] = mm(ct, w[...], NT).astype(BF)
    for d, ref in enumerate((g0, g1, g2, g3)):
        head = lax.rem(pos[2] + d, 4)
        ref[...] = buf[:, pl.ds(pl.multiple_of(head * 256, 256), 256)]


def backward_kernel(pos, g0, g1, g2, g3, k_all, v_all, q_all, p_all, *refs):
    q0, q1, q2, q3, own, near, far, dk, dv = refs
    b = pl.program_id(0)
    y = pos[2]
    source = lax.rem(y + 4 - b, 4)
    target = lax.rem(b + 4 - y, 4)

    @pl.when(b == 0)
    def _():
        dk[...] = jnp.zeros_like(dk)
        dv[...] = jnp.zeros_like(dv)

    g = jnp.where(
        source < 2,
        jnp.where(source == 0, g0[...], g1[...]),
        jnp.where(source == 2, g2[...], g3[...]),
    )
    g = two_heads(g)
    rows = pl.ds(pl.multiple_of(b * HEAD, HEAD), 9 * HEAD)
    keys = k_all[rows, :]
    p_b = p_all[0]
    q = q_all[0]
    dp = mm(v_all[rows, :], g, NT)
    p = p_b.astype(F32)
    ds = (p * (dp - jnp.sum(p * dp, axis=0, keepdims=True))).astype(BF)
    dq = mm(keys, ds, TN) * SCALE
    dq = jnp.concatenate([dq[:, :HEAD].T, dq[:, HEAD:].T], axis=1).astype(BF)
    for d, ref in enumerate((q0, q1, q2, q3)):

        @pl.when(target == d)
        def _():
            ref[...] = dq

    dk[rows, :] += mm(ds, q)
    dv[rows, :] += mm(p_b, g)

    @pl.when(b == 3)
    def _():
        far[:, :HEAD] = (dk[:512, :] * SCALE).astype(BF)
        far[:, HEAD:] = dv[:512, :].astype(BF)
        near[:, :HEAD] = (dk[512:1024, :] * SCALE).astype(BF)
        near[:, HEAD:] = dv[512:1024, :].astype(BF)
        own[:, :HEAD] = dk[1024:, :] * SCALE
        own[:, HEAD:] = dv[1024:, :]


def pair_kernel(pos, own, near, far, *outs):
    y = pos[2]
    for d in range(4):
        rows = pl.ds(pl.multiple_of(lax.rem(y + d, 4) * HEAD, HEAD), HEAD)
        outs[d][...] = (
            own[rows, :] + near[rows, :].astype(F32) + far[rows, :].astype(F32)
        ).astype(BF)


def query_input_kernel(pos, q0, q1, q2, q3, w, _, total, buf):
    place_heads(pos, (q0[...], q1[...], q2[...], q3[...]), buf, 256)
    total[...] = mm(buf[...], w[...], NT)


def pair_input_kernel(pos, c0, c1, c2, c3, base, wk, wv, total, kbuf, vbuf):
    chunks = (c0, c1, c2, c3)
    place_heads(pos, [c[:, :HEAD] for c in chunks], kbuf, HEAD)
    place_heads(pos, [c[:, HEAD:] for c in chunks], vbuf, HEAD)
    total[...] = base[...] + (mm(kbuf[...], wk[...], NT) + mm(vbuf[...], wv[...], NT))


def weight_kernel(pos, *refs):
    mine, r1, r2, r3, p1, p2, p3, c0, c1, c2, c3 = refs[:11]
    outs = refs[11:15]
    line, sems = refs[15:]
    core = pos[3]
    half = r1.shape[0]
    copies = [pltpu.make_async_copy(mine, line.at[:, pl.ds(0, HEAD)], sems.at[0])]
    for d, (r, p) in enumerate(((r1, p1), (r2, p2), (r3, p3)), 1):
        for j, (src, where) in enumerate(((r, core), (p, 1 - core))):
            rows = pl.ds(pl.multiple_of(where * half, half), half)
            copies.append(
                pltpu.make_async_copy(
                    src, line.at[rows, pl.ds(d * HEAD, HEAD)], sems.at[2 * d - 1 + j]
                )
            )
    for c in copies:
        c.start()
    for c in copies:
        c.wait()
    pair = jnp.concatenate([c0[...], c3[...], c2[...], c1[...]], axis=0)
    size = 16 * PIECE
    for d in range(4):
        x = lax.rem(pos[0] + d, 4)
        block = line[pl.ds(pl.multiple_of(x * size, size), size), :]
        outs[d][...] = mm(block, pair).astype(BF)


def add_up(ins, rows):
    total = ins[0][rows, :].astype(F32)
    for r in ins[1:]:
        total += r[rows, :].astype(F32)
    return total


def middle_kernel(pos, *refs):
    ins, outs, total = refs[:4], refs[4:8], refs[8]
    size = 4 * PIECE
    total[...] = add_up(ins, slice(None))
    for d in range(4):
        rows = pl.ds(pl.multiple_of(lax.rem(pos[1] + d, 4) * size, 8), size)
        outs[d][...] = total[rows, :].astype(BF)


def last_kernel(pos, *refs):
    ins, outs = refs[:4], refs[4:]
    total = add_up(ins, slice(None))
    parts = [total[i * PIECE : (i + 1) * PIECE] for i in range(4)]
    for d in range(4):
        at = lax.rem(pos[2] + d, 4)
        outs[d][...] = jnp.where(
            at < 2,
            jnp.where(at == 0, parts[0], parts[1]),
            jnp.where(at == 2, parts[2], parts[3]),
        )


def place_kernel(pos, c0, c1, c2, c3, res):
    for d, c in enumerate((c0, c1, c2, c3)):
        head = pl.multiple_of(lax.rem(pos[2] + 4 - d, 4) * HEAD, HEAD)
        for j in range(2):
            res[:, j, pl.ds(head, HEAD)] = c[: res.shape[0], j * HEAD : (j + 1) * HEAD]


def on_device(tokens, tangent, w_query, w_key, value_weight, w_out):
    rows, width = tokens.shape
    seq = lax.axis_index("seq")
    core = lax.axis_index("mp")
    pos = jnp.stack([seq // 16, seq // 4 % 4, seq % 4, core]).astype(jnp.int32)
    piece_out = [out((4, rows, HEAD), BF)] * 4
    tok_in = (far_memory(), tokens)
    tan_in = (far_memory(), tangent)
    kv = flat_call(
        key_value_kernel,
        [pos, tok_in, tan_in, (far_memory(), w_key), (far_memory(), value_weight)],
        piece_out,
        [
            pltpu.VMEM((2 * rows, width), BF),
            pltpu.VMEM((4, width, 256), BF),
            pltpu.SemaphoreType.DMA((10,)),
        ],
        flops=2 * 256 * width * 1024,
        moved=2 * width * 1024,
        limit=62,
    )
    (line,) = flat_call(
        join_kernel,
        [pos] + [(vmem(), c) for c in exchange(ring_y, kv)],
        [out((4, 4, rows, HEAD), BF)],
        moved=1 << 20,
    )
    lines = [lines_on(line, 2), lines_on(line, 1), line]
    q = flat_call(
        query_kernel,
        [pos, (vmem(), tokens), (vmem(), tangent), (vmem(), w_query)],
        [out((2, rows, 256), BF)] * 4,
        [pltpu.VMEM((2 * rows, width), BF)],
        flops=2 * 256 * width * 1024,
        moved=2 * width * 1024,
    )
    late_tokens, _ = lax.optimization_barrier((tokens, q[0]))
    q = exchange(ring_y, q)
    columns = late_tokens.T
    half = lax.dynamic_slice_in_dim(columns, core * (width // 2), width // 2, 0)
    halves = exchange(ring_y, [half] * 4)[1:]
    partner_halves = [other_core(h) for h in halves]

    attended = call(
        forward_kernel,
        (4,),
        [pos] + [(hbm(), a) for a in lines + q],
        [out((rows, 256), BF)] * 4
        + [
            out((1536, HEAD), BF),
            out((1536, HEAD), BF),
            (pl.BlockSpec((1, 256, HEAD), lambda i, p: (i, 0, 0)), jax.ShapeDtypeStruct((4, 256, HEAD), BF)),
            (pl.BlockSpec((1, 1152, 256), lambda i, p: (i, 0, 0)), jax.ShapeDtypeStruct((4, 1152, 256), BF)),
        ],
        [
            pltpu.VMEM((1536, 256), BF),
            pltpu.VMEM((1536, 256), BF),
            pltpu.VMEM((4, 2, rows, 256), BF),
            pltpu.SemaphoreType.DMA((52,)),
        ],
        flops=2 * 4 * 1152 * 256 * 128 * 5,
        moved=8 << 20,
    )
    o, (k_all, v_all, q_all, p_all) = attended[:4], attended[4:]
    o = exchange(ring_y, o)
    small = whole((rows, 256))
    wide = pltpu.VMEM((rows, 1024), BF)
    total, sent = flat_call(
        out_kernel,
        [pos] + [(vmem(), a) for a in o] + [(vmem(), w_out)],
        [out((rows, width), F32), out((rows, width), BF)],
        [wide],
        flops=2 * rows * width * 1024,
        moved=2 * width * 1024,
    )
    other = other_core(sent)
    g = flat_call(
        gradient_kernel,
        [pos, (vmem(), total), (vmem(), other), (vmem(), w_out)],
        [out((rows, 256), BF)] * 4,
        [wide],
        flops=2 * rows * width * 1024,
        moved=2 * width * 1024,
    )
    g = exchange(ring_y, g)
    back = call(
        backward_kernel,
        (4,),
        [pos]
        + [(small, a) for a in g]
        + [
            (whole((1536, HEAD)), k_all),
            (whole((1536, HEAD)), v_all),
            (pl.BlockSpec((1, 256, HEAD), lambda i, p: (i, 0, 0)), q_all),
            (pl.BlockSpec((1, 1152, 256), lambda i, p: (i, 0, 0)), p_all),
        ],
        [out((rows, 256), BF)] * 4 + [out((512, 256), F32), out((512, 256), BF), out((512, 256), BF)],
        [pltpu.VMEM((1536, HEAD), F32), pltpu.VMEM((1536, HEAD), F32)],
        flops=2 * 4 * 1152 * 256 * 128 * 4,
        moved=6 << 20,
    )
    dq, (own, to_near, to_far) = back[:4], back[4:]
    from_far = lines_on(to_far, -2)
    from_near = lines_on(to_near, -1)
    dq = exchange(ring_y, dq)
    pair = call(
        pair_kernel,
        (1,),
        [pos] + [(whole((512, 256)), a) for a in (own, from_near, from_far)],
        [out((rows, 256), BF)] * 4,
        moved=1 << 20,
    )
    mixed_pair = exchange(ring_y, pair)

    part = (16 * PIECE, 256)
    stage = call(
        weight_kernel,
        (1,),
        [pos] + [(hbm(), a) for a in [columns] + halves + partner_halves] + [(small, a) for a in pair],
        [out(part, BF)] * 4,
        [pltpu.VMEM((64 * PIECE, 512), BF), pltpu.SemaphoreType.DMA((7,))],
        flops=2 * 3072 * 512 * 256,
        moved=5 << 20,
    )
    first = stage[0]
    stage = exchange(ring_x, stage)
    stage = flat_call(
        middle_kernel,
        [pos] + [(vmem(), v) for v in stage],
        [out((4 * PIECE, 256), BF)] * 4,
        [pltpu.VMEM((16 * PIECE, 256), F32)],
        moved=2 << 20,
    )
    stage = exchange(ring_z, stage)
    stage = flat_call(
        last_kernel,
        [pos] + [(vmem(), v) for v in stage],
        [out((PIECE, 256), F32)] * 4,
        moved=1 << 19,
    )
    stage = exchange(ring_y, stage)
    (weight_grad,) = call(
        place_kernel,
        (1,),
        [pos] + [(whole((PIECE, 256)), v) for v in stage],
        [out((width // 64, 2, 512), F32)],
        moved=1 << 18,
    )

    (base,) = flat_call(
        query_input_kernel,
        [pos] + [(vmem(), a) for a in dq] + [(vmem(), w_query), (hbm(), first)],
        [out((rows, width), F32)],
        [wide],
        flops=2 * rows * width * 1024,
        moved=2 * width * 1024,
    )
    narrow = pltpu.VMEM((rows, 512), BF)
    (terms,) = flat_call(
        pair_input_kernel,
        [pos]
        + [(vmem(), c) for c in mixed_pair]
        + [(vmem(), base), (vmem(), w_key), (vmem(), value_weight)],
        [out((rows, width), F32)],
        [narrow, narrow],
        flops=2 * rows * width * 1024,
        moved=2 * width * 1024,
    )
    low, high = terms[:, : width // 2], terms[:, width // 2 :]
    kept = jnp.where(core == 0, low, high)
    given = jnp.where(core == 0, high, low).astype(BF)
    input_grad = (kept + other_core(given).astype(F32)).astype(BF)
    return input_grad, weight_grad


def solution(mesh):
    placed = (
        P("seq", None),
        P("seq", None),
        P(None, "mp"),
        P(None, "mp"),
        P(None, "mp"),
        P("mp", None),
    )
    return jax.shard_map(
        on_device,
        mesh=mesh,
        in_specs=placed,
        out_specs=(P("seq", "mp"), P("seq", None, "mp")),
        check_vma=False,
    )
```

profile of v0, /device:TPU:0, one launch (start us, length us, event | category | flops | bytes accessed | tf_op | source)
XLA Modules:
  0.0 162.7 jit_solution(16885963752625961564)
XLA Ops:
  1.3 6.8 %shard_map.77 = (bf16[4,128,128]{2,1,0:T(8,128)(2,1)}, bf16[4,128,128]{2,1,0:T(8,128)(2,1)}, bf16[4,128,128]{2,1,0:T(8,128)(2,1)}, bf16[4,128,128]{2,1,0:T(8,128)(2,1)}) custom-call(s32[4]{0:T(128)} %pad_add_fusion.pos, bf16[128,2688]{1,0:T(8,128)(2,1)} %tok.3, bf16[128,2688]{1,0:T(8,128)(2,1)} %tan.3, bf16[2688,512]{1,0:T(8,128)(2,1)} %wk.3, ...), custom_call_target="tpu_custom_call" | custom-call | flops 1409286144 | bytes 5505024 | tf_op jit(solution)/shard_map/pallas_call | solution.py:77
  9.9 2.9 %collective-permute-start.1 = (bf16[4,128,128]{2,1,0:T(8,128)(2,1)}, bf16[4,128,128]{2,1,0:T(8,128)(2,1)S(1)}, u32[]{:S(2)}, u32[]{:S(2)}) collective-permute-start(bf16[4,128,128]{2,1,0:T(8,128)(2,1)} %get-tuple-element.50), channel_id=1, source_target_pairs={{0,4},{2,6},{4,0},{6,2},{8,12},{10,14},{12,8},{14,10},{16,20},{18,... | collective-permute-start | bytes 393224 | tf_op jit(solution)/shard_map/ppermute | solution.py:28
  15.0 4.0 %collective-permute-done.1.c = bf16[4,128,128]{2,1,0:T(8,128)(2,1)S(1)} collective-permute-done((bf16[4,128,128]{2,1,0:T(8,128)(2,1)}, bf16[4,128,128]{2,1,0:T(8,128)(2,1)S(1)}, u32[]{:S(2)}, u32[]{:S(2)}) %collective-permute-start.1) | collective-permute-done | bytes 131104 | tf_op jit(solution)/shard_map/ppermute | solution.py:28
  20.5 6.1 %collective-permute-start.3 = (bf16[4,4,128,128]{3,2,1,0:T(8,128)(2,1)S(1)}, bf16[4,4,128,128]{3,2,1,0:T(8,128)(2,1)S(1)}, u32[]{:S(2)}, u32[]{:S(2)}) collective-permute-start(bf16[4,4,128,128]{3,2,1,0:T(8,128)(2,1)S(1)} %shard_map.78.refs_2_), channel_id=1, source_target_pairs={{0,16},{2,18},{4,20},{6,22},{8,24},{10,26},{12,28},{14,30},{16,32}... | collective-permute-start | bytes 1572872 | tf_op jit(solution)/shard_map/ppermute | solution.py:42
  26.6 3.0 %collective-permute-start.4 = (bf16[4,4,128,128]{3,2,1,0:T(8,128)(2,1)S(1)}, bf16[4,4,128,128]{3,2,1,0:T(8,128)(2,1)S(1)}, u32[]{:S(2)}, u32[]{:S(2)}) collective-permute-start(bf16[4,4,128,128]{3,2,1,0:T(8,128)(2,1)S(1)} %shard_map.78.refs_2_), channel_id=1, source_target_pairs={{0,8},{2,10},{4,12},{6,14},{8,16},{10,18},{12,20},{14,22},{16,24},... | collective-permute-start | bytes 1572872 | tf_op jit(solution)/shard_map/ppermute | solution.py:42
  29.6 2.6 %copy-done.1 = bf16[2688,1024]{1,0:T(8,128)(2,1)S(1)} copy-done((bf16[2688,1024]{1,0:T(8,128)(2,1)S(1)}, bf16[2688,1024]{1,0:T(8,128)(2,1)}, u32[]{:S(2)}) %copy-start.1) | copy-done | bytes 5505048
  43.1 5.0 %collective-permute-done.4.refs_1_ = bf16[4,4,128,128]{3,2,1,0:T(8,128)(2,1)S(1)} collective-permute-done((bf16[4,4,128,128]{3,2,1,0:T(8,128)(2,1)S(1)}, bf16[4,4,128,128]{3,2,1,0:T(8,128)(2,1)S(1)}, u32[]{:S(2)}, u32[]{:S(2)}) %collective-permute-start.4) | collective-permute-done | bytes 524320 | tf_op jit(solution)/shard_map/ppermute | solution.py:42
  48.2 8.0 %shard_map.80 = (bf16[128,256]{1,0:T(8,128)(2,1)S(1)}, bf16[128,256]{1,0:T(8,128)(2,1)S(1)}, bf16[128,256]{1,0:T(8,128)(2,1)S(1)}, bf16[128,256]{1,0:T(8,128)(2,...) custom-call(s32[4]{0:T(128)S(1)} %copy-done.10, ...), custom_call_target="tpu_custom_call" | custom-call | flops 1509949440 | bytes 8388608 | tf_op jit(solution)/shard_map/pallas_call | solution.py:57
  57.8 2.5 %collective-permute-start.9 = (bf16[128,256]{1,0:T(8,128)(2,1)S(1)}, bf16[128,256]{1,0:T(8,128)(2,1)S(1)}, u32[]{:S(2)}, u32[]{:S(2)}) collective-permute-start(bf16[128,256]{1,0:T(8,128)(2,1)S(1)} %get-tuple-element.58), channel_id=1, source_target_pairs={{0,4},{2,6},{4,0},{6,2},{8,12},{10,14},{12,8},{14,10},{16,20},{18,... | collective-permute-start | bytes 196616 | tf_op jit(solution)/shard_map/ppermute | solution.py:28
  68.2 3.2 %collective-permute-start.24 = (bf16[1344,128]{1,0:T(8,128)(2,1)S(1)}, bf16[1344,128]{1,0:T(8,128)(2,1)S(1)}, u32[]{:S(2)}, u32[]{:S(2)}) collective-permute-start(bf16[1344,128]{1,0:T(8,128)(2,1)S(1)} %dynamic-slice_bitcast_fusion), channel_id=1, source_target_pairs={{0,4},{2,6},{4,0},{6,2},{8,12},{10,14},{12,8},{14,10},{16,20},{18,... | collective-permute-start | bytes 1032200 | tf_op jit(solution)/shard_map/ppermute | solution.py:28
  71.8 2.6 %copy-done = bf16[1024,2688]{1,0:T(8,128)(2,1)S(1)} copy-done((bf16[1024,2688]{1,0:T(8,128)(2,1)S(1)}, bf16[1024,2688]{1,0:T(8,128)(2,1)}, u32[]{:S(2)}) %copy-start) | copy-done | bytes 5505048
  75.7 2.5 %shard_map.82 = (bf16[128,256]{1,0:T(8,128)(2,1)S(1)}, bf16[128,256]{1,0:T(8,128)(2,1)S(1)}, bf16[128,256]{1,0:T(8,128)(2,1)S(1)}, bf16[128,256]{1,0:T(8,128)(2,1)S(1)}) custom-call(s32[4]{0:T(128)S(1)} %copy-done.10, f32[128,2688]{1,0:T(8,128)S(1)} %copy-done.8, bf16[128,2688]{1,0:T(8,128)(2,1)S(1)} %collective-permute-done.11.other, ...), custom_call_target="tpu_custom_call" | custom-call | flops 704643072 | bytes 5505024 | tf_op jit(solution)/shard_map/pallas_call | solution.py:77
  80.4 2.5 %collective-permute-start.14 = (bf16[128,256]{1,0:T(8,128)(2,1)S(1)}, bf16[128,256]{1,0:T(8,128)(2,1)S(1)}, u32[]{:S(2)}, u32[]{:S(2)}) collective-permute-start(bf16[128,256]{1,0:T(8,128)(2,1)S(1)} %get-tuple-element.65), channel_id=1, source_target_pairs={{0,6},{2,0},{4,2},{6,4},{8,14},{10,8},{12,10},{14,12},{16,22},{18,... | collective-permute-start | bytes 196616 | tf_op jit(solution)/shard_map/ppermute | solution.py:28
  82.9 4.7 %collective-permute-done.24.refs_2_ = bf16[1344,128]{1,0:T(8,128)(2,1)S(1)} collective-permute-done((bf16[1344,128]{1,0:T(8,128)(2,1)S(1)}, bf16[1344,128]{1,0:T(8,128)(2,1)S(1)}, u32[]{:S(2)}, u32[]{:S(2)}) %collective-permute-start.24) | collective-permute-done | bytes 344096 | tf_op jit(solution)/shard_map/ppermute | solution.py:28
  90.1 7.8 %shard_map.83 = (bf16[128,256]{1,0:T(8,128)(2,1)S(1)}, bf16[128,256]{1,0:T(8,128)(2,1)}, bf16[128,256]{1,0:T(8,128)(2,1)}, bf16[128,256]{1,0:T(8,128)(2,1)S(1)},...) custom-call(s32[4]{0:T(128)S(1)} %copy-done.10, ...), custom_call_target="tpu_custom_call" | custom-call | flops 1207959552 | bytes 6291456 | tf_op jit(solution)/shard_map/pallas_call | solution.py:57
  100.5 9.6 %collective-permute-done.15.near = bf16[512,256]{1,0:T(8,128)(2,1)} collective-permute-done((bf16[512,256]{1,0:T(8,128)(2,1)}, bf16[512,256]{1,0:T(8,128)(2,1)}, u32[]{:S(2)}, u32[]{:S(2)}) %collective-permute-start.15) | collective-permute-done | bytes 262176 | tf_op jit(solution)/shard_map/ppermute | solution.py:42
  122.2 2.6 %collective-permute-start.19 = (bf16[128,256]{1,0:T(8,128)(2,1)S(1)}, bf16[128,256]{1,0:T(8,128)(2,1)S(1)}, u32[]{:S(2)}, u32[]{:S(2)}) collective-permute-start(bf16[128,256]{1,0:T(8,128)(2,1)S(1)} %get-tuple-element.76.refs_10_), channel_id=1, source_target_pairs={{0,6},{2,0},{4,2},{6,4},{8,14},{10,8},{12,10},{14,12},{16,22},{18,... | collective-permute-start | bytes 196616 | tf_op jit(solution)/shard_map/ppermute | solution.py:28
  124.8 5.4 %collective-permute-start.30 = (bf16[672,256]{1,0:T(8,128)(2,1)S(1)}, bf16[672,256]{1,0:T(8,128)(2,1)S(1)}, u32[]{:S(2)}, u32[]{:S(2)}) collective-permute-start(bf16[672,256]{1,0:T(8,128)(2,1)S(1)} %get-tuple-element.83), channel_id=1, source_target_pairs={{0,32},{2,34},{4,36},{6,38},{8,40},{10,42},{12,44},{14,46},{16,48}... | collective-permute-start | bytes 1032200 | tf_op jit(solution)/shard_map/ppermute | solution.py:38
  131.8 2.6 %copy-done.2 = bf16[2688,1024]{1,0:T(8,128)(2,1)S(1)} copy-done((bf16[2688,1024]{1,0:T(8,128)(2,1)S(1)}, bf16[2688,1024]{1,0:T(8,128)(2,1)}, u32[]{:S(2)}) %copy-start.2) | copy-done | bytes 5505048
  134.4 2.4 %shard_map.86.base = f32[128,2688]{1,0:T(8,128)S(1)} custom-call(s32[4]{0:T(128)S(1)} %copy-done.10, bf16[128,256]{1,0:T(8,128)(2,1)S(1)} %get-tuple-element.77.q0, bf16[128,256]{1,0:T(8,128)(2,1)S(1)} %collective-permute-done.20.q1, bf16[128,256]{1,0:T(8,128)(2,1)S(1)} %collective-permute-done.21.q2, bf16[128,256]{1,0:T(8,128)(2,1)S(1)} %collective-permute-done.22.q3, ...), custom_call_target="tpu_custom_call" | custom-call | flops 704643072 | bytes 5505024 | tf_op jit(solution)/shard_map/pallas_call | solution.py:77
  136.8 2.6 %collective-permute-start.32 = (bf16[672,256]{1,0:T(8,128)(2,1)S(1)}, bf16[672,256]{1,0:T(8,128)(2,1)S(1)}, u32[]{:S(2)}, u32[]{:S(2)}) collective-permute-start(bf16[672,256]{1,0:T(8,128)(2,1)S(1)} %get-tuple-element.85), channel_id=1, source_target_pairs={{0,96},{2,98},{4,100},{6,102},{8,104},{10,106},{12,108},{14,110},{... | collective-permute-start | bytes 1032200 | tf_op jit(solution)/shard_map/ppermute | solution.py:38
  139.4 2.5 %shard_map.87 = f32[128,2688]{1,0:T(8,128)S(1)} custom-call(s32[4]{0:T(128)S(1)} %copy-done.10, bf16[128,256]{1,0:T(8,128)(2,1)S(1)} %get-tuple-element.73.refs_7_.c0, bf16[128,256]{1,0:T(8,128)(2,1)S(1)} %collective-permute-done.17.c1, bf16[128,256]{1,0:T(8,128)(2,1)S(1)} %collective-permute-done.18.c2, bf16[128,256]{1,0:T(8,128)(2,1)S(1)} %collective-permute-done.19.c3, ...), custom_call_target="tpu_custom_call" | custom-call | flops 704643072 | bytes 5505024 | tf_op jit(solution)/shard_map/pallas_call | solution.py:77
  145.1 2.4 %collective-permute-start.33 = (bf16[168,256]{1,0:T(8,128)(2,1)S(1)}, bf16[168,256]{1,0:T(8,128)(2,1)S(1)}, u32[]{:S(2)}, u32[]{:S(2)}) collective-permute-start(bf16[168,256]{1,0:T(8,128)(2,1)S(1)} %get-tuple-element.87), channel_id=1, source_target_pairs={{0,8},{2,10},{4,12},{6,14},{8,16},{10,18},{12,20},{14,22},{16,24},... | collective-permute-start | bytes 258056 | tf_op jit(solution)/shard_map/ppermute | solution.py:32
  156.4 2.5 %collective-permute-start.38 = (f32[42,256]{1,0:T(8,128)S(1)}, f32[42,256]{1,0:T(8,128)S(1)}, u32[]{:S(2)}, u32[]{:S(2)}) collective-permute-start(f32[42,256]{1,0:T(8,128)S(1)} %get-tuple-element.93), channel_id=1, source_target_pairs={{0,6},{2,0},{4,2},{6,4},{8,14},{10,8},{12,10},{14,12},{16,22},{18,... | collective-permute-start | bytes 129032 | tf_op jit(solution)/shard_map/ppermute | solution.py:28
  (117 shorter events, 65.0 us)
Async XLA Ops:
  9.9 9.1 %collective-permute-start.1 = (bf16[4,128,128]{2,1,0:T(8,128)(2,1)}, bf16[4,128,128]{2,1,0:T(8,128)(2,1)S(1)}, u32[]{:S(2)}, u32[]{:S(2)}) collective-permute-start(bf16[4,128,128]{2,1,0:T(8,128)(2,1)} %get-tuple-element.50), channel_id=1, source_target_pairs={{0,4},{2,6},{4,0},{6,2},{8,12},{10,14},{12,8},{14,10},{16,20},{18,... | collective-permute-start | bytes 393224 | tf_op jit(solution)/shard_map/ppermute | solution.py:28
  20.5 22.6 %collective-permute-start.3 = (bf16[4,4,128,128]{3,2,1,0:T(8,128)(2,1)S(1)}, bf16[4,4,128,128]{3,2,1,0:T(8,128)(2,1)S(1)}, u32[]{:S(2)}, u32[]{:S(2)}) collective-permute-start(bf16[4,4,128,128]{3,2,1,0:T(8,128)(2,1)S(1)} %shard_map.78.refs_2_), channel_id=1, source_target_pairs={{0,16},{2,18},{4,20},{6,22},{8,24},{10,26},{12,28},{14,30},{16,32}... | collective-permute-start | bytes 1572872 | tf_op jit(solution)/shard_map/ppermute | solution.py:42
  26.6 21.6 %collective-permute-start.4 = (bf16[4,4,128,128]{3,2,1,0:T(8,128)(2,1)S(1)}, bf16[4,4,128,128]{3,2,1,0:T(8,128)(2,1)S(1)}, u32[]{:S(2)}, u32[]{:S(2)}) collective-permute-start(bf16[4,4,128,128]{3,2,1,0:T(8,128)(2,1)S(1)} %shard_map.78.refs_2_), channel_id=1, source_target_pairs={{0,8},{2,10},{4,12},{6,14},{8,16},{10,18},{12,20},{14,22},{16,24},... | collective-permute-start | bytes 1572872 | tf_op jit(solution)/shard_map/ppermute | solution.py:42
  67.6 12.8 %collective-permute-start.23 = (bf16[1344,128]{1,0:T(8,128)(2,1)S(1)}, bf16[1344,128]{1,0:T(8,128)(2,1)S(1)}, u32[]{:S(2)}, u32[]{:S(2)}) collective-permute-start(bf16[1344,128]{1,0:T(8,128)(2,1)S(1)} %dynamic-slice_bitcast_fusion), channel_id=1, source_target_pairs={{0,2},{2,4},{4,6},{6,0},{8,10},{10,12},{12,14},{14,8},{16,18},{18,... | collective-permute-start | bytes 1032200 | tf_op jit(solution)/shard_map/ppermute | solution.py:28
  68.2 19.5 %collective-permute-start.24 = (bf16[1344,128]{1,0:T(8,128)(2,1)S(1)}, bf16[1344,128]{1,0:T(8,128)(2,1)S(1)}, u32[]{:S(2)}, u32[]{:S(2)}) collective-permute-start(bf16[1344,128]{1,0:T(8,128)(2,1)S(1)} %dynamic-slice_bitcast_fusion), channel_id=1, source_target_pairs={{0,4},{2,6},{4,0},{6,2},{8,12},{10,14},{12,8},{14,10},{16,20},{18,... | collective-permute-start | bytes 1032200 | tf_op jit(solution)/shard_map/ppermute | solution.py:28
  71.3 16.7 %collective-permute-start.25 = (bf16[1344,128]{1,0:T(8,128)(2,1)S(1)}, bf16[1344,128]{1,0:T(8,128)(2,1)S(1)}, u32[]{:S(2)}, u32[]{:S(2)}) collective-permute-start(bf16[1344,128]{1,0:T(8,128)(2,1)S(1)} %dynamic-slice_bitcast_fusion), channel_id=1, source_target_pairs={{0,6},{2,0},{4,2},{6,4},{8,14},{10,8},{12,10},{14,12},{16,22},{18,... | collective-permute-start | bytes 1032200 | tf_op jit(solution)/shard_map/ppermute | solution.py:28
  78.2 10.8 %collective-permute-start.12 = (bf16[128,256]{1,0:T(8,128)(2,1)S(1)}, bf16[128,256]{1,0:T(8,128)(2,1)S(1)}, u32[]{:S(2)}, u32[]{:S(2)}) collective-permute-start(bf16[128,256]{1,0:T(8,128)(2,1)S(1)} %get-tuple-element.63), channel_id=1, source_target_pairs={{0,2},{2,4},{4,6},{6,0},{8,10},{10,12},{12,14},{14,8},{16,18},{18,... | collective-permute-start | bytes 196616 | tf_op jit(solution)/shard_map/ppermute | solution.py:28
  79.8 10.2 %collective-permute-start.13 = (bf16[128,256]{1,0:T(8,128)(2,1)S(1)}, bf16[128,256]{1,0:T(8,128)(2,1)S(1)}, u32[]{:S(2)}, u32[]{:S(2)}) collective-permute-start(bf16[128,256]{1,0:T(8,128)(2,1)S(1)} %get-tuple-element.64), channel_id=1, source_target_pairs={{0,4},{2,6},{4,0},{6,2},{8,12},{10,14},{12,8},{14,10},{16,20},{18,... | collective-permute-start | bytes 196616 | tf_op jit(solution)/shard_map/ppermute | solution.py:28
  80.4 9.7 %collective-permute-start.14 = (bf16[128,256]{1,0:T(8,128)(2,1)S(1)}, bf16[128,256]{1,0:T(8,128)(2,1)S(1)}, u32[]{:S(2)}, u32[]{:S(2)}) collective-permute-start(bf16[128,256]{1,0:T(8,128)(2,1)S(1)} %get-tuple-element.65), channel_id=1, source_target_pairs={{0,6},{2,0},{4,2},{6,4},{8,14},{10,8},{12,10},{14,12},{16,22},{18,... | collective-permute-start | bytes 196616 | tf_op jit(solution)/shard_map/ppermute | solution.py:28
  87.7 28.6 %collective-permute-start.26 = (bf16[1344,128]{1,0:T(8,128)(2,1)S(1)}, bf16[1344,128]{1,0:T(8,128)(2,1)S(1)}, u32[]{:S(2)}, u32[]{:S(2)}) collective-permute-start(bf16[1344,128]{1,0:T(8,128)(2,1)S(1)} %collective-permute-done.23.refs_1_), channel_id=1, source_target_pairs={{0,1},{1,0},{2,3},{3,2},{4,5},{5,4},{6,7},{7,6},{8,9},{9,8},{10,11... | collective-permute-start | bytes 1032200 | tf_op jit(solution)/shard_map/ppermute | solution.py:51
  88.1 30.0 %collective-permute-start.27 = (bf16[1344,128]{1,0:T(8,128)(2,1)S(1)}, bf16[1344,128]{1,0:T(8,128)(2,1)S(1)}, u32[]{:S(2)}, u32[]{:S(2)}) collective-permute-start(bf16[1344,128]{1,0:T(8,128)(2,1)S(1)} %collective-permute-done.24.refs_2_), channel_id=1, source_target_pairs={{0,1},{1,0},{2,3},{3,2},{4,5},{5,4},{6,7},{7,6},{8,9},{9,8},{10,11... | collective-permute-start | bytes 1032200 | tf_op jit(solution)/shard_map/ppermute | solution.py:51
  89.0 29.4 %collective-permute-start.28 = (bf16[1344,128]{1,0:T(8,128)(2,1)S(1)}, bf16[1344,128]{1,0:T(8,128)(2,1)S(1)}, u32[]{:S(2)}, u32[]{:S(2)}) collective-permute-start(bf16[1344,128]{1,0:T(8,128)(2,1)S(1)} %collective-permute-done.25.refs_3_), channel_id=1, source_target_pairs={{0,1},{1,0},{2,3},{3,2},{4,5},{5,4},{6,7},{7,6},{8,9},{9,8},{10,11... | collective-permute-start | bytes 1032200 | tf_op jit(solution)/shard_map/ppermute | solution.py:51
  97.9 12.2 %collective-permute-start.15 = (bf16[512,256]{1,0:T(8,128)(2,1)}, bf16[512,256]{1,0:T(8,128)(2,1)}, u32[]{:S(2)}, u32[]{:S(2)}) collective-permute-start(bf16[512,256]{1,0:T(8,128)(2,1)} %get-tuple-element.71), channel_id=1, source_target_pairs={{8,0},{10,2},{12,4},{14,6},{16,8},{18,10},{20,12},{22,14},{24,16},... | collective-permute-start | bytes 786440 | tf_op jit(solution)/shard_map/ppermute | solution.py:42
  99.2 13.1 %collective-permute-start.16 = (bf16[512,256]{1,0:T(8,128)(2,1)}, bf16[512,256]{1,0:T(8,128)(2,1)}, u32[]{:S(2)}, u32[]{:S(2)}) collective-permute-start(bf16[512,256]{1,0:T(8,128)(2,1)} %get-tuple-element.72), channel_id=1, source_target_pairs={{16,0},{18,2},{20,4},{22,6},{24,8},{26,10},{28,12},{30,14},{32,16}... | collective-permute-start | bytes 786440 | tf_op jit(solution)/shard_map/ppermute | solution.py:42
  110.2 12.0 %collective-permute-start.20 = (bf16[128,256]{1,0:T(8,128)(2,1)}, bf16[128,256]{1,0:T(8,128)(2,1)S(1)}, u32[]{:S(2)}, u32[]{:S(2)}) collective-permute-start(bf16[128,256]{1,0:T(8,128)(2,1)} %get-tuple-element.78), channel_id=1, source_target_pairs={{0,2},{2,4},{4,6},{6,0},{8,10},{10,12},{12,14},{14,8},{16,18},{18,... | collective-permute-start | bytes 196616 | tf_op jit(solution)/shard_map/ppermute | solution.py:28
  112.3 12.5 %collective-permute-start.21 = (bf16[128,256]{1,0:T(8,128)(2,1)}, bf16[128,256]{1,0:T(8,128)(2,1)S(1)}, u32[]{:S(2)}, u32[]{:S(2)}) collective-permute-start(bf16[128,256]{1,0:T(8,128)(2,1)} %get-tuple-element.79), channel_id=1, source_target_pairs={{0,4},{2,6},{4,0},{6,2},{8,12},{10,14},{12,8},{14,10},{16,20},{18,... | collective-permute-start | bytes 196616 | tf_op jit(solution)/shard_map/ppermute | solution.py:28
  116.3 13.9 %collective-permute-start.22 = (bf16[128,256]{1,0:T(8,128)(2,1)S(1)}, bf16[128,256]{1,0:T(8,128)(2,1)S(1)}, u32[]{:S(2)}, u32[]{:S(2)}) collective-permute-start(bf16[128,256]{1,0:T(8,128)(2,1)S(1)} %get-tuple-element.80), channel_id=1, source_target_pairs={{0,6},{2,0},{4,2},{6,4},{8,14},{10,8},{12,10},{14,12},{16,22},{18,... | collective-permute-start | bytes 196616 | tf_op jit(solution)/shard_map/ppermute | solution.py:28
  118.1 18.7 %collective-permute-start.17 = (bf16[128,256]{1,0:T(8,128)(2,1)S(1)}, bf16[128,256]{1,0:T(8,128)(2,1)S(1)}, u32[]{:S(2)}, u32[]{:S(2)}) collective-permute-start(bf16[128,256]{1,0:T(8,128)(2,1)S(1)} %get-tuple-element.74.refs_8_), channel_id=1, source_target_pairs={{0,2},{2,4},{4,6},{6,0},{8,10},{10,12},{12,14},{14,8},{16,18},{18,... | collective-permute-start | bytes 196616 | tf_op jit(solution)/shard_map/ppermute | solution.py:28
  118.4 21.0 %collective-permute-start.18 = (bf16[128,256]{1,0:T(8,128)(2,1)S(1)}, bf16[128,256]{1,0:T(8,128)(2,1)S(1)}, u32[]{:S(2)}, u32[]{:S(2)}) collective-permute-start(bf16[128,256]{1,0:T(8,128)(2,1)S(1)} %get-tuple-element.75.refs_9_), channel_id=1, source_target_pairs={{0,4},{2,6},{4,0},{6,2},{8,12},{10,14},{12,8},{14,10},{16,20},{18,... | collective-permute-start | bytes 196616 | tf_op jit(solution)/shard_map/ppermute | solution.py:28
  122.2 17.2 %collective-permute-start.19 = (bf16[128,256]{1,0:T(8,128)(2,1)S(1)}, bf16[128,256]{1,0:T(8,128)(2,1)S(1)}, u32[]{:S(2)}, u32[]{:S(2)}) collective-permute-start(bf16[128,256]{1,0:T(8,128)(2,1)S(1)} %get-tuple-element.76.refs_10_), channel_id=1, source_target_pairs={{0,6},{2,0},{4,2},{6,4},{8,14},{10,8},{12,10},{14,12},{16,22},{18,... | collective-permute-start | bytes 196616 | tf_op jit(solution)/shard_map/ppermute | solution.py:28
  124.8 17.4 %collective-permute-start.30 = (bf16[672,256]{1,0:T(8,128)(2,1)S(1)}, bf16[672,256]{1,0:T(8,128)(2,1)S(1)}, u32[]{:S(2)}, u32[]{:S(2)}) collective-permute-start(bf16[672,256]{1,0:T(8,128)(2,1)S(1)} %get-tuple-element.83), channel_id=1, source_target_pairs={{0,32},{2,34},{4,36},{6,38},{8,40},{10,42},{12,44},{14,46},{16,48}... | collective-permute-start | bytes 1032200 | tf_op jit(solution)/shard_map/ppermute | solution.py:38
  130.2 13.2 %collective-permute-start.31 = (bf16[672,256]{1,0:T(8,128)(2,1)S(1)}, bf16[672,256]{1,0:T(8,128)(2,1)S(1)}, u32[]{:S(2)}, u32[]{:S(2)}) collective-permute-start(bf16[672,256]{1,0:T(8,128)(2,1)S(1)} %get-tuple-element.84), channel_id=1, source_target_pairs={{0,64},{2,66},{4,68},{6,70},{8,72},{10,74},{12,76},{14,78},{16,80}... | collective-permute-start | bytes 1032200 | tf_op jit(solution)/shard_map/ppermute | solution.py:38
  136.8 7.5 %collective-permute-start.32 = (bf16[672,256]{1,0:T(8,128)(2,1)S(1)}, bf16[672,256]{1,0:T(8,128)(2,1)S(1)}, u32[]{:S(2)}, u32[]{:S(2)}) collective-permute-start(bf16[672,256]{1,0:T(8,128)(2,1)S(1)} %get-tuple-element.85), channel_id=1, source_target_pairs={{0,96},{2,98},{4,100},{6,102},{8,104},{10,106},{12,108},{14,110},{... | collective-permute-start | bytes 1032200 | tf_op jit(solution)/shard_map/ppermute | solution.py:38
  142.1 16.8 %collective-permute-start.29 = (bf16[128,1344]{1,0:T(8,128)(2,1)S(1)}, bf16[128,1344]{1,0:T(8,128)(2,1)S(1)}, u32[]{:S(2)}, u32[]{:S(2)}) collective-permute-start(bf16[128,1344]{1,0:T(8,128)(2,1)S(1)} %select_convert_fusion), channel_id=1, source_target_pairs={{0,1},{1,0},{2,3},{3,2},{4,5},{5,4},{6,7},{7,6},{8,9},{9,8},{10,11... | collective-permute-start | bytes 1032200 | tf_op jit(solution)/shard_map/ppermute | solution.py:51
  (36 other events, 367.7 us)
where the time goes:
time: 164 us; the launch traced here: 163 us
  starting transfers between devices  67.3 us (41%)
  Pallas kernels  40.7 us (25%)
  waiting for transfers between devices  40.2 us (25%)
  local copies, waits for them, and re-layouts  12.4 us (8%)
    ppermute x24, starting transfers between devices, ring_y(): lax.ppermute(x, 'seq', [(i, i // 4 * 4 + (i + d) % 4) for i in range(64)])  39.6 us
    pallas_call x5, Pallas kernels, call(): pl.pallas_call(kernel, grid_spec=pltpu.PrefetchScalarGridSpec(num_scalar_...  20.8 us
    pallas_call x9, Pallas kernels, flat_call(): pl.pallas_call(kernel, in_specs=[pl.BlockSpec(memory_space=pltpu.SMEM)] +...  20 us
    ppermute x24, waiting for transfers between devices, ring_y(): lax.ppermute(x, 'seq', [(i, i // 4 * 4 + (i + d) % 4) for i in range(64)])  20 us
    ppermute x4, waiting for transfers between devices, lines_on(): lax.ppermute(x, 'seq', [(i, i + 4 * d) for i in range(64) if 0 <= i + 4 *...  15.6 us
    unnamed x43, local copies, waits for them, and re-layouts  12 us
    ppermute x4, starting transfers between devices, lines_on(): lax.ppermute(x, 'seq', [(i, i + 4 * d) for i in range(64) if 0 <= i + 4 *...  11.6 us
    ppermute x3, starting transfers between devices, ring_x(): lax.ppermute(x, 'seq', [(i, (i // 16 + d) % 4 * 16 + i % 16) for i in ran...  9.61 us
  transfers between devices with their start and end apart: 39, of which 22 were waited for; matrix products, arithmetic and copies ran while one was open for 1% of the time, Pallas kernels for 14%

commit v1 on v0

v1 whole, which is shorter than its diff:
```python
import math

import jax
import jax.numpy as jnp
from jax import lax
from jax.experimental import pallas as pl
from jax.experimental.pallas import tpu as pltpu
from jax.sharding import PartitionSpec as P

BF = jnp.bfloat16
F32 = jnp.float32
HEAD = 128
SCALE = 168.0 ** (-0.5)
SCALE2 = SCALE * math.log2(math.e)
PIECE = 42


NT = (((1,), (1,)), ((), ()))
TN = (((0,), (0,)), ((), ()))
NN = (((1,), (0,)), ((), ()))


def mm(a, b, dims=NN):
    return lax.dot_general(a, b, dims, preferred_element_type=F32)


def ring_y(x, d):
    return lax.ppermute(x, "seq", [(i, i // 4 * 4 + (i + d) % 4) for i in range(64)])


def ring_z(x, d):
    return lax.ppermute(
        x, "seq", [(i, i // 16 * 16 + (i // 4 + d) % 4 * 4 + i % 4) for i in range(64)]
    )


def ring_x(x, d):
    return lax.ppermute(x, "seq", [(i, (i // 16 + d) % 4 * 16 + i % 16) for i in range(64)])


def lines_on(x, d):
    return lax.ppermute(x, "seq", [(i, i + 4 * d) for i in range(64) if 0 <= i + 4 * d < 64])


def exchange(ring, chunks):
    got = {d: ring(chunks[d], d) for d in (1, 3, 2)}
    return [chunks[0], got[1], got[2], got[3]]


def far_one(x):
    return lax.ppermute(
        x, "seq", [(i, i // 16 * 16 + (i // 4 + 3) % 4 * 4 + i % 4) for i in range(64)]
    )


def far_two(x):
    route = []
    for i in range(64):
        source = i // 16 * 16 + (i // 4 + 1) % 4 * 4 + i % 4
        if source + 8 < 64:
            route.append((i, source + 8))
    return lax.ppermute(x, "seq", route)


def other_core(x):
    return lax.ppermute(x, "mp", [(0, 1), (1, 0)])


def call(kernel, grid, ins, outs, scratch=(), flops=0, moved=0, limit=20):
    specs_in, values = zip(*ins[1:])
    specs_out, shapes = zip(*outs)
    return pl.pallas_call(
        kernel,
        grid_spec=pltpu.PrefetchScalarGridSpec(
            num_scalar_prefetch=1,
            grid=grid,
            in_specs=list(specs_in),
            out_specs=list(specs_out),
            scratch_shapes=list(scratch),
        ),
        out_shape=list(shapes),
        compiler_params=pltpu.CompilerParams(
            dimension_semantics=("arbitrary",) * len(grid), vmem_limit_bytes=limit << 20
        ),
        cost_estimate=pl.CostEstimate(flops=flops, bytes_accessed=moved, transcendentals=0),
    )(ins[0], *values)


def flat_call(kernel, ins, outs, scratch=(), flops=0, moved=0, limit=20):
    specs_in, values = zip(*ins[1:])
    _, shapes = zip(*outs)
    return pl.pallas_call(
        kernel,
        in_specs=[pl.BlockSpec(memory_space=pltpu.SMEM)] + list(specs_in),
        out_specs=[pl.BlockSpec(memory_space=pltpu.VMEM)] * len(shapes),
        scratch_shapes=list(scratch),
        out_shape=list(shapes),
        compiler_params=pltpu.CompilerParams(vmem_limit_bytes=limit << 20),
        cost_estimate=pl.CostEstimate(flops=flops, bytes_accessed=moved, transcendentals=0),
    )(ins[0], *values)


def whole(shape):
    return pl.BlockSpec(shape, lambda *_: (0,) * len(shape))


def hbm():
    return pl.BlockSpec(memory_space=pl.ANY)


def far_memory():
    return pl.BlockSpec(memory_space=pltpu.HBM)


def vmem():
    return pl.BlockSpec(memory_space=pltpu.VMEM)


def out(shape, dtype):
    return whole(shape), jax.ShapeDtypeStruct(shape, dtype)


CUTS = (0, 640, 1280, 1920, 2688)


def key_value_kernel(pos, tok, tan, wk, wv, *refs):
    outs, (both, w, acc, flat, sem) = refs[:4], refs[4:]
    rows = tok.shape[0]
    half = wk.shape[1]
    copies = [
        pltpu.make_async_copy(tok, both.at[pl.ds(0, rows)], sem.at[0]),
        pltpu.make_async_copy(tan, both.at[pl.ds(rows, rows)], sem.at[1]),
    ]
    for j in range(4):
        part = pl.ds(CUTS[j], CUTS[j + 1] - CUTS[j])
        for i, src in enumerate((wk, wv)):
            copies.append(
                pltpu.make_async_copy(
                    src.at[part], w.at[part, pl.ds(i * half, half)], sem.at[2 + 2 * j + i]
                )
            )
    for c in copies[:6]:
        c.start()
    copies[0].wait()
    copies[1].wait()
    for j in range(4):
        copies[2 + 2 * j].wait()
        copies[3 + 2 * j].wait()
        for c in copies[6 + 2 * j : 8 + 2 * j]:
            c.start()
        part = slice(CUTS[j], CUTS[j + 1])
        res = mm(both[:, part], w[part, :])
        if j == 0:
            acc[...] = res
        elif j < 3:
            acc[...] += res
        else:
            flat[...] = (acc[...] + res).astype(BF)
    for d in range(4):
        head = lax.rem(pos[2] + d, 4) * HEAD
        k = flat[:, pl.ds(pl.multiple_of(head, HEAD), HEAD)]
        v = flat[:, pl.ds(pl.multiple_of(head + half, HEAD), HEAD)]
        outs[d][0] = k[:rows]
        outs[d][1] = k[rows:]
        outs[d][2] = v[:rows]
        outs[d][3] = v[rows:]


def query_kernel(pos, tok, tan, w, *refs):
    outs, both = refs[:4], refs[4]
    rows = tok.shape[0]
    both[:rows] = tok[...]
    both[rows:] = tan[...]
    for d in range(4):
        cols = pl.ds(pl.multiple_of(lax.rem(pos[2] + d, 4) * 256, 256), 256)
        res = mm(both[...], w[:, cols]).astype(BF)
        outs[d][0] = res[:rows]
        outs[d][1] = res[rows:]


def join_kernel(pos, a, b, c, e, line, low, high):
    for d, ref in enumerate((a, b, c, e)):
        block = lax.rem(pos[2] + 4 - d, 4)
        rows = pl.ds(pl.multiple_of(block * HEAD, HEAD), HEAD)
        for part in range(4):
            line[rows, part * HEAD : (part + 1) * HEAD] = ref[part]
    low[...] = line[:256]
    high[...] = line[256:]


def load_kernel(pos, src, dst, sem):
    copy = pltpu.make_async_copy(src, dst, sem)
    copy.start()
    copy.wait()


def two_heads(block):
    return jnp.concatenate([block[:, :HEAD], block[:, HEAD:]], axis=0)


def window_of(refs, b, cols):
    low, high, near, own = refs
    parts = []
    if b < 2:
        parts.append(low[b * HEAD :, cols])
        parts.append(high[:, cols])
    else:
        parts.append(high[(b - 2) * HEAD :, cols])
    parts += [near[:, cols], own[: (b + 1) * HEAD, cols]]
    return jnp.concatenate(parts, axis=0)


def forward_kernel(pos, low, high, near, own, q0, q1, q2, q3, *refs):
    o0, o1, o2, o3, q_all, p_all, qbuf, obuf = refs
    lines = (low, high, near, own)
    line = 4 * pos[0] + pos[1]
    far_bias = jnp.where(line < 2, -1e30, 0.0).astype(F32)
    near_bias = jnp.where(line < 1, -1e30, 0.0).astype(F32)
    for d, q in enumerate((q0, q1, q2, q3)):
        qbuf[lax.rem(pos[2] + 4 - d, 4)] = q[...]
    u = lax.broadcasted_iota(jnp.int32, (HEAD, 256), 0)
    t = lax.rem(lax.broadcasted_iota(jnp.int32, (HEAD, 256), 1), HEAD)
    for b in range(4):
        q = two_heads(qbuf[b, 0])
        qd = two_heads(qbuf[b, 1])
        q_all[b] = q
        keys = window_of(lines, b, slice(0, 256))
        values = window_of(lines, b, slice(256, 512))
        s = mm(keys[:, :HEAD], q, NT)
        split = (4 - b) * HEAD
        parts = [jnp.where(u > t, s[:HEAD] + far_bias, -1e30)]
        if b < 3:
            parts.append(s[HEAD:split] + far_bias)
        parts.append(s[split : split + 512] + near_bias)
        if b > 0:
            parts.append(s[split + 512 : 8 * HEAD])
        parts.append(jnp.where(u <= t, s[8 * HEAD :], -1e30))
        s = jnp.concatenate(parts, axis=0)
        e = jnp.exp2((s - jnp.max(s, axis=0, keepdims=True)) * SCALE2)
        inv = 1.0 / jnp.sum(e, axis=0, keepdims=True)
        sd = mm(keys, jnp.concatenate([qd, q], axis=1), NT)
        mean = jnp.sum(e * sd, axis=0, keepdims=True) * inv
        p_b = (e * inv).astype(BF)
        pd_b = (e * ((sd - mean) * (inv * SCALE))).astype(BF)
        p_all[b] = p_b
        mixed = mm(values[:, :HEAD], pd_b, TN) + mm(values[:, HEAD:], p_b, TN)
        obuf[b, :, :HEAD] = mixed[:, :HEAD].T.astype(BF)
        obuf[b, :, HEAD:] = mixed[:, HEAD:].T.astype(BF)
    for d, o in enumerate((o0, o1, o2, o3)):
        o[...] = obuf[lax.rem(pos[2] + d, 4)]


def place_heads(pos, chunks, buf, size):
    for d, c in enumerate(chunks):
        head = lax.rem(pos[2] + 4 - d, 4)
        buf[:, pl.ds(pl.multiple_of(head * size, size), size)] = c


def out_kernel(pos, o0, o1, o2, o3, w, total, sent, buf):
    place_heads(pos, (o0[...], o1[...], o2[...], o3[...]), buf, 256)
    full = mm(buf[...], w[...])
    total[...] = full
    sent[...] = full.astype(BF)


def gradient_kernel(pos, total, other, w, g0, g1, g2, g3, buf):
    ct = (total[...] + other[...].astype(F32)).astype(BF)
    buf[...] = mm(ct, w[...], NT).astype(BF)
    for d, ref in enumerate((g0, g1, g2, g3)):
        head = lax.rem(pos[2] + d, 4)
        ref[...] = buf[:, pl.ds(pl.multiple_of(head * 256, 256), 256)]


def backward_kernel(pos, g0, g1, g2, g3, low, high, near_kv, own_kv, q_all, p_all, *refs):
    q0, q1, q2, q3, own, near, far, dk, dv, gbuf, dqbuf = refs
    lines = (low, high, near_kv, own_kv)
    for d, g in enumerate((g0, g1, g2, g3)):
        gbuf[lax.rem(pos[2] + 4 - d, 4)] = g[...]
    for b in range(4):
        g = two_heads(gbuf[b])
        keys = window_of(lines, b, slice(0, HEAD))
        values = window_of(lines, b, slice(256, 384))
        p_b = p_all[b]
        dp = mm(values, g, NT)
        p = p_b.astype(F32)
        ds = (p * (dp - jnp.sum(p * dp, axis=0, keepdims=True))).astype(BF)
        dq = mm(keys, ds, TN) * SCALE
        dqbuf[b, :, :HEAD] = dq[:, :HEAD].T.astype(BF)
        dqbuf[b, :, HEAD:] = dq[:, HEAD:].T.astype(BF)
        dk_part = mm(ds, q_all[b])
        dv_part = mm(p_b, g)
        rows = slice(b * HEAD, b * HEAD + 9 * HEAD)
        if b == 0:
            dk[rows] = dk_part
            dv[rows] = dv_part
        else:
            fresh = slice(b * HEAD + 8 * HEAD, b * HEAD + 9 * HEAD)
            rows = slice(b * HEAD, b * HEAD + 8 * HEAD)
            dk[rows] += dk_part[: 8 * HEAD]
            dv[rows] += dv_part[: 8 * HEAD]
            dk[fresh] = dk_part[8 * HEAD :]
            dv[fresh] = dv_part[8 * HEAD :]
    far[:, :HEAD] = (dk[:512, :] * SCALE).astype(BF)
    far[:, HEAD:] = dv[:512, :].astype(BF)
    near[:, :HEAD] = (dk[512:1024, :] * SCALE).astype(BF)
    near[:, HEAD:] = dv[512:1024, :].astype(BF)
    own[:, :HEAD] = dk[1024:, :] * SCALE
    own[:, HEAD:] = dv[1024:, :]
    for d, q in enumerate((q0, q1, q2, q3)):
        q[...] = dqbuf[lax.rem(pos[2] + d, 4)]


def pair_kernel(pos, own, near, far, *outs):
    y = pos[2]
    for d in range(4):
        rows = pl.ds(pl.multiple_of(lax.rem(y + d, 4) * HEAD, HEAD), HEAD)
        outs[d][...] = (
            own[rows, :] + near[rows, :].astype(F32) + far[rows, :].astype(F32)
        ).astype(BF)


def query_input_kernel(pos, q0, q1, q2, q3, w, _, total, buf):
    place_heads(pos, (q0[...], q1[...], q2[...], q3[...]), buf, 256)
    total[...] = mm(w[...], buf[...], NT)


def pair_input_kernel(pos, c0, c1, c2, c3, base, wk, wv, kept, given, kbuf, vbuf, total):
    chunks = (c0, c1, c2, c3)
    place_heads(pos, [c[:, :HEAD] for c in chunks], kbuf, HEAD)
    place_heads(pos, [c[:, HEAD:] for c in chunks], vbuf, HEAD)
    total[...] = base[...] + (mm(wk[...], kbuf[...], NT) + mm(wv[...], vbuf[...], NT))
    half = kept.shape[0]
    kept[...] = total[pl.ds(pl.multiple_of(pos[3] * half, half), half), :]
    given[...] = total[pl.ds(pl.multiple_of((1 - pos[3]) * half, half), half), :].astype(BF)


def weight_kernel(pos, *refs):
    mine, r1, r2, r3, p1, p2, p3, c0, c1, c2, c3 = refs[:11]
    outs = refs[11:17]
    line, sems = refs[17:]
    core = pos[3]
    half = r1.shape[0]
    copies = [pltpu.make_async_copy(mine, line.at[:, pl.ds(0, HEAD)], sems.at[0])]
    for d, (r, p) in enumerate(((r1, p1), (r2, p2), (r3, p3)), 1):
        for j, (src, where) in enumerate(((r, core), (p, 1 - core))):
            rows = pl.ds(pl.multiple_of(where * half, half), half)
            copies.append(
                pltpu.make_async_copy(
                    src, line.at[rows, pl.ds(d * HEAD, HEAD)], sems.at[2 * d - 1 + j]
                )
            )
    for c in copies:
        c.start()
    for c in copies:
        c.wait()
    pair = jnp.concatenate([c0[...], c3[...], c2[...], c1[...]], axis=0)
    size = 16 * PIECE
    for d in range(4):
        x = lax.rem(pos[0] + d, 4)
        block = line[pl.ds(pl.multiple_of(x * size, size), size), :]
        part = mm(block, pair).astype(BF)
        outs[d][...] = part
        if d == 2:
            outs[4][...] = part[: size // 2]
            outs[5][...] = part[size // 2 :]


def across(stage):
    up = ring_x(stage[4], 1)
    down = ring_x(stage[5], 3)
    one, three = ring_x(stage[1], 1), ring_x(stage[3], 3)
    up, down = ring_x(up, 1), ring_x(down, 3)
    return [stage[0], one, three, up, down]


def add_up(ins, rows):
    total = ins[0][rows, :].astype(F32)
    for r in ins[1:]:
        total += r[rows, :].astype(F32)
    return total


def middle_kernel(pos, mine, one, three, up, down, *refs):
    outs, total = refs[:4], refs[4]
    size = 4 * PIECE
    for i, half in enumerate((up, down)):
        rows = slice(i * half.shape[0], (i + 1) * half.shape[0])
        total[rows, :] = add_up((mine, one, three), rows) + half[...].astype(F32)
    for d in range(4):
        rows = pl.ds(pl.multiple_of(lax.rem(pos[1] + d, 4) * size, 8), size)
        outs[d][...] = total[rows, :].astype(BF)


def last_kernel(pos, *refs):
    ins, outs = refs[:4], refs[4:]
    total = add_up(ins, slice(None))
    parts = [total[i * PIECE : (i + 1) * PIECE] for i in range(4)]
    for d in range(4):
        at = lax.rem(pos[2] + d, 4)
        outs[d][...] = jnp.where(
            at < 2,
            jnp.where(at == 0, parts[0], parts[1]),
            jnp.where(at == 2, parts[2], parts[3]),
        )


def place_kernel(pos, c0, c1, c2, c3, res):
    for d, c in enumerate((c0, c1, c2, c3)):
        head = pl.multiple_of(lax.rem(pos[2] + 4 - d, 4) * HEAD, HEAD)
        for j in range(2):
            res[:, j, pl.ds(head, HEAD)] = c[: res.shape[0], j * HEAD : (j + 1) * HEAD]


def on_device(tokens, tangent, w_query, w_key, value_weight, w_out):
    rows, width = tokens.shape
    seq = lax.axis_index("seq")
    core = lax.axis_index("mp")
    pos = jnp.stack([seq // 16, seq // 4 % 4, seq % 4, core]).astype(jnp.int32)
    piece_out = [out((4, rows, HEAD), BF)] * 4
    tok_in = (far_memory(), tokens)
    tan_in = (far_memory(), tangent)
    kv = flat_call(
        key_value_kernel,
        [pos, tok_in, tan_in, (far_memory(), w_key), (far_memory(), value_weight)],
        piece_out,
        [
            pltpu.VMEM((2 * rows, width), BF),
            pltpu.VMEM((width, 1024), BF),
            pltpu.VMEM((2 * rows, 1024), F32),
            pltpu.VMEM((2 * rows, 1024), BF),
            pltpu.SemaphoreType.DMA((10,)),
        ],
        flops=2 * 256 * width * 1024,
        moved=2 * width * 1024,
        limit=62,
    )
    line, low, high = flat_call(
        join_kernel,
        [pos] + [(vmem(), c) for c in exchange(ring_y, kv)],
        [out((512, 512), BF), out((256, 512), BF), out((256, 512), BF)],
        moved=1 << 20,
    )
    passed = far_one(high)
    near = lines_on(line, 1)
    far_low = lines_on(low, 2)
    far_high = far_two(passed)
    lines = [far_low, far_high, near, line]
    q = flat_call(
        query_kernel,
        [pos, (vmem(), tokens), (vmem(), tangent), (vmem(), w_query)],
        [out((2, rows, 256), BF)] * 4,
        [pltpu.VMEM((2 * rows, width), BF)],
        flops=2 * 256 * width * 1024,
        moved=2 * width * 1024,
    )
    late_tokens, _ = lax.optimization_barrier((tokens, q[0]))
    q = exchange(ring_y, q)
    columns = late_tokens.T
    half = lax.dynamic_slice_in_dim(columns, core * (width // 2), width // 2, 0)
    (w_out,) = flat_call(
        load_kernel,
        [pos, (far_memory(), w_out)],
        [out(w_out.shape, BF)],
        [pltpu.SemaphoreType.DMA],
        moved=2 * w_out.size,
    )
    halves = exchange(ring_y, [half] * 4)[1:]
    partner_halves = [other_core(h) for h in halves]

    attended = flat_call(
        forward_kernel,
        [pos] + [(vmem(), a) for a in lines + q],
        [out((rows, 256), BF)] * 4 + [out((4, 256, HEAD), BF), out((4, 1152, 256), BF)],
        [pltpu.VMEM((4, 2, rows, 256), BF), pltpu.VMEM((4, rows, 256), BF)],
        flops=2 * 4 * 1152 * 256 * 128 * 5,
        moved=8 << 20,
        limit=24,
    )
    o, (q_all, p_all) = attended[:4], attended[4:]
    o = exchange(ring_y, o)
    small = whole((rows, 256))
    wide = pltpu.VMEM((rows, 1024), BF)
    total, sent = flat_call(
        out_kernel,
        [pos] + [(vmem(), a) for a in o] + [(vmem(), w_out)],
        [out((rows, width), F32), out((rows, width), BF)],
        [wide],
        flops=2 * rows * width * 1024,
        moved=2 * width * 1024,
    )
    other = other_core(sent)
    g = flat_call(
        gradient_kernel,
        [pos, (vmem(), total), (vmem(), other), (vmem(), w_out)],
        [out((rows, 256), BF)] * 4,
        [wide],
        flops=2 * rows * width * 1024,
        moved=2 * width * 1024,
    )
    g = exchange(ring_y, g)
    back = flat_call(
        backward_kernel,
        [pos] + [(vmem(), a) for a in g + lines + [q_all, p_all]],
        [out((rows, 256), BF)] * 4 + [out((512, 256), F32), out((512, 256), BF), out((512, 256), BF)],
        [
            pltpu.VMEM((1536, HEAD), F32),
            pltpu.VMEM((1536, HEAD), F32),
            pltpu.VMEM((4, rows, 256), BF),
            pltpu.VMEM((4, rows, 256), BF),
        ],
        flops=2 * 4 * 1152 * 256 * 128 * 4,
        moved=6 << 20,
        limit=24,
    )
    dq, (own, to_near, to_far) = back[:4], back[4:]
    from_far = lines_on(to_far, -2)
    from_near = lines_on(to_near, -1)
    dq = exchange(ring_y, dq)
    pair = call(
        pair_kernel,
        (1,),
        [pos] + [(whole((512, 256)), a) for a in (own, from_near, from_far)],
        [out((rows, 256), BF)] * 4,
        moved=1 << 20,
    )
    mixed_pair = exchange(ring_y, pair)

    part = (16 * PIECE, 256)
    stage = call(
        weight_kernel,
        (1,),
        [pos] + [(hbm(), a) for a in [columns] + halves + partner_halves] + [(small, a) for a in pair],
        [out(part, BF)] * 4 + [out((8 * PIECE, 256), BF)] * 2,
        [pltpu.VMEM((64 * PIECE, 512), BF), pltpu.SemaphoreType.DMA((7,))],
        flops=2 * 3072 * 512 * 256,
        moved=5 << 20,
    )
    first = stage[0]
    stage = across(stage)
    stage = flat_call(
        middle_kernel,
        [pos] + [(vmem(), v) for v in stage],
        [out((4 * PIECE, 256), BF)] * 4,
        [pltpu.VMEM((16 * PIECE, 256), F32)],
        moved=2 << 20,
    )
    stage = exchange(ring_z, stage)
    stage = flat_call(
        last_kernel,
        [pos] + [(vmem(), v) for v in stage],
        [out((PIECE, 256), F32)] * 4,
        moved=1 << 19,
    )
    stage = exchange(ring_y, stage)
    (weight_grad,) = call(
        place_kernel,
        (1,),
        [pos] + [(whole((PIECE, 256)), v) for v in stage],
        [out((width // 64, 2, 512), F32)],
        moved=1 << 18,
    )

    (base,) = flat_call(
        query_input_kernel,
        [pos] + [(vmem(), a) for a in dq] + [(vmem(), w_query), (hbm(), first)],
        [out((width, rows), F32)],
        [wide],
        flops=2 * rows * width * 1024,
        moved=2 * width * 1024,
    )
    narrow = pltpu.VMEM((rows, 512), BF)
    kept, given = flat_call(
        pair_input_kernel,
        [pos]
        + [(vmem(), c) for c in mixed_pair]
        + [(vmem(), base), (vmem(), w_key), (vmem(), value_weight)],
        [out((width // 2, rows), F32), out((width // 2, rows), BF)],
        [narrow, narrow, pltpu.VMEM((width, rows), F32)],
        flops=2 * rows * width * 1024,
        moved=2 * width * 1024,
    )
    theirs = other_core(given)
    input_grad = (kept + theirs.astype(F32)).astype(BF).T
    return input_grad, weight_grad


def solution(mesh):
    placed = (
        P("seq", None),
        P("seq", None),
        P(None, "mp"),
        P(None, "mp"),
        P(None, "mp"),
        P("mp", None),
    )
    return jax.shard_map(
        on_device,
        mesh=mesh,
        in_specs=placed,
        out_specs=(P("seq", "mp"), P("seq", None, "mp")),
        check_vma=False,
    )
```

time: 164 us -> 163 us (level)
  starting transfers between devices: 67.3 us -> 77 us
  Pallas kernels: 40.7 us -> 35.6 us
  waiting for transfers between devices: 40.2 us -> 36.6 us
  local copies, waits for them, and re-layouts: 12.4 us -> 10.7 us
    pallas_call x5 -> x3, Pallas kernels: 20.8 us -> 4.68 us  [call(): pl.pallas_call(kernel, grid_spec=pltpu.PrefetchScalarGridSpec(num_scalar_...]
    pallas_call x9 -> x12, Pallas kernels: 20 us -> 30.9 us  [flat_call(): pl.pallas_call(kernel, in_specs=[pl.BlockSpec(memory_space=pltpu.SMEM)] +...]
    ppermute x0 -> x2, starting transfers between devices: none -> 8.32 us  [the longest x1 4.22 us: far_two(): return lax.ppermute(x, 'seq', route)]
    ppermute x4, waiting for transfers between devices: 15.6 us -> 10.8 us  [lines_on(): lax.ppermute(x, 'seq', [(i, i + 4 * d) for i in range(64) if 0 <= i + 4 *...]
    ppermute x4, starting transfers between devices: 11.6 us -> 8.26 us  [lines_on(): lax.ppermute(x, 'seq', [(i, i + 4 * d) for i in range(64) if 0 <= i + 4 *...]
    ppermute x3 -> x6, starting transfers between devices: 9.61 us -> 12.5 us  [ring_x(): lax.ppermute(x, 'seq', [(i, (i // 16 + d) % 4 * 16 + i % 16) for i in ran...]
    ppermute x3 -> x6, waiting for transfers between devices: 2.1 us -> 4.76 us  [ring_x(): lax.ppermute(x, 'seq', [(i, (i // 16 + d) % 4 * 16 + i % 16) for i in ran...]
    ppermute x24, waiting for transfers between devices: 20 us -> 18 us  [ring_y(): lax.ppermute(x, 'seq', [(i, i // 4 * 4 + (i + d) % 4) for i in range(64)])]
  transfers between devices with their start and end apart: 39 -> 44, of which waited for: 22 -> 18; matrix products, arithmetic and copies ran while one was open for 1% -> 1% of each run, Pallas kernels for 14% -> 12%
where the time goes in v1:
time: 163 us; the launch traced here: 162 us
  starting transfers between devices  77 us (47%)
  waiting for transfers between devices  36.6 us (22%)
  Pallas kernels  35.6 us (22%)
  local copies, waits for them, and re-layouts  10.7 us (7%)
    ppermute x24, starting transfers between devices, ring_y(): lax.ppermute(x, 'seq', [(i, i // 4 * 4 + (i + d) % 4) for i in range(64)])  39.6 us
    pallas_call x12, Pallas kernels, flat_call(): pl.pallas_call(kernel, in_specs=[pl.BlockSpec(memory_space=pltpu.SMEM)] +...  30.9 us
    ppermute x24, waiting for transfers between devices, ring_y(): lax.ppermute(x, 'seq', [(i, i // 4 * 4 + (i + d) % 4) for i in range(64)])  18 us
    ppermute x6, starting transfers between devices, ring_x(): lax.ppermute(x, 'seq', [(i, (i // 16 + d) % 4 * 16 + i % 16) for i in ran...  12.5 us
    ppermute x4, waiting for transfers between devices, lines_on(): lax.ppermute(x, 'seq', [(i, i + 4 * d) for i in range(64) if 0 <= i + 4 *...  10.8 us
    unnamed x44, local copies, waits for them, and re-layouts  10.4 us
    ppermute x4, starting transfers between devices, lines_on(): lax.ppermute(x, 'seq', [(i, i + 4 * d) for i in range(64) if 0 <= i + 4 *...  8.26 us
    ppermute x3, starting transfers between devices, ring_z(): lax.ppermute(x, 'seq', [(i, i // 16 * 16 + (i // 4 + d) % 4 * 4 + i % 4)...  7.73 us
  transfers between devices with their start and end apart: 44, of which 18 were waited for; matrix products, arithmetic and copies ran while one was open for 1% of the time, Pallas kernels for 12%

profile of v1, /device:TPU:0, one launch (start us, length us, event | category | flops | bytes accessed | tf_op | source)
XLA Modules:
  0.0 162.4 jit_solution(9749935671816520449)
XLA Ops:
  1.3 6.0 %shard_map.77 = (bf16[4,128,128]{2,1,0:T(8,128)(2,1)}, bf16[4,128,128]{2,1,0:T(8,128)(2,1)}, bf16[4,128,128]{2,1,0:T(8,128)(2,1)}, bf16[4,128,128]{2,1,0:T(8,128)(2,1)}) custom-call(s32[4]{0:T(128)} %pad_add_fusion.pos, bf16[128,2688]{1,0:T(8,128)(2,1)} %tok.3, bf16[128,2688]{1,0:T(8,128)(2,1)} %tan.3, bf16[2688,512]{1,0:T(8,128)(2,1)} %wk.3, ...), custom_call_target="tpu_custom_call" | custom-call | flops 1409286144 | bytes 5505024 | tf_op jit(solution)/shard_map/pallas_call | solution.py:92
  9.0 2.9 %collective-permute-start.1 = (bf16[4,128,128]{2,1,0:T(8,128)(2,1)}, bf16[4,128,128]{2,1,0:T(8,128)(2,1)S(1)}, u32[]{:S(2)}, u32[]{:S(2)}) collective-permute-start(bf16[4,128,128]{2,1,0:T(8,128)(2,1)} %get-tuple-element.54), channel_id=1, source_target_pairs={{0,4},{2,6},{4,0},{6,2},{8,12},{10,14},{12,8},{14,10},{16,20},{18,... | collective-permute-start | bytes 393224 | tf_op jit(solution)/shard_map/ppermute | solution.py:28
  14.2 4.0 %collective-permute-done.1.c = bf16[4,128,128]{2,1,0:T(8,128)(2,1)S(1)} collective-permute-done((bf16[4,128,128]{2,1,0:T(8,128)(2,1)}, bf16[4,128,128]{2,1,0:T(8,128)(2,1)S(1)}, u32[]{:S(2)}, u32[]{:S(2)}) %collective-permute-start.1) | collective-permute-done | bytes 131104 | tf_op jit(solution)/shard_map/ppermute | solution.py:28
  19.8 4.1 %collective-permute-start.4 = (bf16[256,512]{1,0:T(8,128)(2,1)S(1)}, bf16[256,512]{1,0:T(8,128)(2,1)S(1)}, u32[]{:S(2)}, u32[]{:S(2)}) collective-permute-start(bf16[256,512]{1,0:T(8,128)(2,1)S(1)} %get-tuple-element.57), channel_id=1, source_target_pairs={{0,24},{2,26},{4,28},{6,30},{8,0},{10,2},{12,4},{14,6},{16,8},{18,... | collective-permute-start | bytes 786440 | tf_op jit(solution)/shard_map/ppermute | solution.py:51
  25.2 2.6 %copy-done.2 = bf16[2688,1024]{1,0:T(8,128)(2,1)S(1)} copy-done((bf16[2688,1024]{1,0:T(8,128)(2,1)S(1)}, bf16[2688,1024]{1,0:T(8,128)(2,1)}, u32[]{:S(2)}) %copy-start.2) | copy-done | bytes 5505048
  31.3 4.4 %collective-permute-start.3 = (bf16[256,512]{1,0:T(8,128)(2,1)S(1)}, bf16[256,512]{1,0:T(8,128)(2,1)S(1)}, u32[]{:S(2)}, u32[]{:S(2)}) collective-permute-start(bf16[256,512]{1,0:T(8,128)(2,1)S(1)} %get-tuple-element.56), channel_id=1, source_target_pairs={{0,16},{2,18},{4,20},{6,22},{8,24},{10,26},{12,28},{14,30},{16,32}... | collective-permute-start | bytes 786440 | tf_op jit(solution)/shard_map/ppermute | solution.py:42
  35.7 4.2 %collective-permute-start.5 = (bf16[256,512]{1,0:T(8,128)(2,1)S(1)}, bf16[256,512]{1,0:T(8,128)(2,1)S(1)}, u32[]{:S(2)}, u32[]{:S(2)}) collective-permute-start(bf16[256,512]{1,0:T(8,128)(2,1)S(1)} %collective-permute-done.4), channel_id=1, source_target_pairs={{0,24},{2,26},{4,28},{6,30},{8,32},{10,34},{12,36},{14,38},{16,40}... | collective-permute-start | bytes 786440 | tf_op jit(solution)/shard_map/ppermute | solution.py:62
  44.0 2.5 %collective-permute-done.8.q2 = bf16[2,128,256]{2,1,0:T(8,128)(2,1)S(1)} collective-permute-done((bf16[2,128,256]{2,1,0:T(8,128)(2,1)S(1)}, bf16[2,128,256]{2,1,0:T(8,128)(2,1)S(1)}, u32[]{:S(2)}, u32[]{:S(2)}) %collective-permute-start.8) | collective-permute-done | bytes 131104 | tf_op jit(solution)/shard_map/ppermute | solution.py:28
  48.0 5.4 %shard_map.80 = (bf16[128,256]{1,0:T(8,128)(2,1)S(1)}, bf16[128,256]{1,0:T(8,128)(2,1)S(1)}, bf16[128,256]{1,0:T(8,128)(2,1)S(1)}, bf16[128,256]{1,0:T(8,128)(2,...) custom-call(s32[4]{0:T(128)S(1)} %copy-done.11, ...), custom_call_target="tpu_custom_call" | custom-call | flops 1509949440 | bytes 8388608 | tf_op jit(solution)/shard_map/pallas_call | solution.py:92
  67.8 3.1 %collective-permute-start.26 = (bf16[1344,128]{1,0:T(8,128)(2,1)S(1)}, bf16[1344,128]{1,0:T(8,128)(2,1)S(1)}, u32[]{:S(2)}, u32[]{:S(2)}) collective-permute-start(bf16[1344,128]{1,0:T(8,128)(2,1)S(1)} %dynamic-slice_bitcast_fusion), channel_id=1, source_target_pairs={{0,4},{2,6},{4,0},{6,2},{8,12},{10,14},{12,8},{14,10},{16,20},{18,... | collective-permute-start | bytes 1032200 | tf_op jit(solution)/shard_map/ppermute | solution.py:28
  71.2 2.6 %copy-done.1 = bf16[1024,2688]{1,0:T(8,128)(2,1)S(1)} copy-done((bf16[1024,2688]{1,0:T(8,128)(2,1)S(1)}, bf16[1024,2688]{1,0:T(8,128)(2,1)}, u32[]{:S(2)}) %copy-start.1) | copy-done | bytes 5505048
  75.1 2.5 %shard_map.83 = (bf16[128,256]{1,0:T(8,128)(2,1)S(1)}, bf16[128,256]{1,0:T(8,128)(2,1)S(1)}, bf16[128,256]{1,0:T(8,128)(2,1)S(1)}, bf16[128,256]{1,0:T(8,128)(2,1)S(1)}) custom-call(s32[4]{0:T(128)S(1)} %copy-done.11, f32[128,2688]{1,0:T(8,128)S(1)} %copy-done.9, bf16[128,2688]{1,0:T(8,128)(2,1)S(1)} %collective-permute-done.13.other, ...), custom_call_target="tpu_custom_call" | custom-call | flops 704643072 | bytes 5505024 | tf_op jit(solution)/shard_map/pallas_call | solution.py:92
  82.2 5.0 %collective-permute-done.26.refs_2_ = bf16[1344,128]{1,0:T(8,128)(2,1)S(1)} collective-permute-done((bf16[1344,128]{1,0:T(8,128)(2,1)S(1)}, bf16[1344,128]{1,0:T(8,128)(2,1)S(1)}, u32[]{:S(2)}, u32[]{:S(2)}) %collective-permute-start.26) | collective-permute-done | bytes 344096 | tf_op jit(solution)/shard_map/ppermute | solution.py:28
  89.6 5.0 %shard_map.84 = (bf16[128,256]{1,0:T(8,128)(2,1)S(1)}, bf16[128,256]{1,0:T(8,128)(2,1)S(1)}, bf16[128,256]{1,0:T(8,128)(2,1)S(1)}, bf16[128,256]{1,0:T(8,128)(2,...) custom-call(s32[4]{0:T(128)S(1)} %copy-done.11, ...), custom_call_target="tpu_custom_call" | custom-call | flops 1207959552 | bytes 6291456 | tf_op jit(solution)/shard_map/pallas_call | solution.py:92
  97.2 8.2 %collective-permute-done.17.near = bf16[512,256]{1,0:T(8,128)(2,1)S(1)} collective-permute-done((bf16[512,256]{1,0:T(8,128)(2,1)S(1)}, bf16[512,256]{1,0:T(8,128)(2,1)S(1)}, u32[]{:S(2)}, u32[]{:S(2)}) %collective-permute-start.17) | collective-permute-done | bytes 262176 | tf_op jit(solution)/shard_map/ppermute | solution.py:42
  105.5 2.6 %collective-permute-done.18.far = bf16[512,256]{1,0:T(8,128)(2,1)S(1)} collective-permute-done((bf16[512,256]{1,0:T(8,128)(2,1)S(1)}, bf16[512,256]{1,0:T(8,128)(2,1)S(1)}, u32[]{:S(2)}, u32[]{:S(2)}) %collective-permute-start.18) | collective-permute-done | bytes 262176 | tf_op jit(solution)/shard_map/ppermute | solution.py:42
  110.0 3.0 %collective-permute-start.24 = (bf16[128,256]{1,0:T(8,128)(2,1)S(1)}, bf16[128,256]{1,0:T(8,128)(2,1)S(1)}, u32[]{:S(2)}, u32[]{:S(2)}) collective-permute-start(bf16[128,256]{1,0:T(8,128)(2,1)S(1)} %get-tuple-element.85), channel_id=1, source_target_pairs={{0,6},{2,0},{4,2},{6,4},{8,14},{10,8},{12,10},{14,12},{16,22},{18,... | collective-permute-start | bytes 196616 | tf_op jit(solution)/shard_map/ppermute | solution.py:28
  115.1 2.7 %shard_map.86 = (bf16[672,256]{1,0:T(8,128)(2,1)S(1)}, bf16[672,256]{1,0:T(8,128)(2,1)S(1)}, bf16[672,256]{1,0:T(8,128)(2,1)}, bf16[672,256]{1,0:T(8,128)(2,1)S(...) custom-call(s32[4]{0:T(128)S(1)} %copy-done.11, bf16[2688,128]{1,0:T(8,128)(2,1)S(1)} %bitcast.11, ...), custom_call_target="tpu_custom_call" | custom-call | flops 805306368 | bytes 5242880 | tf_op jit(solution)/shard_map/pallas_call | solution.py:72
  117.8 2.6 %collective-permute-start.21 = (bf16[128,256]{1,0:T(8,128)(2,1)S(1)}, bf16[128,256]{1,0:T(8,128)(2,1)S(1)}, u32[]{:S(2)}, u32[]{:S(2)}) collective-permute-start(bf16[128,256]{1,0:T(8,128)(2,1)S(1)} %get-tuple-element.81.refs_10_), channel_id=1, source_target_pairs={{0,6},{2,0},{4,2},{6,4},{8,14},{10,8},{12,10},{14,12},{16,22},{18,... | collective-permute-start | bytes 196616 | tf_op jit(solution)/shard_map/ppermute | solution.py:28
  120.5 4.6 %collective-permute-start.32 = (bf16[672,256]{1,0:T(8,128)(2,1)S(1)}, bf16[672,256]{1,0:T(8,128)(2,1)S(1)}, u32[]{:S(2)}, u32[]{:S(2)}) collective-permute-start(bf16[672,256]{1,0:T(8,128)(2,1)S(1)} %get-tuple-element.90), channel_id=1, source_target_pairs={{0,32},{2,34},{4,36},{6,38},{8,40},{10,42},{12,44},{14,46},{16,48}... | collective-permute-start | bytes 1032200 | tf_op jit(solution)/shard_map/ppermute | solution.py:38
  136.3 3.1 %collective-permute-start.37 = (bf16[336,256]{1,0:T(8,128)(2,1)S(1)}, bf16[336,256]{1,0:T(8,128)(2,1)S(1)}, u32[]{:S(2)}, u32[]{:S(2)}) collective-permute-start(bf16[336,256]{1,0:T(8,128)(2,1)S(1)} %collective-permute-done.36), channel_id=1, source_target_pairs={{0,96},{2,98},{4,100},{6,102},{8,104},{10,106},{12,108},{14,110},{... | collective-permute-start | bytes 516104 | tf_op jit(solution)/shard_map/ppermute | solution.py:38
  139.3 3.4 %collective-permute-done.35.up = bf16[336,256]{1,0:T(8,128)(2,1)S(1)} collective-permute-done((bf16[336,256]{1,0:T(8,128)(2,1)S(1)}, bf16[336,256]{1,0:T(8,128)(2,1)S(1)}, u32[]{:S(2)}, u32[]{:S(2)}) %collective-permute-start.35) | collective-permute-done | bytes 172064 | tf_op jit(solution)/shard_map/ppermute | solution.py:38
  143.5 3.2 %collective-permute-start.38 = (bf16[168,256]{1,0:T(8,128)(2,1)S(1)}, bf16[168,256]{1,0:T(8,128)(2,1)S(1)}, u32[]{:S(2)}, u32[]{:S(2)}) collective-permute-start(bf16[168,256]{1,0:T(8,128)(2,1)S(1)} %get-tuple-element.95), channel_id=1, source_target_pairs={{0,8},{2,10},{4,12},{6,14},{8,16},{10,18},{12,20},{14,22},{16,24},... | collective-permute-start | bytes 258056 | tf_op jit(solution)/shard_map/ppermute | solution.py:32
  156.7 2.5 %collective-permute-start.43 = (f32[42,256]{1,0:T(8,128)S(1)}, f32[42,256]{1,0:T(8,128)S(1)}, u32[]{:S(2)}, u32[]{:S(2)}) collective-permute-start(f32[42,256]{1,0:T(8,128)S(1)} %get-tuple-element.101), channel_id=1, source_target_pairs={{0,6},{2,0},{4,2},{6,4},{8,14},{10,8},{12,10},{14,12},{16,22},{18,... | collective-permute-start | bytes 129032 | tf_op jit(solution)/shard_map/ppermute | solution.py:28
  (128 shorter events, 71.2 us)
Async XLA Ops:
  19.8 15.9 %collective-permute-start.4 = (bf16[256,512]{1,0:T(8,128)(2,1)S(1)}, bf16[256,512]{1,0:T(8,128)(2,1)S(1)}, u32[]{:S(2)}, u32[]{:S(2)}) collective-permute-start(bf16[256,512]{1,0:T(8,128)(2,1)S(1)} %get-tuple-element.57), channel_id=1, source_target_pairs={{0,24},{2,26},{4,28},{6,30},{8,0},{10,2},{12,4},{14,6},{16,8},{18,... | collective-permute-start | bytes 786440 | tf_op jit(solution)/shard_map/ppermute | solution.py:51
  23.9 24.1 %collective-permute-start.6 = (bf16[512,512]{1,0:T(8,128)(2,1)S(1)}, bf16[512,512]{1,0:T(8,128)(2,1)S(1)}, u32[]{:S(2)}, u32[]{:S(2)}) collective-permute-start(bf16[512,512]{1,0:T(8,128)(2,1)S(1)} %get-tuple-element.58.own.own_kv), channel_id=1, source_target_pairs={{0,8},{2,10},{4,12},{6,14},{8,16},{10,18},{12,20},{14,22},{16,24},... | collective-permute-start | bytes 1572872 | tf_op jit(solution)/shard_map/ppermute | solution.py:42
  30.0 12.4 %collective-permute-start.7 = (bf16[2,128,256]{2,1,0:T(8,128)(2,1)S(1)}, bf16[2,128,256]{2,1,0:T(8,128)(2,1)S(1)}, u32[]{:S(2)}, u32[]{:S(2)}) collective-permute-start(bf16[2,128,256]{2,1,0:T(8,128)(2,1)S(1)} %get-tuple-element.60), channel_id=1, source_target_pairs={{0,2},{2,4},{4,6},{6,0},{8,10},{10,12},{12,14},{14,8},{16,18},{18,... | collective-permute-start | bytes 393224 | tf_op jit(solution)/shard_map/ppermute | solution.py:28
  31.3 16.1 %collective-permute-start.3 = (bf16[256,512]{1,0:T(8,128)(2,1)S(1)}, bf16[256,512]{1,0:T(8,128)(2,1)S(1)}, u32[]{:S(2)}, u32[]{:S(2)}) collective-permute-start(bf16[256,512]{1,0:T(8,128)(2,1)S(1)} %get-tuple-element.56), channel_id=1, source_target_pairs={{0,16},{2,18},{4,20},{6,22},{8,24},{10,26},{12,28},{14,30},{16,32}... | collective-permute-start | bytes 786440 | tf_op jit(solution)/shard_map/ppermute | solution.py:42
  35.7 12.3 %collective-permute-start.5 = (bf16[256,512]{1,0:T(8,128)(2,1)S(1)}, bf16[256,512]{1,0:T(8,128)(2,1)S(1)}, u32[]{:S(2)}, u32[]{:S(2)}) collective-permute-start(bf16[256,512]{1,0:T(8,128)(2,1)S(1)} %collective-permute-done.4), channel_id=1, source_target_pairs={{0,24},{2,26},{4,28},{6,30},{8,32},{10,34},{12,36},{14,38},{16,40}... | collective-permute-start | bytes 786440 | tf_op jit(solution)/shard_map/ppermute | solution.py:62
  66.7 13.2 %collective-permute-start.25 = (bf16[1344,128]{1,0:T(8,128)(2,1)S(1)}, bf16[1344,128]{1,0:T(8,128)(2,1)S(1)}, u32[]{:S(2)}, u32[]{:S(2)}) collective-permute-start(bf16[1344,128]{1,0:T(8,128)(2,1)S(1)} %dynamic-slice_bitcast_fusion), channel_id=1, source_target_pairs={{0,2},{2,4},{4,6},{6,0},{8,10},{10,12},{12,14},{14,8},{16,18},{18,... | collective-permute-start | bytes 1032200 | tf_op jit(solution)/shard_map/ppermute | solution.py:28
  67.8 19.4 %collective-permute-start.26 = (bf16[1344,128]{1,0:T(8,128)(2,1)S(1)}, bf16[1344,128]{1,0:T(8,128)(2,1)S(1)}, u32[]{:S(2)}, u32[]{:S(2)}) collective-permute-start(bf16[1344,128]{1,0:T(8,128)(2,1)S(1)} %dynamic-slice_bitcast_fusion), channel_id=1, source_target_pairs={{0,4},{2,6},{4,0},{6,2},{8,12},{10,14},{12,8},{14,10},{16,20},{18,... | collective-permute-start | bytes 1032200 | tf_op jit(solution)/shard_map/ppermute | solution.py:28
  70.9 16.3 %collective-permute-start.27 = (bf16[1344,128]{1,0:T(8,128)(2,1)S(1)}, bf16[1344,128]{1,0:T(8,128)(2,1)S(1)}, u32[]{:S(2)}, u32[]{:S(2)}) collective-permute-start(bf16[1344,128]{1,0:T(8,128)(2,1)S(1)} %dynamic-slice_bitcast_fusion), channel_id=1, source_target_pairs={{0,6},{2,0},{4,2},{6,4},{8,14},{10,8},{12,10},{14,12},{16,22},{18,... | collective-permute-start | bytes 1032200 | tf_op jit(solution)/shard_map/ppermute | solution.py:28
  77.6 11.0 %collective-permute-start.14 = (bf16[128,256]{1,0:T(8,128)(2,1)S(1)}, bf16[128,256]{1,0:T(8,128)(2,1)S(1)}, u32[]{:S(2)}, u32[]{:S(2)}) collective-permute-start(bf16[128,256]{1,0:T(8,128)(2,1)S(1)} %get-tuple-element.70), channel_id=1, source_target_pairs={{0,2},{2,4},{4,6},{6,0},{8,10},{10,12},{12,14},{14,8},{16,18},{18,... | collective-permute-start | bytes 196616 | tf_op jit(solution)/shard_map/ppermute | solution.py:28
  79.4 10.2 %collective-permute-start.15 = (bf16[128,256]{1,0:T(8,128)(2,1)S(1)}, bf16[128,256]{1,0:T(8,128)(2,1)S(1)}, u32[]{:S(2)}, u32[]{:S(2)}) collective-permute-start(bf16[128,256]{1,0:T(8,128)(2,1)S(1)} %get-tuple-element.71), channel_id=1, source_target_pairs={{0,4},{2,6},{4,0},{6,2},{8,12},{10,14},{12,8},{14,10},{16,20},{18,... | collective-permute-start | bytes 196616 | tf_op jit(solution)/shard_map/ppermute | solution.py:28
  87.2 22.8 %collective-permute-start.28 = (bf16[1344,128]{1,0:T(8,128)(2,1)S(1)}, bf16[1344,128]{1,0:T(8,128)(2,1)S(1)}, u32[]{:S(2)}, u32[]{:S(2)}) collective-permute-start(bf16[1344,128]{1,0:T(8,128)(2,1)S(1)} %collective-permute-done.25.refs_1_), channel_id=1, source_target_pairs={{0,1},{1,0},{2,3},{3,2},{4,5},{5,4},{6,7},{7,6},{8,9},{9,8},{10,11... | collective-permute-start | bytes 1032200 | tf_op jit(solution)/shard_map/ppermute | solution.py:66
  87.2 25.8 %collective-permute-start.29 = (bf16[1344,128]{1,0:T(8,128)(2,1)S(1)}, bf16[1344,128]{1,0:T(8,128)(2,1)S(1)}, u32[]{:S(2)}, u32[]{:S(2)}) collective-permute-start(bf16[1344,128]{1,0:T(8,128)(2,1)S(1)} %collective-permute-done.26.refs_2_), channel_id=1, source_target_pairs={{0,1},{1,0},{2,3},{3,2},{4,5},{5,4},{6,7},{7,6},{8,9},{9,8},{10,11... | collective-permute-start | bytes 1032200 | tf_op jit(solution)/shard_map/ppermute | solution.py:66
  88.5 24.5 %collective-permute-start.30 = (bf16[1344,128]{1,0:T(8,128)(2,1)S(1)}, bf16[1344,128]{1,0:T(8,128)(2,1)S(1)}, u32[]{:S(2)}, u32[]{:S(2)}) collective-permute-start(bf16[1344,128]{1,0:T(8,128)(2,1)S(1)} %collective-permute-done.27.refs_3_), channel_id=1, source_target_pairs={{0,1},{1,0},{2,3},{3,2},{4,5},{5,4},{6,7},{7,6},{8,9},{9,8},{10,11... | collective-permute-start | bytes 1032200 | tf_op jit(solution)/shard_map/ppermute | solution.py:66
  94.6 10.8 %collective-permute-start.17 = (bf16[512,256]{1,0:T(8,128)(2,1)S(1)}, bf16[512,256]{1,0:T(8,128)(2,1)S(1)}, u32[]{:S(2)}, u32[]{:S(2)}) collective-permute-start(bf16[512,256]{1,0:T(8,128)(2,1)S(1)} %get-tuple-element.76), channel_id=1, source_target_pairs={{8,0},{10,2},{12,4},{14,6},{16,8},{18,10},{20,12},{22,14},{24,16},... | collective-permute-start | bytes 786440 | tf_op jit(solution)/shard_map/ppermute | solution.py:42
  95.9 12.2 %collective-permute-start.18 = (bf16[512,256]{1,0:T(8,128)(2,1)S(1)}, bf16[512,256]{1,0:T(8,128)(2,1)S(1)}, u32[]{:S(2)}, u32[]{:S(2)}) collective-permute-start(bf16[512,256]{1,0:T(8,128)(2,1)S(1)} %get-tuple-element.77), channel_id=1, source_target_pairs={{16,0},{18,2},{20,4},{22,6},{24,8},{26,10},{28,12},{30,14},{32,16}... | collective-permute-start | bytes 786440 | tf_op jit(solution)/shard_map/ppermute | solution.py:42
  105.5 12.4 %collective-permute-start.22 = (bf16[128,256]{1,0:T(8,128)(2,1)S(1)}, bf16[128,256]{1,0:T(8,128)(2,1)S(1)}, u32[]{:S(2)}, u32[]{:S(2)}) collective-permute-start(bf16[128,256]{1,0:T(8,128)(2,1)S(1)} %get-tuple-element.83), channel_id=1, source_target_pairs={{0,2},{2,4},{4,6},{6,0},{8,10},{10,12},{12,14},{14,8},{16,18},{18,... | collective-permute-start | bytes 196616 | tf_op jit(solution)/shard_map/ppermute | solution.py:28
  108.1 12.3 %collective-permute-start.23 = (bf16[128,256]{1,0:T(8,128)(2,1)S(1)}, bf16[128,256]{1,0:T(8,128)(2,1)S(1)}, u32[]{:S(2)}, u32[]{:S(2)}) collective-permute-start(bf16[128,256]{1,0:T(8,128)(2,1)S(1)} %get-tuple-element.84), channel_id=1, source_target_pairs={{0,4},{2,6},{4,0},{6,2},{8,12},{10,14},{12,8},{14,10},{16,20},{18,... | collective-permute-start | bytes 196616 | tf_op jit(solution)/shard_map/ppermute | solution.py:28
  110.0 15.1 %collective-permute-start.24 = (bf16[128,256]{1,0:T(8,128)(2,1)S(1)}, bf16[128,256]{1,0:T(8,128)(2,1)S(1)}, u32[]{:S(2)}, u32[]{:S(2)}) collective-permute-start(bf16[128,256]{1,0:T(8,128)(2,1)S(1)} %get-tuple-element.85), channel_id=1, source_target_pairs={{0,6},{2,0},{4,2},{6,4},{8,14},{10,8},{12,10},{14,12},{16,22},{18,... | collective-permute-start | bytes 196616 | tf_op jit(solution)/shard_map/ppermute | solution.py:28
  113.0 13.5 %collective-permute-start.19 = (bf16[128,256]{1,0:T(8,128)(2,1)S(1)}, bf16[128,256]{1,0:T(8,128)(2,1)S(1)}, u32[]{:S(2)}, u32[]{:S(2)}) collective-permute-start(bf16[128,256]{1,0:T(8,128)(2,1)S(1)} %get-tuple-element.79.refs_8_), channel_id=1, source_target_pairs={{0,2},{2,4},{4,6},{6,0},{8,10},{10,12},{12,14},{14,8},{16,18},{18,... | collective-permute-start | bytes 196616 | tf_op jit(solution)/shard_map/ppermute | solution.py:28
  113.1 15.1 %collective-permute-start.20 = (bf16[128,256]{1,0:T(8,128)(2,1)S(1)}, bf16[128,256]{1,0:T(8,128)(2,1)S(1)}, u32[]{:S(2)}, u32[]{:S(2)}) collective-permute-start(bf16[128,256]{1,0:T(8,128)(2,1)S(1)} %get-tuple-element.80.refs_9_), channel_id=1, source_target_pairs={{0,4},{2,6},{4,0},{6,2},{8,12},{10,14},{12,8},{14,10},{16,20},{18,... | collective-permute-start | bytes 196616 | tf_op jit(solution)/shard_map/ppermute | solution.py:28
  117.8 14.1 %collective-permute-start.21 = (bf16[128,256]{1,0:T(8,128)(2,1)S(1)}, bf16[128,256]{1,0:T(8,128)(2,1)S(1)}, u32[]{:S(2)}, u32[]{:S(2)}) collective-permute-start(bf16[128,256]{1,0:T(8,128)(2,1)S(1)} %get-tuple-element.81.refs_10_), channel_id=1, source_target_pairs={{0,6},{2,0},{4,2},{6,4},{8,14},{10,8},{12,10},{14,12},{16,22},{18,... | collective-permute-start | bytes 196616 | tf_op jit(solution)/shard_map/ppermute | solution.py:28
  120.5 18.9 %collective-permute-start.32 = (bf16[672,256]{1,0:T(8,128)(2,1)S(1)}, bf16[672,256]{1,0:T(8,128)(2,1)S(1)}, u32[]{:S(2)}, u32[]{:S(2)}) collective-permute-start(bf16[672,256]{1,0:T(8,128)(2,1)S(1)} %get-tuple-element.90), channel_id=1, source_target_pairs={{0,32},{2,34},{4,36},{6,38},{8,40},{10,42},{12,44},{14,46},{16,48}... | collective-permute-start | bytes 1032200 | tf_op jit(solution)/shard_map/ppermute | solution.py:38
  125.1 14.3 %collective-permute-start.33 = (bf16[672,256]{1,0:T(8,128)(2,1)S(1)}, bf16[672,256]{1,0:T(8,128)(2,1)S(1)}, u32[]{:S(2)}, u32[]{:S(2)}) collective-permute-start(bf16[672,256]{1,0:T(8,128)(2,1)S(1)} %get-tuple-element.91), channel_id=1, source_target_pairs={{0,96},{2,98},{4,100},{6,102},{8,104},{10,106},{12,108},{14,110},{... | collective-permute-start | bytes 1032200 | tf_op jit(solution)/shard_map/ppermute | solution.py:38
  134.6 24.7 %collective-permute-start.31 = (bf16[1344,128]{1,0:T(8,128)(2,1)S(1)}, bf16[1344,128]{1,0:T(8,128)(2,1)S(1)}, u32[]{:S(2)}, u32[]{:S(2)}) collective-permute-start(bf16[1344,128]{1,0:T(8,128)(2,1)S(1)} %get-tuple-element.89), channel_id=1, source_target_pairs={{0,1},{1,0},{2,3},{3,2},{4,5},{5,4},{6,7},{7,6},{8,9},{9,8},{10,11... | collective-permute-start | bytes 1032200 | tf_op jit(solution)/shard_map/ppermute | solution.py:66
  (42 other events, 403.0 us)

commit v2 on v1

--- a/solution.py
+++ b/solution.py
@@ -39,7 +39,7 @@
 
 
 def lines_on(x, d):
-    return lax.ppermute(x, "seq", [(i, i + 4 * d) for i in range(64) if 0 <= i + 4 * d < 64])
+    return lax.ppermute(x, "seq", [(i, (i + 4 * d) % 64) for i in range(64)])
 
 
 def exchange(ring, chunks):
@@ -57,8 +57,7 @@
     route = []
     for i in range(64):
         source = i // 16 * 16 + (i // 4 + 1) % 4 * 4 + i % 4
-        if source + 8 < 64:
-            route.append((i, source + 8))
+        route.append((i, (source + 8) % 64))
     return lax.ppermute(x, "seq", route)
 
 
@@ -88,16 +87,19 @@
 
 def flat_call(kernel, ins, outs, scratch=(), flops=0, moved=0, limit=20):
     specs_in, values = zip(*ins[1:])
+    if ins[0] is not None:
+        specs_in = (pl.BlockSpec(memory_space=pltpu.SMEM),) + specs_in
+        values = (ins[0],) + values
     _, shapes = zip(*outs)
     return pl.pallas_call(
         kernel,
-        in_specs=[pl.BlockSpec(memory_space=pltpu.SMEM)] + list(specs_in),
+        in_specs=list(specs_in),
         out_specs=[pl.BlockSpec(memory_space=pltpu.VMEM)] * len(shapes),
         scratch_shapes=list(scratch),
         out_shape=list(shapes),
         compiler_params=pltpu.CompilerParams(vmem_limit_bytes=limit << 20),
         cost_estimate=pl.CostEstimate(flops=flops, bytes_accessed=moved, transcendentals=0),
-    )(ins[0], *values)
+    )(*values)
 
 
 def whole(shape):
@@ -120,10 +122,11 @@
     return whole(shape), jax.ShapeDtypeStruct(shape, dtype)
 
 
-CUTS = (0, 640, 1280, 1920, 2688)
-
-
-def key_value_kernel(pos, tok, tan, wk, wv, *refs):
+CUTS = (0, 512, 1152, 1920, 2688)
+
+
+def key_value_kernel(tok, tan, wk, wv, *refs):
+    y = lax.rem(lax.axis_index("seq"), 4)
     outs, (both, w, acc, flat, sem) = refs[:4], refs[4:]
     rows = tok.shape[0]
     half = wk.shape[1]
@@ -157,7 +160,7 @@
         else:
             flat[...] = (acc[...] + res).astype(BF)
     for d in range(4):
-        head = lax.rem(pos[2] + d, 4) * HEAD
+        head = lax.rem(y + d, 4) * HEAD
         k = flat[:, pl.ds(pl.multiple_of(head, HEAD), HEAD)]
         v = flat[:, pl.ds(pl.multiple_of(head + half, HEAD), HEAD)]
         outs[d][0] = k[:rows]
@@ -319,7 +322,7 @@
         ).astype(BF)
 
 
-def query_input_kernel(pos, q0, q1, q2, q3, w, _, total, buf):
+def query_input_kernel(pos, q0, q1, q2, q3, w, total, buf):
     place_heads(pos, (q0[...], q1[...], q2[...], q3[...]), buf, 256)
     total[...] = mm(w[...], buf[...], NT)
 
@@ -334,15 +337,11 @@
     given[...] = total[pl.ds(pl.multiple_of((1 - pos[3]) * half, half), half), :].astype(BF)
 
 
-def weight_kernel(pos, *refs):
-    mine, r1, r2, r3, p1, p2, p3, c0, c1, c2, c3 = refs[:11]
-    outs = refs[11:17]
-    line, sems = refs[17:]
-    core = pos[3]
+def token_kernel(pos, mine, r1, r2, r3, p1, p2, p3, line, sems):
     half = r1.shape[0]
     copies = [pltpu.make_async_copy(mine, line.at[:, pl.ds(0, HEAD)], sems.at[0])]
     for d, (r, p) in enumerate(((r1, p1), (r2, p2), (r3, p3)), 1):
-        for j, (src, where) in enumerate(((r, core), (p, 1 - core))):
+        for j, (src, where) in enumerate(((r, pos[3]), (p, 1 - pos[3]))):
             rows = pl.ds(pl.multiple_of(where * half, half), half)
             copies.append(
                 pltpu.make_async_copy(
@@ -353,6 +352,9 @@
         c.start()
     for c in copies:
         c.wait()
+
+
+def weight_kernel(pos, line, c0, c1, c2, c3, *outs):
     pair = jnp.concatenate([c0[...], c3[...], c2[...], c1[...]], axis=0)
     size = 16 * PIECE
     for d in range(4):
@@ -360,17 +362,6 @@
         block = line[pl.ds(pl.multiple_of(x * size, size), size), :]
         part = mm(block, pair).astype(BF)
         outs[d][...] = part
-        if d == 2:
-            outs[4][...] = part[: size // 2]
-            outs[5][...] = part[size // 2 :]
-
-
-def across(stage):
-    up = ring_x(stage[4], 1)
-    down = ring_x(stage[5], 3)
-    one, three = ring_x(stage[1], 1), ring_x(stage[3], 3)
-    up, down = ring_x(up, 1), ring_x(down, 3)
-    return [stage[0], one, three, up, down]
 
 
 def add_up(ins, rows):
@@ -380,12 +371,10 @@
     return total
 
 
-def middle_kernel(pos, mine, one, three, up, down, *refs):
-    outs, total = refs[:4], refs[4]
+def middle_kernel(pos, *refs):
+    ins, outs, total = refs[:4], refs[4:8], refs[8]
     size = 4 * PIECE
-    for i, half in enumerate((up, down)):
-        rows = slice(i * half.shape[0], (i + 1) * half.shape[0])
-        total[rows, :] = add_up((mine, one, three), rows) + half[...].astype(F32)
+    total[...] = add_up(ins, slice(None))
     for d in range(4):
         rows = pl.ds(pl.multiple_of(lax.rem(pos[1] + d, 4) * size, 8), size)
         outs[d][...] = total[rows, :].astype(BF)
@@ -421,7 +410,7 @@
     tan_in = (far_memory(), tangent)
     kv = flat_call(
         key_value_kernel,
-        [pos, tok_in, tan_in, (far_memory(), w_key), (far_memory(), value_weight)],
+        [None, tok_in, tan_in, (far_memory(), w_key), (far_memory(), value_weight)],
         piece_out,
         [
             pltpu.VMEM((2 * rows, width), BF),
@@ -526,17 +515,21 @@
     mixed_pair = exchange(ring_y, pair)
 
     part = (16 * PIECE, 256)
-    stage = call(
+    (token_line,) = flat_call(
+        token_kernel,
+        [pos] + [(hbm(), a) for a in [columns] + halves + partner_halves],
+        [out((width, 512), BF)],
+        [pltpu.SemaphoreType.DMA((7,))],
+        moved=5 << 20,
+    )
+    stage = flat_call(
         weight_kernel,
-        (1,),
-        [pos] + [(hbm(), a) for a in [columns] + halves + partner_halves] + [(small, a) for a in pair],
-        [out(part, BF)] * 4 + [out((8 * PIECE, 256), BF)] * 2,
-        [pltpu.VMEM((64 * PIECE, 512), BF), pltpu.SemaphoreType.DMA((7,))],
-        flops=2 * 3072 * 512 * 256,
+        [pos, (vmem(), token_line)] + [(vmem(), a) for a in pair],
+        [out(part, BF)] * 4,
+        flops=2 * 2688 * 512 * 256,
         moved=5 << 20,
     )
-    first = stage[0]
-    stage = across(stage)
+    stage = exchange(ring_x, stage)
     stage = flat_call(
         middle_kernel,
         [pos] + [(vmem(), v) for v in stage],
@@ -562,7 +555,7 @@
 
     (base,) = flat_call(
         query_input_kernel,
-        [pos] + [(vmem(), a) for a in dq] + [(vmem(), w_query), (hbm(), first)],
+        [pos] + [(vmem(), a) for a in dq] + [(vmem(), w_query)],
         [out((width, rows), F32)],
         [wide],
         flops=2 * rows * width * 1024,

time: 163 us -> 151 us (0.926)
  starting transfers between devices: 77 us -> 69.1 us
  Pallas kernels: 35.6 us -> 33.7 us
    ppermute x6 -> x3, starting transfers between devices: 12.5 us -> 6.39 us  [ring_x(): lax.ppermute(x, 'seq', [(i, (i // 16 + d) % 4 * 16 + i % 16) for i in ran...]
    ppermute x4, waiting for transfers between devices: 10.8 us -> 5.46 us  [lines_on(): return lax.ppermute(x, 'seq', [(i, (i + 4 * d) % 64) for i in range(64)])]
    ppermute x6 -> x3, waiting for transfers between devices: 4.76 us -> 7.72 us  [ring_x(): lax.ppermute(x, 'seq', [(i, (i // 16 + d) % 4 * 16 + i % 16) for i in ran...]
    ppermute x4, starting transfers between devices: 8.26 us -> 11.2 us  [lines_on(): return lax.ppermute(x, 'seq', [(i, (i + 4 * d) % 64) for i in range(64)])]
    pallas_call x3 -> x2, Pallas kernels: 4.68 us -> 1.98 us  [call(): pl.pallas_call(kernel, grid_spec=pltpu.PrefetchScalarGridSpec(num_scalar_...]
    ppermute x24, waiting for transfers between devices: 18 us -> 20 us  [ring_y(): lax.ppermute(x, 'seq', [(i, i // 4 * 4 + (i + d) % 4) for i in range(64)])]
    ppermute x1, starting transfers between devices: 4.22 us -> 2.3 us  [far_two(): return lax.ppermute(x, 'seq', route)]
    ppermute x24, starting transfers between devices: 39.6 us -> 37.9 us  [ring_y(): lax.ppermute(x, 'seq', [(i, i // 4 * 4 + (i + d) % 4) for i in range(64)])]
  transfers between devices with their start and end apart: 44 -> 41, of which waited for: 18 -> 20; matrix products, arithmetic and copies ran while one was open for 1% -> 1% of each run, Pallas kernels for 12% -> 13%
where the time goes in v2:
time: 151 us
  starting transfers between devices  69.1 us (46%)
  waiting for transfers between devices  35.2 us (23%)
  Pallas kernels  33.7 us (22%)
  local copies, waits for them, and re-layouts  10.7 us (7%)
    ppermute x24, starting transfers between devices, ring_y(): lax.ppermute(x, 'seq', [(i, i // 4 * 4 + (i + d) % 4) for i in range(64)])  37.9 us
    pallas_call x14, Pallas kernels, flat_call(): pl.pallas_call(kernel, in_specs=list(specs_in), out_specs=[pl.BlockSpec(m...  31.7 us
    ppermute x24, waiting for transfers between devices, ring_y(): lax.ppermute(x, 'seq', [(i, i // 4 * 4 + (i + d) % 4) for i in range(64)])  20 us
    ppermute x4, starting transfers between devices, lines_on(): return lax.ppermute(x, 'seq', [(i, (i + 4 * d) % 64) for i in range(64)])  11.2 us
    unnamed x46, local copies, waits for them, and re-layouts  10.4 us
    ppermute x3, waiting for transfers between devices, ring_x(): lax.ppermute(x, 'seq', [(i, (i // 16 + d) % 4 * 16 + i % 16) for i in ran...  7.72 us
    ppermute x3, starting transfers between devices, ring_z(): lax.ppermute(x, 'seq', [(i, i // 16 * 16 + (i // 4 + d) % 4 * 4 + i % 4)...  7.03 us
    ppermute x3, starting transfers between devices, ring_x(): lax.ppermute(x, 'seq', [(i, (i // 16 + d) % 4 * 16 + i % 16) for i in ran...  6.39 us
  transfers between devices with their start and end apart: 41, of which 20 were waited for; matrix products, arithmetic and copies ran while one was open for 1% of the time, Pallas kernels for 13%

profile of v2, /device:TPU:0, one launch (start us, length us, event | category | flops | bytes accessed | tf_op | source)
XLA Modules:
  0.0 150.7 jit_solution(14643387983697820899)
XLA Ops:
  0.6 5.2 %shard_map.77 = (bf16[4,128,128]{2,1,0:T(8,128)(2,1)}, bf16[4,128,128]{2,1,0:T(8,128)(2,1)}, bf16[4,128,128]{2,1,0:T(8,128)(2,1)}, bf16[4,128,128]{2,1,0:T(8,128)(2,1)}) custom-call(bf16[128,2688]{1,0:T(8,128)(2,1)} %tok.3, bf16[128,2688]{1,0:T(8,128)(2,1)} %tan.3, bf16[2688,512]{1,0:T(8,128)(2,1)} %wk.3, bf16[2688,512]{1,0:T(8,128)(2,1)} %wv.3), custom_call_target="tpu_custom_call" | custom-call | flops 1409286144 | bytes 5505024 | tf_op jit(solution)/shard_map/pallas_call | solution.py:94
  7.6 2.9 %collective-permute-start.1 = (bf16[4,128,128]{2,1,0:T(8,128)(2,1)}, bf16[4,128,128]{2,1,0:T(8,128)(2,1)S(1)}, u32[]{:S(2)}, u32[]{:S(2)}) collective-permute-start(bf16[4,128,128]{2,1,0:T(8,128)(2,1)} %get-tuple-element.53), channel_id=1, source_target_pairs={{0,4},{2,6},{4,0},{6,2},{8,12},{10,14},{12,8},{14,10},{16,20},{18,... | collective-permute-start | bytes 393224 | tf_op jit(solution)/shard_map/ppermute | solution.py:28
  12.8 4.0 %collective-permute-done.1.c = bf16[4,128,128]{2,1,0:T(8,128)(2,1)S(1)} collective-permute-done((bf16[4,128,128]{2,1,0:T(8,128)(2,1)}, bf16[4,128,128]{2,1,0:T(8,128)(2,1)S(1)}, u32[]{:S(2)}, u32[]{:S(2)}) %collective-permute-start.1) | collective-permute-done | bytes 131104 | tf_op jit(solution)/shard_map/ppermute | solution.py:28
  18.4 4.1 %collective-permute-start.4 = (bf16[256,512]{1,0:T(8,128)(2,1)S(1)}, bf16[256,512]{1,0:T(8,128)(2,1)S(1)}, u32[]{:S(2)}, u32[]{:S(2)}) collective-permute-start(bf16[256,512]{1,0:T(8,128)(2,1)S(1)} %get-tuple-element.56), channel_id=1, source_target_pairs={{0,24},{2,26},{4,28},{6,30},{8,0},{10,2},{12,4},{14,6},{16,8},{18,... | collective-permute-start | bytes 786440 | tf_op jit(solution)/shard_map/ppermute | solution.py:51
  22.5 2.6 %copy-done.2 = bf16[2688,1024]{1,0:T(8,128)(2,1)S(1)} copy-done((bf16[2688,1024]{1,0:T(8,128)(2,1)S(1)}, bf16[2688,1024]{1,0:T(8,128)(2,1)}, u32[]{:S(2)}) %copy-start.2) | copy-done | bytes 5505048
  36.7 2.5 %collective-permute-done.8.q2 = bf16[2,128,256]{2,1,0:T(8,128)(2,1)S(1)} collective-permute-done((bf16[2,128,256]{2,1,0:T(8,128)(2,1)S(1)}, bf16[2,128,256]{2,1,0:T(8,128)(2,1)S(1)}, u32[]{:S(2)}, u32[]{:S(2)}) %collective-permute-start.8) | collective-permute-done | bytes 131104 | tf_op jit(solution)/shard_map/ppermute | solution.py:28
  40.1 3.8 %collective-permute-done.3.low = bf16[256,512]{1,0:T(8,128)(2,1)S(1)} collective-permute-done((bf16[256,512]{1,0:T(8,128)(2,1)S(1)}, bf16[256,512]{1,0:T(8,128)(2,1)S(1)}, u32[]{:S(2)}, u32[]{:S(2)}) %collective-permute-start.3) | collective-permute-done | bytes 262176 | tf_op jit(solution)/shard_map/ppermute | solution.py:42
  44.0 5.3 %shard_map.80 = (bf16[128,256]{1,0:T(8,128)(2,1)S(1)}, bf16[128,256]{1,0:T(8,128)(2,1)S(1)}, bf16[128,256]{1,0:T(8,128)(2,1)S(1)}, bf16[128,256]{1,0:T(8,128)(2,...) custom-call(s32[4]{0:T(128)S(1)} %pad_add_fusion.pos, ...), custom_call_target="tpu_custom_call" | custom-call | flops 1509949440 | bytes 8388608 | tf_op jit(solution)/shard_map/pallas_call | solution.py:94
  52.2 2.5 %collective-permute-start.11 = (bf16[128,256]{1,0:T(8,128)(2,1)S(1)}, bf16[128,256]{1,0:T(8,128)(2,1)S(1)}, u32[]{:S(2)}, u32[]{:S(2)}) collective-permute-start(bf16[128,256]{1,0:T(8,128)(2,1)S(1)} %get-tuple-element.64), channel_id=1, source_target_pairs={{0,4},{2,6},{4,0},{6,2},{8,12},{10,14},{12,8},{14,10},{16,20},{18,... | collective-permute-start | bytes 196616 | tf_op jit(solution)/shard_map/ppermute | solution.py:28
  62.6 3.2 %collective-permute-start.27 = (bf16[1344,128]{1,0:T(8,128)(2,1)S(1)}, bf16[1344,128]{1,0:T(8,128)(2,1)S(1)}, u32[]{:S(2)}, u32[]{:S(2)}) collective-permute-start(bf16[1344,128]{1,0:T(8,128)(2,1)S(1)} %dynamic-slice_bitcast_fusion), channel_id=1, source_target_pairs={{0,4},{2,6},{4,0},{6,2},{8,12},{10,14},{12,8},{14,10},{16,20},{18,... | collective-permute-start | bytes 1032200 | tf_op jit(solution)/shard_map/ppermute | solution.py:28
  66.2 2.6 %copy-done.1 = bf16[1024,2688]{1,0:T(8,128)(2,1)S(1)} copy-done((bf16[1024,2688]{1,0:T(8,128)(2,1)S(1)}, bf16[1024,2688]{1,0:T(8,128)(2,1)}, u32[]{:S(2)}) %copy-start.1) | copy-done | bytes 5505048
  70.1 2.5 %shard_map.83 = (bf16[128,256]{1,0:T(8,128)(2,1)S(1)}, bf16[128,256]{1,0:T(8,128)(2,1)S(1)}, bf16[128,256]{1,0:T(8,128)(2,1)S(1)}, bf16[128,256]{1,0:T(8,128)(2,1)S(1)}) custom-call(s32[4]{0:T(128)S(1)} %pad_add_fusion.pos, f32[128,2688]{1,0:T(8,128)S(1)} %copy-done.9, bf16[128,2688]{1,0:T(8,128)(2,1)S(1)} %collective-permute-done.13.other, ...), custom_call_target="tpu_custom_call" | custom-call | flops 704643072 | bytes 5505024 | tf_op jit(solution)/shard_map/pallas_call | solution.py:94
  74.8 2.5 %collective-permute-start.16 = (bf16[128,256]{1,0:T(8,128)(2,1)S(1)}, bf16[128,256]{1,0:T(8,128)(2,1)S(1)}, u32[]{:S(2)}, u32[]{:S(2)}) collective-permute-start(bf16[128,256]{1,0:T(8,128)(2,1)S(1)} %get-tuple-element.71), channel_id=1, source_target_pairs={{0,6},{2,0},{4,2},{6,4},{8,14},{10,8},{12,10},{14,12},{16,22},{18,... | collective-permute-start | bytes 196616 | tf_op jit(solution)/shard_map/ppermute | solution.py:28
  77.3 4.7 %collective-permute-done.27.r2 = bf16[1344,128]{1,0:T(8,128)(2,1)S(1)} collective-permute-done((bf16[1344,128]{1,0:T(8,128)(2,1)S(1)}, bf16[1344,128]{1,0:T(8,128)(2,1)S(1)}, u32[]{:S(2)}, u32[]{:S(2)}) %collective-permute-start.27) | collective-permute-done | bytes 344096 | tf_op jit(solution)/shard_map/ppermute | solution.py:28
  84.6 5.0 %shard_map.84 = (bf16[128,256]{1,0:T(8,128)(2,1)S(1)}, bf16[128,256]{1,0:T(8,128)(2,1)S(1)}, bf16[128,256]{1,0:T(8,128)(2,1)S(1)}, bf16[128,256]{1,0:T(8,128)(2,...) custom-call(s32[4]{0:T(128)S(1)} %pad_add_fusion.pos, ...), custom_call_target="tpu_custom_call" | custom-call | flops 1207959552 | bytes 6291456 | tf_op jit(solution)/shard_map/pallas_call | solution.py:94
  89.6 3.9 %collective-permute-start.17 = (bf16[512,256]{1,0:T(8,128)(2,1)S(1)}, bf16[512,256]{1,0:T(8,128)(2,1)S(1)}, u32[]{:S(2)}, u32[]{:S(2)}) collective-permute-start(bf16[512,256]{1,0:T(8,128)(2,1)S(1)} %get-tuple-element.75), channel_id=1, source_target_pairs={{0,120},{2,122},{4,124},{6,126},{8,0},{10,2},{12,4},{14,6},{16,8},... | collective-permute-start | bytes 786440 | tf_op jit(solution)/shard_map/ppermute | solution.py:42
  93.5 5.4 %collective-permute-start.18 = (bf16[512,256]{1,0:T(8,128)(2,1)S(1)}, bf16[512,256]{1,0:T(8,128)(2,1)S(1)}, u32[]{:S(2)}, u32[]{:S(2)}) collective-permute-start(bf16[512,256]{1,0:T(8,128)(2,1)S(1)} %get-tuple-element.76), channel_id=1, source_target_pairs={{0,112},{2,114},{4,116},{6,118},{8,120},{10,122},{12,124},{14,126}... | collective-permute-start | bytes 786440 | tf_op jit(solution)/shard_map/ppermute | solution.py:42
  100.9 3.2 %collective-permute-start.23 = (bf16[128,256]{1,0:T(8,128)(2,1)S(1)}, bf16[128,256]{1,0:T(8,128)(2,1)S(1)}, u32[]{:S(2)}, u32[]{:S(2)}) collective-permute-start(bf16[128,256]{1,0:T(8,128)(2,1)S(1)} %get-tuple-element.83), channel_id=1, source_target_pairs={{0,4},{2,6},{4,0},{6,2},{8,12},{10,14},{12,8},{14,10},{16,20},{18,... | collective-permute-start | bytes 196616 | tf_op jit(solution)/shard_map/ppermute | solution.py:28
  108.2 3.2 %collective-permute-start.20 = (bf16[128,256]{1,0:T(8,128)(2,1)S(1)}, bf16[128,256]{1,0:T(8,128)(2,1)S(1)}, u32[]{:S(2)}, u32[]{:S(2)}) collective-permute-start(bf16[128,256]{1,0:T(8,128)(2,1)S(1)} %get-tuple-element.79.c2), channel_id=1, source_target_pairs={{0,4},{2,6},{4,0},{6,2},{8,12},{10,14},{12,8},{14,10},{16,20},{18,... | collective-permute-start | bytes 196616 | tf_op jit(solution)/shard_map/ppermute | solution.py:28
  115.1 2.7 %collective-permute-start.33 = (bf16[672,256]{1,0:T(8,128)(2,1)S(1)}, bf16[672,256]{1,0:T(8,128)(2,1)S(1)}, u32[]{:S(2)}, u32[]{:S(2)}) collective-permute-start(bf16[672,256]{1,0:T(8,128)(2,1)S(1)} %get-tuple-element.90), channel_id=1, source_target_pairs={{0,64},{2,66},{4,68},{6,70},{8,72},{10,74},{12,76},{14,78},{16,80}... | collective-permute-start | bytes 1032200 | tf_op jit(solution)/shard_map/ppermute | solution.py:38
  124.3 7.6 %collective-permute-done.33.refs_2_ = bf16[672,256]{1,0:T(8,128)(2,1)S(1)} collective-permute-done((bf16[672,256]{1,0:T(8,128)(2,1)S(1)}, bf16[672,256]{1,0:T(8,128)(2,1)S(1)}, u32[]{:S(2)}, u32[]{:S(2)}) %collective-permute-start.33) | collective-permute-done | bytes 344096 | tf_op jit(solution)/shard_map/ppermute | solution.py:38
  134.1 3.2 %collective-permute-start.36 = (bf16[168,256]{1,0:T(8,128)(2,1)S(1)}, bf16[168,256]{1,0:T(8,128)(2,1)S(1)}, u32[]{:S(2)}, u32[]{:S(2)}) collective-permute-start(bf16[168,256]{1,0:T(8,128)(2,1)S(1)} %get-tuple-element.94), channel_id=1, source_target_pairs={{0,16},{2,18},{4,20},{6,22},{8,24},{10,26},{12,28},{14,30},{16,0},... | collective-permute-start | bytes 258056 | tf_op jit(solution)/shard_map/ppermute | solution.py:32
  137.3 2.5 %collective-permute-start.37 = (bf16[168,256]{1,0:T(8,128)(2,1)S(1)}, bf16[168,256]{1,0:T(8,128)(2,1)S(1)}, u32[]{:S(2)}, u32[]{:S(2)}) collective-permute-start(bf16[168,256]{1,0:T(8,128)(2,1)S(1)} %get-tuple-element.95), channel_id=1, source_target_pairs={{0,24},{2,26},{4,28},{6,30},{8,0},{10,2},{12,4},{14,6},{16,8},{18,... | collective-permute-start | bytes 258056 | tf_op jit(solution)/shard_map/ppermute | solution.py:32
  142.7 2.4 %collective-permute-start.39 = (f32[42,256]{1,0:T(8,128)S(1)}, f32[42,256]{1,0:T(8,128)S(1)}, u32[]{:S(2)}, u32[]{:S(2)}) collective-permute-start(f32[42,256]{1,0:T(8,128)S(1)} %get-tuple-element.98), channel_id=1, source_target_pairs={{0,4},{2,6},{4,0},{6,2},{8,12},{10,14},{12,8},{14,10},{16,20},{18,... | collective-permute-start | bytes 129032 | tf_op jit(solution)/shard_map/ppermute | solution.py:28
  (125 shorter events, 62.1 us)
Async XLA Ops:
  18.4 12.1 %collective-permute-start.4 = (bf16[256,512]{1,0:T(8,128)(2,1)S(1)}, bf16[256,512]{1,0:T(8,128)(2,1)S(1)}, u32[]{:S(2)}, u32[]{:S(2)}) collective-permute-start(bf16[256,512]{1,0:T(8,128)(2,1)S(1)} %get-tuple-element.56), channel_id=1, source_target_pairs={{0,24},{2,26},{4,28},{6,30},{8,0},{10,2},{12,4},{14,6},{16,8},{18,... | collective-permute-start | bytes 786440 | tf_op jit(solution)/shard_map/ppermute | solution.py:51
  22.5 21.5 %collective-permute-start.6 = (bf16[512,512]{1,0:T(8,128)(2,1)S(1)}, bf16[512,512]{1,0:T(8,128)(2,1)S(1)}, u32[]{:S(2)}, u32[]{:S(2)}) collective-permute-start(bf16[512,512]{1,0:T(8,128)(2,1)S(1)} %get-tuple-element.57.own.own_kv), channel_id=1, source_target_pairs={{0,8},{2,10},{4,12},{6,14},{8,16},{10,18},{12,20},{14,22},{16,24},... | collective-permute-start | bytes 1572872 | tf_op jit(solution)/shard_map/ppermute | solution.py:42
  28.6 15.3 %collective-permute-start.3 = (bf16[256,512]{1,0:T(8,128)(2,1)S(1)}, bf16[256,512]{1,0:T(8,128)(2,1)S(1)}, u32[]{:S(2)}, u32[]{:S(2)}) collective-permute-start(bf16[256,512]{1,0:T(8,128)(2,1)S(1)} %get-tuple-element.55), channel_id=1, source_target_pairs={{0,16},{2,18},{4,20},{6,22},{8,24},{10,26},{12,28},{14,30},{16,32}... | collective-permute-start | bytes 786440 | tf_op jit(solution)/shard_map/ppermute | solution.py:42
  30.5 13.5 %collective-permute-start.5 = (bf16[256,512]{1,0:T(8,128)(2,1)S(1)}, bf16[256,512]{1,0:T(8,128)(2,1)S(1)}, u32[]{:S(2)}, u32[]{:S(2)}) collective-permute-start(bf16[256,512]{1,0:T(8,128)(2,1)S(1)} %collective-permute-done.4), channel_id=1, source_target_pairs={{0,24},{2,26},{4,28},{6,30},{8,32},{10,34},{12,36},{14,38},{16,40}... | collective-permute-start | bytes 786440 | tf_op jit(solution)/shard_map/ppermute | solution.py:61
  62.0 12.8 %collective-permute-start.26 = (bf16[1344,128]{1,0:T(8,128)(2,1)S(1)}, bf16[1344,128]{1,0:T(8,128)(2,1)S(1)}, u32[]{:S(2)}, u32[]{:S(2)}) collective-permute-start(bf16[1344,128]{1,0:T(8,128)(2,1)S(1)} %dynamic-slice_bitcast_fusion), channel_id=1, source_target_pairs={{0,2},{2,4},{4,6},{6,0},{8,10},{10,12},{12,14},{14,8},{16,18},{18,... | collective-permute-start | bytes 1032200 | tf_op jit(solution)/shard_map/ppermute | solution.py:28
  62.6 19.5 %collective-permute-start.27 = (bf16[1344,128]{1,0:T(8,128)(2,1)S(1)}, bf16[1344,128]{1,0:T(8,128)(2,1)S(1)}, u32[]{:S(2)}, u32[]{:S(2)}) collective-permute-start(bf16[1344,128]{1,0:T(8,128)(2,1)S(1)} %dynamic-slice_bitcast_fusion), channel_id=1, source_target_pairs={{0,4},{2,6},{4,0},{6,2},{8,12},{10,14},{12,8},{14,10},{16,20},{18,... | collective-permute-start | bytes 1032200 | tf_op jit(solution)/shard_map/ppermute | solution.py:28
  65.7 16.7 %collective-permute-start.28 = (bf16[1344,128]{1,0:T(8,128)(2,1)S(1)}, bf16[1344,128]{1,0:T(8,128)(2,1)S(1)}, u32[]{:S(2)}, u32[]{:S(2)}) collective-permute-start(bf16[1344,128]{1,0:T(8,128)(2,1)S(1)} %dynamic-slice_bitcast_fusion), channel_id=1, source_target_pairs={{0,6},{2,0},{4,2},{6,4},{8,14},{10,8},{12,10},{14,12},{16,22},{18,... | collective-permute-start | bytes 1032200 | tf_op jit(solution)/shard_map/ppermute | solution.py:28
  72.6 10.8 %collective-permute-start.14 = (bf16[128,256]{1,0:T(8,128)(2,1)S(1)}, bf16[128,256]{1,0:T(8,128)(2,1)S(1)}, u32[]{:S(2)}, u32[]{:S(2)}) collective-permute-start(bf16[128,256]{1,0:T(8,128)(2,1)S(1)} %get-tuple-element.69), channel_id=1, source_target_pairs={{0,2},{2,4},{4,6},{6,0},{8,10},{10,12},{12,14},{14,8},{16,18},{18,... | collective-permute-start | bytes 196616 | tf_op jit(solution)/shard_map/ppermute | solution.py:28
  74.2 10.2 %collective-permute-start.15 = (bf16[128,256]{1,0:T(8,128)(2,1)S(1)}, bf16[128,256]{1,0:T(8,128)(2,1)S(1)}, u32[]{:S(2)}, u32[]{:S(2)}) collective-permute-start(bf16[128,256]{1,0:T(8,128)(2,1)S(1)} %get-tuple-element.70), channel_id=1, source_target_pairs={{0,4},{2,6},{4,0},{6,2},{8,12},{10,14},{12,8},{14,10},{16,20},{18,... | collective-permute-start | bytes 196616 | tf_op jit(solution)/shard_map/ppermute | solution.py:28
  74.8 9.7 %collective-permute-start.16 = (bf16[128,256]{1,0:T(8,128)(2,1)S(1)}, bf16[128,256]{1,0:T(8,128)(2,1)S(1)}, u32[]{:S(2)}, u32[]{:S(2)}) collective-permute-start(bf16[128,256]{1,0:T(8,128)(2,1)S(1)} %get-tuple-element.71), channel_id=1, source_target_pairs={{0,6},{2,0},{4,2},{6,4},{8,14},{10,8},{12,10},{14,12},{16,22},{18,... | collective-permute-start | bytes 196616 | tf_op jit(solution)/shard_map/ppermute | solution.py:28
  82.1 16.8 %collective-permute-start.29 = (bf16[1344,128]{1,0:T(8,128)(2,1)S(1)}, bf16[1344,128]{1,0:T(8,128)(2,1)S(1)}, u32[]{:S(2)}, u32[]{:S(2)}) collective-permute-start(bf16[1344,128]{1,0:T(8,128)(2,1)S(1)} %collective-permute-done.26.r1), channel_id=1, source_target_pairs={{0,1},{1,0},{2,3},{3,2},{4,5},{5,4},{6,7},{7,6},{8,9},{9,8},{10,11... | collective-permute-start | bytes 1032200 | tf_op jit(solution)/shard_map/ppermute | solution.py:65
  82.4 16.4 %collective-permute-start.30 = (bf16[1344,128]{1,0:T(8,128)(2,1)S(1)}, bf16[1344,128]{1,0:T(8,128)(2,1)S(1)}, u32[]{:S(2)}, u32[]{:S(2)}) collective-permute-start(bf16[1344,128]{1,0:T(8,128)(2,1)S(1)} %collective-permute-done.27.r2), channel_id=1, source_target_pairs={{0,1},{1,0},{2,3},{3,2},{4,5},{5,4},{6,7},{7,6},{8,9},{9,8},{10,11... | collective-permute-start | bytes 1032200 | tf_op jit(solution)/shard_map/ppermute | solution.py:65
  83.4 15.5 %collective-permute-start.31 = (bf16[1344,128]{1,0:T(8,128)(2,1)S(1)}, bf16[1344,128]{1,0:T(8,128)(2,1)S(1)}, u32[]{:S(2)}, u32[]{:S(2)}) collective-permute-start(bf16[1344,128]{1,0:T(8,128)(2,1)S(1)} %collective-permute-done.28.r3), channel_id=1, source_target_pairs={{0,1},{1,0},{2,3},{3,2},{4,5},{5,4},{6,7},{7,6},{8,9},{9,8},{10,11... | collective-permute-start | bytes 1032200 | tf_op jit(solution)/shard_map/ppermute | solution.py:65
  89.6 16.2 %collective-permute-start.17 = (bf16[512,256]{1,0:T(8,128)(2,1)S(1)}, bf16[512,256]{1,0:T(8,128)(2,1)S(1)}, u32[]{:S(2)}, u32[]{:S(2)}) collective-permute-start(bf16[512,256]{1,0:T(8,128)(2,1)S(1)} %get-tuple-element.75), channel_id=1, source_target_pairs={{0,120},{2,122},{4,124},{6,126},{8,0},{10,2},{12,4},{14,6},{16,8},... | collective-permute-start | bytes 786440 | tf_op jit(solution)/shard_map/ppermute | solution.py:42
  93.5 12.4 %collective-permute-start.18 = (bf16[512,256]{1,0:T(8,128)(2,1)S(1)}, bf16[512,256]{1,0:T(8,128)(2,1)S(1)}, u32[]{:S(2)}, u32[]{:S(2)}) collective-permute-start(bf16[512,256]{1,0:T(8,128)(2,1)S(1)} %get-tuple-element.76), channel_id=1, source_target_pairs={{0,112},{2,114},{4,116},{6,118},{8,120},{10,122},{12,124},{14,126}... | collective-permute-start | bytes 786440 | tf_op jit(solution)/shard_map/ppermute | solution.py:42
  100.0 12.8 %collective-permute-start.22 = (bf16[128,256]{1,0:T(8,128)(2,1)S(1)}, bf16[128,256]{1,0:T(8,128)(2,1)S(1)}, u32[]{:S(2)}, u32[]{:S(2)}) collective-permute-start(bf16[128,256]{1,0:T(8,128)(2,1)S(1)} %get-tuple-element.82), channel_id=1, source_target_pairs={{0,2},{2,4},{4,6},{6,0},{8,10},{10,12},{12,14},{14,8},{16,18},{18,... | collective-permute-start | bytes 196616 | tf_op jit(solution)/shard_map/ppermute | solution.py:28
  100.9 11.9 %collective-permute-start.23 = (bf16[128,256]{1,0:T(8,128)(2,1)S(1)}, bf16[128,256]{1,0:T(8,128)(2,1)S(1)}, u32[]{:S(2)}, u32[]{:S(2)}) collective-permute-start(bf16[128,256]{1,0:T(8,128)(2,1)S(1)} %get-tuple-element.83), channel_id=1, source_target_pairs={{0,4},{2,6},{4,0},{6,2},{8,12},{10,14},{12,8},{14,10},{16,20},{18,... | collective-permute-start | bytes 196616 | tf_op jit(solution)/shard_map/ppermute | solution.py:28
  104.2 10.9 %collective-permute-start.24 = (bf16[128,256]{1,0:T(8,128)(2,1)S(1)}, bf16[128,256]{1,0:T(8,128)(2,1)S(1)}, u32[]{:S(2)}, u32[]{:S(2)}) collective-permute-start(bf16[128,256]{1,0:T(8,128)(2,1)S(1)} %get-tuple-element.84), channel_id=1, source_target_pairs={{0,6},{2,0},{4,2},{6,4},{8,14},{10,8},{12,10},{14,12},{16,22},{18,... | collective-permute-start | bytes 196616 | tf_op jit(solution)/shard_map/ppermute | solution.py:28
  106.5 11.3 %collective-permute-start.19 = (bf16[128,256]{1,0:T(8,128)(2,1)S(1)}, bf16[128,256]{1,0:T(8,128)(2,1)S(1)}, u32[]{:S(2)}, u32[]{:S(2)}) collective-permute-start(bf16[128,256]{1,0:T(8,128)(2,1)S(1)} %get-tuple-element.78.c1), channel_id=1, source_target_pairs={{0,2},{2,4},{4,6},{6,0},{8,10},{10,12},{12,14},{14,8},{16,18},{18,... | collective-permute-start | bytes 196616 | tf_op jit(solution)/shard_map/ppermute | solution.py:28
  108.2 13.3 %collective-permute-start.20 = (bf16[128,256]{1,0:T(8,128)(2,1)S(1)}, bf16[128,256]{1,0:T(8,128)(2,1)S(1)}, u32[]{:S(2)}, u32[]{:S(2)}) collective-permute-start(bf16[128,256]{1,0:T(8,128)(2,1)S(1)} %get-tuple-element.79.c2), channel_id=1, source_target_pairs={{0,4},{2,6},{4,0},{6,2},{8,12},{10,14},{12,8},{14,10},{16,20},{18,... | collective-permute-start | bytes 196616 | tf_op jit(solution)/shard_map/ppermute | solution.py:28
  112.9 11.5 %collective-permute-start.32 = (bf16[672,256]{1,0:T(8,128)(2,1)S(1)}, bf16[672,256]{1,0:T(8,128)(2,1)S(1)}, u32[]{:S(2)}, u32[]{:S(2)}) collective-permute-start(bf16[672,256]{1,0:T(8,128)(2,1)S(1)} %get-tuple-element.89), channel_id=1, source_target_pairs={{0,32},{2,34},{4,36},{6,38},{8,40},{10,42},{12,44},{14,46},{16,48}... | collective-permute-start | bytes 1032200 | tf_op jit(solution)/shard_map/ppermute | solution.py:38
  115.1 16.9 %collective-permute-start.33 = (bf16[672,256]{1,0:T(8,128)(2,1)S(1)}, bf16[672,256]{1,0:T(8,128)(2,1)S(1)}, u32[]{:S(2)}, u32[]{:S(2)}) collective-permute-start(bf16[672,256]{1,0:T(8,128)(2,1)S(1)} %get-tuple-element.90), channel_id=1, source_target_pairs={{0,64},{2,66},{4,68},{6,70},{8,72},{10,74},{12,76},{14,78},{16,80}... | collective-permute-start | bytes 1032200 | tf_op jit(solution)/shard_map/ppermute | solution.py:38
  117.8 14.2 %collective-permute-start.34 = (bf16[672,256]{1,0:T(8,128)(2,1)S(1)}, bf16[672,256]{1,0:T(8,128)(2,1)S(1)}, u32[]{:S(2)}, u32[]{:S(2)}) collective-permute-start(bf16[672,256]{1,0:T(8,128)(2,1)S(1)} %get-tuple-element.91), channel_id=1, source_target_pairs={{0,96},{2,98},{4,100},{6,102},{8,104},{10,106},{12,108},{14,110},{... | collective-permute-start | bytes 1032200 | tf_op jit(solution)/shard_map/ppermute | solution.py:38
  124.2 22.0 %collective-permute-start.25 = (bf16[1344,128]{1,0:T(8,128)(2,1)S(1)}, bf16[1344,128]{1,0:T(8,128)(2,1)S(1)}, u32[]{:S(2)}, u32[]{:S(2)}) collective-permute-start(bf16[1344,128]{1,0:T(8,128)(2,1)S(1)} %get-tuple-element.86), channel_id=1, source_target_pairs={{0,1},{1,0},{2,3},{3,2},{4,5},{5,4},{6,7},{7,6},{8,9},{9,8},{10,11... | collective-permute-start | bytes 1032200 | tf_op jit(solution)/shard_map/ppermute | solution.py:65
  (40 other events, 328.1 us)

commit v3 on v2

--- a/solution.py
+++ b/solution.py
@@ -187,8 +187,8 @@
         rows = pl.ds(pl.multiple_of(block * HEAD, HEAD), HEAD)
         for part in range(4):
             line[rows, part * HEAD : (part + 1) * HEAD] = ref[part]
-    low[...] = line[:256]
-    high[...] = line[256:]
+    low[...] = line[: low.shape[0]]
+    high[...] = line[low.shape[0] :]
 
 
 def load_kernel(pos, src, dst, sem):
@@ -204,11 +204,12 @@
 def window_of(refs, b, cols):
     low, high, near, own = refs
     parts = []
-    if b < 2:
+    cut = low.shape[0] // HEAD
+    if b < cut:
         parts.append(low[b * HEAD :, cols])
         parts.append(high[:, cols])
     else:
-        parts.append(high[(b - 2) * HEAD :, cols])
+        parts.append(high[(b - cut) * HEAD :, cols])
     parts += [near[:, cols], own[: (b + 1) * HEAD, cols]]
     return jnp.concatenate(parts, axis=0)
 
@@ -426,7 +427,7 @@
     line, low, high = flat_call(
         join_kernel,
         [pos] + [(vmem(), c) for c in exchange(ring_y, kv)],
-        [out((512, 512), BF), out((256, 512), BF), out((256, 512), BF)],
+        [out((512, 512), BF), out((128, 512), BF), out((384, 512), BF)],
         moved=1 << 20,
     )
     passed = far_one(high)

time: 151 us -> 157 us (1.040)
  waiting for transfers between devices: 35.2 us -> 50.2 us
  starting transfers between devices: 69.1 us -> 60.3 us
    ppermute x4, starting transfers between devices: 11.2 us -> 1.39 us  [lines_on(): return lax.ppermute(x, 'seq', [(i, (i + 4 * d) % 64) for i in range(64)])]
    ppermute x4, waiting for transfers between devices: 5.46 us -> 13.4 us  [lines_on(): return lax.ppermute(x, 'seq', [(i, (i + 4 * d) % 64) for i in range(64)])]
    ppermute x1, waiting for transfers between devices: 0.01 us -> 7.51 us  [far_one(): lax.ppermute(x, 'seq', [(i, i // 16 * 16 + (i // 4 + 3) % 4 * 4 + i % 4)...]
    unnamed x46 -> x42, local copies, waits for them, and re-layouts: 10.4 us -> 10.4 us
where the time goes in v3:
time: 157 us
  starting transfers between devices  60.3 us (38%)
  waiting for transfers between devices  50.2 us (32%)
  Pallas kernels  33.7 us (21%)
  local copies, waits for them, and re-layouts  10.8 us (7%)
    ppermute x24, starting transfers between devices, ring_y(): lax.ppermute(x, 'seq', [(i, i // 4 * 4 + (i + d) % 4) for i in range(64)])  37.3 us
    pallas_call x14, Pallas kernels, flat_call(): pl.pallas_call(kernel, in_specs=list(specs_in), out_specs=[pl.BlockSpec(m...  31.7 us
    ppermute x24, waiting for transfers between devices, ring_y(): lax.ppermute(x, 'seq', [(i, i // 4 * 4 + (i + d) % 4) for i in range(64)])  19.3 us
    ppermute x4, waiting for transfers between devices, lines_on(): return lax.ppermute(x, 'seq', [(i, (i + 4 * d) % 64) for i in range(64)])  13.4 us
    unnamed x42, local copies, waits for them, and re-layouts  10.4 us
    ppermute x3, waiting for transfers between devices, ring_x(): lax.ppermute(x, 'seq', [(i, (i // 16 + d) % 4 * 16 + i % 16) for i in ran...  7.81 us
    ppermute x1, waiting for transfers between devices, far_one(): lax.ppermute(x, 'seq', [(i, i // 16 * 16 + (i // 4 + 3) % 4 * 4 + i % 4)...  7.51 us
    ppermute x3, starting transfers between devices, ring_z(): lax.ppermute(x, 'seq', [(i, i // 16 * 16 + (i // 4 + d) % 4 * 4 + i % 4)...  7.27 us
  transfers between devices with their start and end apart: 41, of which 20 were waited for; matrix products, arithmetic and copies ran while one was open for 1% of the time, Pallas kernels for 13%

profile of v3, /device:TPU:0, one launch (start us, length us, event | category | flops | bytes accessed | tf_op | source)
XLA Modules:
  0.0 156.8 jit_solution(12860673503807913848)
XLA Ops:
  0.6 5.2 %shard_map.77 = (bf16[4,128,128]{2,1,0:T(8,128)(2,1)}, bf16[4,128,128]{2,1,0:T(8,128)(2,1)}, bf16[4,128,128]{2,1,0:T(8,128)(2,1)}, bf16[4,128,128]{2,1,0:T(8,128)(2,1)}) custom-call(bf16[128,2688]{1,0:T(8,128)(2,1)} %tok.3, bf16[128,2688]{1,0:T(8,128)(2,1)} %tan.3, bf16[2688,512]{1,0:T(8,128)(2,1)} %wk.3, bf16[2688,512]{1,0:T(8,128)(2,1)} %wv.3), custom_call_target="tpu_custom_call" | custom-call | flops 1409286144 | bytes 5505024 | tf_op jit(solution)/shard_map/pallas_call | solution.py:94
  7.6 2.9 %collective-permute-start.1 = (bf16[4,128,128]{2,1,0:T(8,128)(2,1)}, bf16[4,128,128]{2,1,0:T(8,128)(2,1)S(1)}, u32[]{:S(2)}, u32[]{:S(2)}) collective-permute-start(bf16[4,128,128]{2,1,0:T(8,128)(2,1)} %get-tuple-element.53), channel_id=1, source_target_pairs={{0,4},{2,6},{4,0},{6,2},{8,12},{10,14},{12,8},{14,10},{16,20},{18,... | collective-permute-start | bytes 393224 | tf_op jit(solution)/shard_map/ppermute | solution.py:28
  12.8 4.0 %collective-permute-done.1.c = bf16[4,128,128]{2,1,0:T(8,128)(2,1)S(1)} collective-permute-done((bf16[4,128,128]{2,1,0:T(8,128)(2,1)}, bf16[4,128,128]{2,1,0:T(8,128)(2,1)S(1)}, u32[]{:S(2)}, u32[]{:S(2)}) %collective-permute-start.1) | collective-permute-done | bytes 131104 | tf_op jit(solution)/shard_map/ppermute | solution.py:28
  18.4 4.1 %collective-permute-start.4 = (bf16[384,512]{1,0:T(8,128)(2,1)S(1)}, bf16[384,512]{1,0:T(8,128)(2,1)S(1)}, u32[]{:S(2)}, u32[]{:S(2)}) collective-permute-start(bf16[384,512]{1,0:T(8,128)(2,1)S(1)} %get-tuple-element.56), channel_id=1, source_target_pairs={{0,24},{2,26},{4,28},{6,30},{8,0},{10,2},{12,4},{14,6},{16,8},{18,... | collective-permute-start | bytes 1179656 | tf_op jit(solution)/shard_map/ppermute | solution.py:51
  22.5 7.5 %collective-permute-done.4 = bf16[384,512]{1,0:T(8,128)(2,1)S(1)} collective-permute-done((bf16[384,512]{1,0:T(8,128)(2,1)S(1)}, bf16[384,512]{1,0:T(8,128)(2,1)S(1)}, u32[]{:S(2)}, u32[]{:S(2)}) %collective-permute-start.4) | collective-permute-done | bytes 393248 | tf_op jit(solution)/shard_map/ppermute | solution.py:51
  30.0 3.7 %collective-permute-start.5 = (bf16[384,512]{1,0:T(8,128)(2,1)S(1)}, bf16[384,512]{1,0:T(8,128)(2,1)S(1)}, u32[]{:S(2)}, u32[]{:S(2)}) collective-permute-start(bf16[384,512]{1,0:T(8,128)(2,1)S(1)} %collective-permute-done.4), channel_id=1, source_target_pairs={{0,24},{2,26},{4,28},{6,30},{8,32},{10,34},{12,36},{14,38},{16,40}... | collective-permute-start | bytes 1179656 | tf_op jit(solution)/shard_map/ppermute | solution.py:61
  33.7 2.6 %copy-done.2 = bf16[2688,1024]{1,0:T(8,128)(2,1)S(1)} copy-done((bf16[2688,1024]{1,0:T(8,128)(2,1)S(1)}, bf16[2688,1024]{1,0:T(8,128)(2,1)}, u32[]{:S(2)}) %copy-start.2) | copy-done | bytes 5505048
  40.0 2.5 %collective-permute-start.8 = (bf16[2,128,256]{2,1,0:T(8,128)(2,1)S(1)}, bf16[2,128,256]{2,1,0:T(8,128)(2,1)S(1)}, u32[]{:S(2)}, u32[]{:S(2)}) collective-permute-start(bf16[2,128,256]{2,1,0:T(8,128)(2,1)S(1)} %get-tuple-element.60), channel_id=1, source_target_pairs={{0,4},{2,6},{4,0},{6,2},{8,12},{10,14},{12,8},{14,10},{16,20},{18,... | collective-permute-start | bytes 393224 | tf_op jit(solution)/shard_map/ppermute | solution.py:28
  47.5 6.6 %collective-permute-done.3.low = bf16[128,512]{1,0:T(8,128)(2,1)S(1)} collective-permute-done((bf16[128,512]{1,0:T(8,128)(2,1)S(1)}, bf16[128,512]{1,0:T(8,128)(2,1)S(1)}, u32[]{:S(2)}, u32[]{:S(2)}) %collective-permute-start.3) | collective-permute-done | bytes 131104 | tf_op jit(solution)/shard_map/ppermute | solution.py:42
  54.1 5.3 %shard_map.80 = (bf16[128,256]{1,0:T(8,128)(2,1)S(1)}, bf16[128,256]{1,0:T(8,128)(2,1)S(1)}, bf16[128,256]{1,0:T(8,128)(2,1)S(1)}, bf16[128,256]{1,0:T(8,128)(2,...) custom-call(s32[4]{0:T(128)S(1)} %pad_add_fusion.pos, ...), custom_call_target="tpu_custom_call" | custom-call | flops 1509949440 | bytes 8388608 | tf_op jit(solution)/shard_map/pallas_call | solution.py:94
  62.9 2.4 %collective-permute-start.12 = (bf16[128,256]{1,0:T(8,128)(2,1)S(1)}, bf16[128,256]{1,0:T(8,128)(2,1)S(1)}, u32[]{:S(2)}, u32[]{:S(2)}) collective-permute-start(bf16[128,256]{1,0:T(8,128)(2,1)S(1)} %get-tuple-element.65), channel_id=1, source_target_pairs={{0,6},{2,0},{4,2},{6,4},{8,14},{10,8},{12,10},{14,12},{16,22},{18,... | collective-permute-start | bytes 196616 | tf_op jit(solution)/shard_map/ppermute | solution.py:28
  72.3 3.0 %collective-permute-start.27 = (bf16[1344,128]{1,0:T(8,128)(2,1)S(1)}, bf16[1344,128]{1,0:T(8,128)(2,1)S(1)}, u32[]{:S(2)}, u32[]{:S(2)}) collective-permute-start(bf16[1344,128]{1,0:T(8,128)(2,1)S(1)} %dynamic-slice_bitcast_fusion), channel_id=1, source_target_pairs={{0,4},{2,6},{4,0},{6,2},{8,12},{10,14},{12,8},{14,10},{16,20},{18,... | collective-permute-start | bytes 1032200 | tf_op jit(solution)/shard_map/ppermute | solution.py:28
  75.4 2.6 %copy-done.1 = bf16[1024,2688]{1,0:T(8,128)(2,1)S(1)} copy-done((bf16[1024,2688]{1,0:T(8,128)(2,1)S(1)}, bf16[1024,2688]{1,0:T(8,128)(2,1)}, u32[]{:S(2)}) %copy-start.1) | copy-done | bytes 5505048
  79.3 2.5 %shard_map.83 = (bf16[128,256]{1,0:T(8,128)(2,1)S(1)}, bf16[128,256]{1,0:T(8,128)(2,1)S(1)}, bf16[128,256]{1,0:T(8,128)(2,1)S(1)}, bf16[128,256]{1,0:T(8,128)(2,1)S(1)}) custom-call(s32[4]{0:T(128)S(1)} %pad_add_fusion.pos, f32[128,2688]{1,0:T(8,128)S(1)} %copy-done.9, bf16[128,2688]{1,0:T(8,128)(2,1)S(1)} %collective-permute-done.13.other, ...), custom_call_target="tpu_custom_call" | custom-call | flops 704643072 | bytes 5505024 | tf_op jit(solution)/shard_map/pallas_call | solution.py:94
  86.6 5.1 %collective-permute-done.27.r2 = bf16[1344,128]{1,0:T(8,128)(2,1)S(1)} collective-permute-done((bf16[1344,128]{1,0:T(8,128)(2,1)S(1)}, bf16[1344,128]{1,0:T(8,128)(2,1)S(1)}, u32[]{:S(2)}, u32[]{:S(2)}) %collective-permute-start.27) | collective-permute-done | bytes 344096 | tf_op jit(solution)/shard_map/ppermute | solution.py:28
  94.0 5.0 %shard_map.84 = (bf16[128,256]{1,0:T(8,128)(2,1)S(1)}, bf16[128,256]{1,0:T(8,128)(2,1)S(1)}, bf16[128,256]{1,0:T(8,128)(2,1)S(1)}, bf16[128,256]{1,0:T(8,128)(2,...) custom-call(s32[4]{0:T(128)S(1)} %pad_add_fusion.pos, ...), custom_call_target="tpu_custom_call" | custom-call | flops 1207959552 | bytes 6291456 | tf_op jit(solution)/shard_map/pallas_call | solution.py:94
  102.2 3.0 %collective-permute-start.23 = (bf16[128,256]{1,0:T(8,128)(2,1)S(1)}, bf16[128,256]{1,0:T(8,128)(2,1)S(1)}, u32[]{:S(2)}, u32[]{:S(2)}) collective-permute-start(bf16[128,256]{1,0:T(8,128)(2,1)S(1)} %get-tuple-element.83), channel_id=1, source_target_pairs={{0,4},{2,6},{4,0},{6,2},{8,12},{10,14},{12,8},{14,10},{16,20},{18,... | collective-permute-start | bytes 196616 | tf_op jit(solution)/shard_map/ppermute | solution.py:28
  105.5 6.8 %collective-permute-done.17.near = bf16[512,256]{1,0:T(8,128)(2,1)S(1)} collective-permute-done((bf16[512,256]{1,0:T(8,128)(2,1)S(1)}, bf16[512,256]{1,0:T(8,128)(2,1)S(1)}, u32[]{:S(2)}, u32[]{:S(2)}) %collective-permute-start.17) | collective-permute-done | bytes 262176 | tf_op jit(solution)/shard_map/ppermute | solution.py:42
  114.0 3.0 %collective-permute-start.20 = (bf16[128,256]{1,0:T(8,128)(2,1)S(1)}, bf16[128,256]{1,0:T(8,128)(2,1)S(1)}, u32[]{:S(2)}, u32[]{:S(2)}) collective-permute-start(bf16[128,256]{1,0:T(8,128)(2,1)S(1)} %get-tuple-element.79.c2), channel_id=1, source_target_pairs={{0,4},{2,6},{4,0},{6,2},{8,12},{10,14},{12,8},{14,10},{16,20},{18,... | collective-permute-start | bytes 196616 | tf_op jit(solution)/shard_map/ppermute | solution.py:28
  120.3 2.7 %collective-permute-start.33 = (bf16[672,256]{1,0:T(8,128)(2,1)S(1)}, bf16[672,256]{1,0:T(8,128)(2,1)S(1)}, u32[]{:S(2)}, u32[]{:S(2)}) collective-permute-start(bf16[672,256]{1,0:T(8,128)(2,1)S(1)} %get-tuple-element.90), channel_id=1, source_target_pairs={{0,64},{2,66},{4,68},{6,70},{8,72},{10,74},{12,76},{14,78},{16,80}... | collective-permute-start | bytes 1032200 | tf_op jit(solution)/shard_map/ppermute | solution.py:38
  127.1 2.3 %shard_map.87 = (f32[1344,128]{1,0:T(8,128)S(1)}, bf16[1344,128]{1,0:T(8,128)(2,1)S(1)}) custom-call(s32[4]{0:T(128)S(1)} %pad_add_fusion.pos, bf16[128,256]{1,0:T(8,128)(2,1)S(1)} %get-tuple-element.77.c0, bf16[128,256]{1,0:T(8,128)(2,1)S(1)} %collective-permute-done.19.c1, bf16[128,256]{1,0:T(8,128)(2,1)S(1)} %collective-permute-done.20.c2, ...), custom_call_target="tpu_custom_call" | custom-call | flops 704643072 | bytes 5505024 | tf_op jit(solution)/shard_map/pallas_call | solution.py:94
  130.6 6.6 %collective-permute-done.33.refs_2_ = bf16[672,256]{1,0:T(8,128)(2,1)S(1)} collective-permute-done((bf16[672,256]{1,0:T(8,128)(2,1)S(1)}, bf16[672,256]{1,0:T(8,128)(2,1)S(1)}, u32[]{:S(2)}, u32[]{:S(2)}) %collective-permute-start.33) | collective-permute-done | bytes 344096 | tf_op jit(solution)/shard_map/ppermute | solution.py:38
  138.2 4.7 %collective-permute-start.36 = (bf16[168,256]{1,0:T(8,128)(2,1)S(1)}, bf16[168,256]{1,0:T(8,128)(2,1)S(1)}, u32[]{:S(2)}, u32[]{:S(2)}) collective-permute-start(bf16[168,256]{1,0:T(8,128)(2,1)S(1)} %get-tuple-element.94), channel_id=1, source_target_pairs={{0,16},{2,18},{4,20},{6,22},{8,24},{10,26},{12,28},{14,30},{16,0},... | collective-permute-start | bytes 258056 | tf_op jit(solution)/shard_map/ppermute | solution.py:32
  142.8 2.5 %collective-permute-start.37 = (bf16[168,256]{1,0:T(8,128)(2,1)S(1)}, bf16[168,256]{1,0:T(8,128)(2,1)S(1)}, u32[]{:S(2)}, u32[]{:S(2)}) collective-permute-start(bf16[168,256]{1,0:T(8,128)(2,1)S(1)} %get-tuple-element.95), channel_id=1, source_target_pairs={{0,24},{2,26},{4,28},{6,30},{8,0},{10,2},{12,4},{14,6},{16,8},{18,... | collective-permute-start | bytes 258056 | tf_op jit(solution)/shard_map/ppermute | solution.py:32
  (121 shorter events, 59.5 us)
Async XLA Ops:
  7.6 9.1 %collective-permute-start.1 = (bf16[4,128,128]{2,1,0:T(8,128)(2,1)}, bf16[4,128,128]{2,1,0:T(8,128)(2,1)S(1)}, u32[]{:S(2)}, u32[]{:S(2)}) collective-permute-start(bf16[4,128,128]{2,1,0:T(8,128)(2,1)} %get-tuple-element.53), channel_id=1, source_target_pairs={{0,4},{2,6},{4,0},{6,2},{8,12},{10,14},{12,8},{14,10},{16,20},{18,... | collective-permute-start | bytes 393224 | tf_op jit(solution)/shard_map/ppermute | solution.py:28
  18.4 11.6 %collective-permute-start.4 = (bf16[384,512]{1,0:T(8,128)(2,1)S(1)}, bf16[384,512]{1,0:T(8,128)(2,1)S(1)}, u32[]{:S(2)}, u32[]{:S(2)}) collective-permute-start(bf16[384,512]{1,0:T(8,128)(2,1)S(1)} %get-tuple-element.56), channel_id=1, source_target_pairs={{0,24},{2,26},{4,28},{6,30},{8,0},{10,2},{12,4},{14,6},{16,8},{18,... | collective-permute-start | bytes 1179656 | tf_op jit(solution)/shard_map/ppermute | solution.py:51
  22.5 31.6 %collective-permute-start.6 = (bf16[512,512]{1,0:T(8,128)(2,1)S(1)}, bf16[512,512]{1,0:T(8,128)(2,1)S(1)}, u32[]{:S(2)}, u32[]{:S(2)}) collective-permute-start(bf16[512,512]{1,0:T(8,128)(2,1)S(1)} %get-tuple-element.57.own.own_kv), channel_id=1, source_target_pairs={{0,8},{2,10},{4,12},{6,14},{8,16},{10,18},{12,20},{14,22},{16,24},... | collective-permute-start | bytes 1572872 | tf_op jit(solution)/shard_map/ppermute | solution.py:42
  30.0 24.1 %collective-permute-start.5 = (bf16[384,512]{1,0:T(8,128)(2,1)S(1)}, bf16[384,512]{1,0:T(8,128)(2,1)S(1)}, u32[]{:S(2)}, u32[]{:S(2)}) collective-permute-start(bf16[384,512]{1,0:T(8,128)(2,1)S(1)} %collective-permute-done.4), channel_id=1, source_target_pairs={{0,24},{2,26},{4,28},{6,30},{8,32},{10,34},{12,36},{14,38},{16,40}... | collective-permute-start | bytes 1179656 | tf_op jit(solution)/shard_map/ppermute | solution.py:61
  45.5 8.6 %collective-permute-start.3 = (bf16[128,512]{1,0:T(8,128)(2,1)S(1)}, bf16[128,512]{1,0:T(8,128)(2,1)S(1)}, u32[]{:S(2)}, u32[]{:S(2)}) collective-permute-start(bf16[128,512]{1,0:T(8,128)(2,1)S(1)} %get-tuple-element.55), channel_id=1, source_target_pairs={{0,16},{2,18},{4,20},{6,22},{8,24},{10,26},{12,28},{14,30},{16,32}... | collective-permute-start | bytes 393224 | tf_op jit(solution)/shard_map/ppermute | solution.py:42
  70.9 13.4 %collective-permute-start.26 = (bf16[1344,128]{1,0:T(8,128)(2,1)S(1)}, bf16[1344,128]{1,0:T(8,128)(2,1)S(1)}, u32[]{:S(2)}, u32[]{:S(2)}) collective-permute-start(bf16[1344,128]{1,0:T(8,128)(2,1)S(1)} %dynamic-slice_bitcast_fusion), channel_id=1, source_target_pairs={{0,2},{2,4},{4,6},{6,0},{8,10},{10,12},{12,14},{14,8},{16,18},{18,... | collective-permute-start | bytes 1032200 | tf_op jit(solution)/shard_map/ppermute | solution.py:28
  72.3 19.3 %collective-permute-start.27 = (bf16[1344,128]{1,0:T(8,128)(2,1)S(1)}, bf16[1344,128]{1,0:T(8,128)(2,1)S(1)}, u32[]{:S(2)}, u32[]{:S(2)}) collective-permute-start(bf16[1344,128]{1,0:T(8,128)(2,1)S(1)} %dynamic-slice_bitcast_fusion), channel_id=1, source_target_pairs={{0,4},{2,6},{4,0},{6,2},{8,12},{10,14},{12,8},{14,10},{16,20},{18,... | collective-permute-start | bytes 1032200 | tf_op jit(solution)/shard_map/ppermute | solution.py:28
  75.3 16.3 %collective-permute-start.28 = (bf16[1344,128]{1,0:T(8,128)(2,1)S(1)}, bf16[1344,128]{1,0:T(8,128)(2,1)S(1)}, u32[]{:S(2)}, u32[]{:S(2)}) collective-permute-start(bf16[1344,128]{1,0:T(8,128)(2,1)S(1)} %dynamic-slice_bitcast_fusion), channel_id=1, source_target_pairs={{0,6},{2,0},{4,2},{6,4},{8,14},{10,8},{12,10},{14,12},{16,22},{18,... | collective-permute-start | bytes 1032200 | tf_op jit(solution)/shard_map/ppermute | solution.py:28
  81.8 11.1 %collective-permute-start.14 = (bf16[128,256]{1,0:T(8,128)(2,1)S(1)}, bf16[128,256]{1,0:T(8,128)(2,1)S(1)}, u32[]{:S(2)}, u32[]{:S(2)}) collective-permute-start(bf16[128,256]{1,0:T(8,128)(2,1)S(1)} %get-tuple-element.69), channel_id=1, source_target_pairs={{0,2},{2,4},{4,6},{6,0},{8,10},{10,12},{12,14},{14,8},{16,18},{18,... | collective-permute-start | bytes 196616 | tf_op jit(solution)/shard_map/ppermute | solution.py:28
  83.8 10.2 %collective-permute-start.15 = (bf16[128,256]{1,0:T(8,128)(2,1)S(1)}, bf16[128,256]{1,0:T(8,128)(2,1)S(1)}, u32[]{:S(2)}, u32[]{:S(2)}) collective-permute-start(bf16[128,256]{1,0:T(8,128)(2,1)S(1)} %get-tuple-element.70), channel_id=1, source_target_pairs={{0,4},{2,6},{4,0},{6,2},{8,12},{10,14},{12,8},{14,10},{16,20},{18,... | collective-permute-start | bytes 196616 | tf_op jit(solution)/shard_map/ppermute | solution.py:28
  84.4 9.6 %collective-permute-start.16 = (bf16[128,256]{1,0:T(8,128)(2,1)S(1)}, bf16[128,256]{1,0:T(8,128)(2,1)S(1)}, u32[]{:S(2)}, u32[]{:S(2)}) collective-permute-start(bf16[128,256]{1,0:T(8,128)(2,1)S(1)} %get-tuple-element.71), channel_id=1, source_target_pairs={{0,6},{2,0},{4,2},{6,4},{8,14},{10,8},{12,10},{14,12},{16,22},{18,... | collective-permute-start | bytes 196616 | tf_op jit(solution)/shard_map/ppermute | solution.py:28
  91.7 8.8 %collective-permute-start.29 = (bf16[1344,128]{1,0:T(8,128)(2,1)S(1)}, bf16[1344,128]{1,0:T(8,128)(2,1)S(1)}, u32[]{:S(2)}, u32[]{:S(2)}) collective-permute-start(bf16[1344,128]{1,0:T(8,128)(2,1)S(1)} %collective-permute-done.26.r1), channel_id=1, source_target_pairs={{0,1},{1,0},{2,3},{3,2},{4,5},{5,4},{6,7},{7,6},{8,9},{9,8},{10,11... | collective-permute-start | bytes 1032200 | tf_op jit(solution)/shard_map/ppermute | solution.py:65
  91.7 8.8 %collective-permute-start.30 = (bf16[1344,128]{1,0:T(8,128)(2,1)S(1)}, bf16[1344,128]{1,0:T(8,128)(2,1)S(1)}, u32[]{:S(2)}, u32[]{:S(2)}) collective-permute-start(bf16[1344,128]{1,0:T(8,128)(2,1)S(1)} %collective-permute-done.27.r2), channel_id=1, source_target_pairs={{0,1},{1,0},{2,3},{3,2},{4,5},{5,4},{6,7},{7,6},{8,9},{9,8},{10,11... | collective-permute-start | bytes 1032200 | tf_op jit(solution)/shard_map/ppermute | solution.py:65
  99.1 13.3 %collective-permute-start.17 = (bf16[512,256]{1,0:T(8,128)(2,1)S(1)}, bf16[512,256]{1,0:T(8,128)(2,1)S(1)}, u32[]{:S(2)}, u32[]{:S(2)}) collective-permute-start(bf16[512,256]{1,0:T(8,128)(2,1)S(1)} %get-tuple-element.75), channel_id=1, source_target_pairs={{0,120},{2,122},{4,124},{6,126},{8,0},{10,2},{12,4},{14,6},{16,8},... | collective-permute-start | bytes 786440 | tf_op jit(solution)/shard_map/ppermute | solution.py:42
  99.3 13.0 %collective-permute-start.18 = (bf16[512,256]{1,0:T(8,128)(2,1)S(1)}, bf16[512,256]{1,0:T(8,128)(2,1)S(1)}, u32[]{:S(2)}, u32[]{:S(2)}) collective-permute-start(bf16[512,256]{1,0:T(8,128)(2,1)S(1)} %get-tuple-element.76), channel_id=1, source_target_pairs={{0,112},{2,114},{4,116},{6,118},{8,120},{10,122},{12,124},{14,126}... | collective-permute-start | bytes 786440 | tf_op jit(solution)/shard_map/ppermute | solution.py:42
  101.6 16.9 %collective-permute-start.22 = (bf16[128,256]{1,0:T(8,128)(2,1)S(1)}, bf16[128,256]{1,0:T(8,128)(2,1)S(1)}, u32[]{:S(2)}, u32[]{:S(2)}) collective-permute-start(bf16[128,256]{1,0:T(8,128)(2,1)S(1)} %get-tuple-element.82), channel_id=1, source_target_pairs={{0,2},{2,4},{4,6},{6,0},{8,10},{10,12},{12,14},{14,8},{16,18},{18,... | collective-permute-start | bytes 196616 | tf_op jit(solution)/shard_map/ppermute | solution.py:28
  102.2 16.3 %collective-permute-start.23 = (bf16[128,256]{1,0:T(8,128)(2,1)S(1)}, bf16[128,256]{1,0:T(8,128)(2,1)S(1)}, u32[]{:S(2)}, u32[]{:S(2)}) collective-permute-start(bf16[128,256]{1,0:T(8,128)(2,1)S(1)} %get-tuple-element.83), channel_id=1, source_target_pairs={{0,4},{2,6},{4,0},{6,2},{8,12},{10,14},{12,8},{14,10},{16,20},{18,... | collective-permute-start | bytes 196616 | tf_op jit(solution)/shard_map/ppermute | solution.py:28
  105.2 15.1 %collective-permute-start.24 = (bf16[128,256]{1,0:T(8,128)(2,1)S(1)}, bf16[128,256]{1,0:T(8,128)(2,1)S(1)}, u32[]{:S(2)}, u32[]{:S(2)}) collective-permute-start(bf16[128,256]{1,0:T(8,128)(2,1)S(1)} %get-tuple-element.84), channel_id=1, source_target_pairs={{0,6},{2,0},{4,2},{6,4},{8,14},{10,8},{12,10},{14,12},{16,22},{18,... | collective-permute-start | bytes 196616 | tf_op jit(solution)/shard_map/ppermute | solution.py:28
  113.0 10.1 %collective-permute-start.19 = (bf16[128,256]{1,0:T(8,128)(2,1)S(1)}, bf16[128,256]{1,0:T(8,128)(2,1)S(1)}, u32[]{:S(2)}, u32[]{:S(2)}) collective-permute-start(bf16[128,256]{1,0:T(8,128)(2,1)S(1)} %get-tuple-element.78.c1), channel_id=1, source_target_pairs={{0,2},{2,4},{4,6},{6,0},{8,10},{10,12},{12,14},{14,8},{16,18},{18,... | collective-permute-start | bytes 196616 | tf_op jit(solution)/shard_map/ppermute | solution.py:28
  114.0 12.6 %collective-permute-start.20 = (bf16[128,256]{1,0:T(8,128)(2,1)S(1)}, bf16[128,256]{1,0:T(8,128)(2,1)S(1)}, u32[]{:S(2)}, u32[]{:S(2)}) collective-permute-start(bf16[128,256]{1,0:T(8,128)(2,1)S(1)} %get-tuple-element.79.c2), channel_id=1, source_target_pairs={{0,4},{2,6},{4,0},{6,2},{8,12},{10,14},{12,8},{14,10},{16,20},{18,... | collective-permute-start | bytes 196616 | tf_op jit(solution)/shard_map/ppermute | solution.py:28
  118.5 12.1 %collective-permute-start.32 = (bf16[672,256]{1,0:T(8,128)(2,1)S(1)}, bf16[672,256]{1,0:T(8,128)(2,1)S(1)}, u32[]{:S(2)}, u32[]{:S(2)}) collective-permute-start(bf16[672,256]{1,0:T(8,128)(2,1)S(1)} %get-tuple-element.89), channel_id=1, source_target_pairs={{0,32},{2,34},{4,36},{6,38},{8,40},{10,42},{12,44},{14,46},{16,48}... | collective-permute-start | bytes 1032200 | tf_op jit(solution)/shard_map/ppermute | solution.py:38
  120.3 16.9 %collective-permute-start.33 = (bf16[672,256]{1,0:T(8,128)(2,1)S(1)}, bf16[672,256]{1,0:T(8,128)(2,1)S(1)}, u32[]{:S(2)}, u32[]{:S(2)}) collective-permute-start(bf16[672,256]{1,0:T(8,128)(2,1)S(1)} %get-tuple-element.90), channel_id=1, source_target_pairs={{0,64},{2,66},{4,68},{6,70},{8,72},{10,74},{12,76},{14,78},{16,80}... | collective-permute-start | bytes 1032200 | tf_op jit(solution)/shard_map/ppermute | solution.py:38
  123.0 14.2 %collective-permute-start.34 = (bf16[672,256]{1,0:T(8,128)(2,1)S(1)}, bf16[672,256]{1,0:T(8,128)(2,1)S(1)}, u32[]{:S(2)}, u32[]{:S(2)}) collective-permute-start(bf16[672,256]{1,0:T(8,128)(2,1)S(1)} %get-tuple-element.91), channel_id=1, source_target_pairs={{0,96},{2,98},{4,100},{6,102},{8,104},{10,106},{12,108},{14,110},{... | collective-permute-start | bytes 1032200 | tf_op jit(solution)/shard_map/ppermute | solution.py:38
  129.3 23.3 %collective-permute-start.25 = (bf16[1344,128]{1,0:T(8,128)(2,1)S(1)}, bf16[1344,128]{1,0:T(8,128)(2,1)S(1)}, u32[]{:S(2)}, u32[]{:S(2)}) collective-permute-start(bf16[1344,128]{1,0:T(8,128)(2,1)S(1)} %get-tuple-element.86), channel_id=1, source_target_pairs={{0,1},{1,0},{2,3},{3,2},{4,5},{5,4},{6,7},{7,6},{8,9},{9,8},{10,11... | collective-permute-start | bytes 1032200 | tf_op jit(solution)/shard_map/ppermute | solution.py:65
  (38 other events, 329.3 us)

commit v4 on v3

--- a/solution.py
+++ b/solution.py
@@ -58,6 +58,20 @@
     for i in range(64):
         source = i // 16 * 16 + (i // 4 + 1) % 4 * 4 + i % 4
         route.append((i, (source + 8) % 64))
+    return lax.ppermute(x, "seq", route)
+
+
+def back_one(x):
+    return lax.ppermute(
+        x, "seq", [(i, i // 16 * 16 + (i // 4 + 1) % 4 * 4 + i % 4) for i in range(64)]
+    )
+
+
+def back_two(x):
+    route = []
+    for i in range(64):
+        source = i // 16 * 16 + (i // 4 + 3) % 4 * 4 + i % 4
+        route.append((i, (source - 8) % 64))
     return lax.ppermute(x, "seq", route)
 
 
@@ -276,7 +290,7 @@
 
 
 def backward_kernel(pos, g0, g1, g2, g3, low, high, near_kv, own_kv, q_all, p_all, *refs):
-    q0, q1, q2, q3, own, near, far, dk, dv, gbuf, dqbuf = refs
+    q0, q1, q2, q3, own, near, far_low, far_high, dk, dv, gbuf, dqbuf = refs
     lines = (low, high, near_kv, own_kv)
     for d, g in enumerate((g0, g1, g2, g3)):
         gbuf[lax.rem(pos[2] + 4 - d, 4)] = g[...]
@@ -304,8 +318,10 @@
             dv[rows] += dv_part[: 8 * HEAD]
             dk[fresh] = dk_part[8 * HEAD :]
             dv[fresh] = dv_part[8 * HEAD :]
-    far[:, :HEAD] = (dk[:512, :] * SCALE).astype(BF)
-    far[:, HEAD:] = dv[:512, :].astype(BF)
+    for i, far in enumerate((far_low, far_high)):
+        rows = slice(i * 256, i * 256 + 256)
+        far[:, :HEAD] = (dk[rows, :] * SCALE).astype(BF)
+        far[:, HEAD:] = dv[rows, :].astype(BF)
     near[:, :HEAD] = (dk[512:1024, :] * SCALE).astype(BF)
     near[:, HEAD:] = dv[512:1024, :].astype(BF)
     own[:, :HEAD] = dk[1024:, :] * SCALE
@@ -314,13 +330,14 @@
         q[...] = dqbuf[lax.rem(pos[2] + d, 4)]
 
 
-def pair_kernel(pos, own, near, far, *outs):
+def pair_kernel(pos, own, near, low, high, *outs):
     y = pos[2]
     for d in range(4):
         rows = pl.ds(pl.multiple_of(lax.rem(y + d, 4) * HEAD, HEAD), HEAD)
-        outs[d][...] = (
-            own[rows, :] + near[rows, :].astype(F32) + far[rows, :].astype(F32)
-        ).astype(BF)
+        block = lax.rem(y + d, 4)
+        half = pl.ds(pl.multiple_of(lax.rem(block, 2) * HEAD, HEAD), HEAD)
+        far = jnp.where(block < 2, low[half, :].astype(F32), high[half, :].astype(F32))
+        outs[d][...] = (own[rows, :] + near[rows, :].astype(F32) + far).astype(BF)
 
 
 def query_input_kernel(pos, q0, q1, q2, q3, w, total, buf):
@@ -491,7 +508,7 @@
     back = flat_call(
         backward_kernel,
         [pos] + [(vmem(), a) for a in g + lines + [q_all, p_all]],
-        [out((rows, 256), BF)] * 4 + [out((512, 256), F32), out((512, 256), BF), out((512, 256), BF)],
+        [out((rows, 256), BF)] * 4 + [out((512, 256), F32), out((512, 256), BF)] + [out((256, 256), BF)] * 2,
         [
             pltpu.VMEM((1536, HEAD), F32),
             pltpu.VMEM((1536, HEAD), F32),
@@ -502,14 +519,15 @@
         moved=6 << 20,
         limit=24,
     )
-    dq, (own, to_near, to_far) = back[:4], back[4:]
-    from_far = lines_on(to_far, -2)
+    dq, (own, to_near, to_low, to_high) = back[:4], back[4:]
+    high = back_one(to_high)
     from_near = lines_on(to_near, -1)
+    from_low = lines_on(to_low, -2)
+    from_high = back_two(high)
     dq = exchange(ring_y, dq)
-    pair = call(
+    pair = flat_call(
         pair_kernel,
-        (1,),
-        [pos] + [(whole((512, 256)), a) for a in (own, from_near, from_far)],
+        [pos] + [(vmem(), a) for a in (own, from_near, from_low, from_high)],
         [out((rows, 256), BF)] * 4,
         moved=1 << 20,
     )

time: 157 us -> 159 us (1.013)
  waiting for transfers between devices: 50.2 us -> 54.5 us
  starting transfers between devices: 60.3 us -> 57.7 us
    ppermute x4, waiting for transfers between devices: 13.4 us -> 6.59 us  [lines_on(): return lax.ppermute(x, 'seq', [(i, (i + 4 * d) % 64) for i in range(64)])]
    ppermute x0 -> x2, waiting for transfers between devices: none -> 5.84 us  [the longest x1 5.83 us: back_one(): lax.ppermute(x, 'seq', [(i, i // 16 * 16 + (i // 4 + 1) % 4 * 4 + i % 4)...]
    ppermute x24, waiting for transfers between devices: 19.3 us -> 23.7 us  [ring_y(): lax.ppermute(x, 'seq', [(i, i // 4 * 4 + (i + d) % 4) for i in range(64)])]
    ppermute x3, starting transfers between devices: 7.27 us -> 4.48 us  [ring_z(): lax.ppermute(x, 'seq', [(i, i // 16 * 16 + (i // 4 + d) % 4 * 4 + i % 4)...]
    ppermute x3, waiting for transfers between devices: 2.1 us -> 4.48 us  [ring_z(): lax.ppermute(x, 'seq', [(i, i // 16 * 16 + (i // 4 + d) % 4 * 4 + i % 4)...]
    ppermute x0 -> x2, starting transfers between devices: none -> 1.84 us  [the longest x1 1.78 us: back_one(): lax.ppermute(x, 'seq', [(i, i // 16 * 16 + (i // 4 + 1) % 4 * 4 + i % 4)...]
    pallas_call x14 -> x15, Pallas kernels: 31.7 us -> 32.4 us  [flat_call(): pl.pallas_call(kernel, in_specs=list(specs_in), out_specs=[pl.BlockSpec(m...]
  transfers between devices with their start and end apart: 41 -> 43, of which waited for: 20 -> 23; matrix products, arithmetic and copies ran while one was open for 1% -> 1% of each run, Pallas kernels for 13% -> 12%
where the time goes in v4:
time: 159 us
  starting transfers between devices  57.7 us (36%)
  waiting for transfers between devices  54.5 us (34%)
  Pallas kernels  33.8 us (21%)
  local copies, waits for them, and re-layouts  10.7 us (7%)
    ppermute x24, starting transfers between devices, ring_y(): lax.ppermute(x, 'seq', [(i, i // 4 * 4 + (i + d) % 4) for i in range(64)])  38.3 us
    pallas_call x15, Pallas kernels, flat_call(): pl.pallas_call(kernel, in_specs=list(specs_in), out_specs=[pl.BlockSpec(m...  32.4 us
    ppermute x24, waiting for transfers between devices, ring_y(): lax.ppermute(x, 'seq', [(i, i // 4 * 4 + (i + d) % 4) for i in range(64)])  23.7 us
    unnamed x42, local copies, waits for them, and re-layouts  10.4 us
    ppermute x1, waiting for transfers between devices, far_one(): lax.ppermute(x, 'seq', [(i, i // 16 * 16 + (i // 4 + 3) % 4 * 4 + i % 4)...  7.51 us
    ppermute x4, waiting for transfers between devices, lines_on(): return lax.ppermute(x, 'seq', [(i, (i + 4 * d) % 64) for i in range(64)])  6.59 us
    ppermute x3, waiting for transfers between devices, ring_x(): lax.ppermute(x, 'seq', [(i, (i // 16 + d) % 4 * 16 + i % 16) for i in ran...  6.44 us
    ppermute x1, waiting for transfers between devices, back_one(): lax.ppermute(x, 'seq', [(i, i // 16 * 16 + (i // 4 + 1) % 4 * 4 + i % 4)...  5.83 us
  transfers between devices with their start and end apart: 43, of which 23 were waited for; matrix products, arithmetic and copies ran while one was open for 1% of the time, Pallas kernels for 12%

profile of v4, /device:TPU:0, one launch (start us, length us, event | category | flops | bytes accessed | tf_op | source)
XLA Modules:
  0.0 158.5 jit_solution(2375413774976699920)
XLA Ops:
  0.6 5.2 %shard_map.77 = (bf16[4,128,128]{2,1,0:T(8,128)(2,1)}, bf16[4,128,128]{2,1,0:T(8,128)(2,1)}, bf16[4,128,128]{2,1,0:T(8,128)(2,1)}, bf16[4,128,128]{2,1,0:T(8,128)(2,1)}) custom-call(bf16[128,2688]{1,0:T(8,128)(2,1)} %tok.3, bf16[128,2688]{1,0:T(8,128)(2,1)} %tan.3, bf16[2688,512]{1,0:T(8,128)(2,1)} %wk.3, bf16[2688,512]{1,0:T(8,128)(2,1)} %wv.3), custom_call_target="tpu_custom_call" | custom-call | flops 1409286144 | bytes 5505024 | tf_op jit(solution)/shard_map/pallas_call | solution.py:108
  7.6 2.9 %collective-permute-start.1 = (bf16[4,128,128]{2,1,0:T(8,128)(2,1)}, bf16[4,128,128]{2,1,0:T(8,128)(2,1)S(1)}, u32[]{:S(2)}, u32[]{:S(2)}) collective-permute-start(bf16[4,128,128]{2,1,0:T(8,128)(2,1)} %get-tuple-element.54), channel_id=1, source_target_pairs={{0,4},{2,6},{4,0},{6,2},{8,12},{10,14},{12,8},{14,10},{16,20},{18,... | collective-permute-start | bytes 393224 | tf_op jit(solution)/shard_map/ppermute | solution.py:28
  12.8 4.0 %collective-permute-done.1.c = bf16[4,128,128]{2,1,0:T(8,128)(2,1)S(1)} collective-permute-done((bf16[4,128,128]{2,1,0:T(8,128)(2,1)}, bf16[4,128,128]{2,1,0:T(8,128)(2,1)S(1)}, u32[]{:S(2)}, u32[]{:S(2)}) %collective-permute-start.1) | collective-permute-done | bytes 131104 | tf_op jit(solution)/shard_map/ppermute | solution.py:28
  18.4 4.1 %collective-permute-start.4 = (bf16[384,512]{1,0:T(8,128)(2,1)S(1)}, bf16[384,512]{1,0:T(8,128)(2,1)S(1)}, u32[]{:S(2)}, u32[]{:S(2)}) collective-permute-start(bf16[384,512]{1,0:T(8,128)(2,1)S(1)} %get-tuple-element.57), channel_id=1, source_target_pairs={{0,24},{2,26},{4,28},{6,30},{8,0},{10,2},{12,4},{14,6},{16,8},{18,... | collective-permute-start | bytes 1179656 | tf_op jit(solution)/shard_map/ppermute | solution.py:51
  22.5 7.5 %collective-permute-done.4 = bf16[384,512]{1,0:T(8,128)(2,1)S(1)} collective-permute-done((bf16[384,512]{1,0:T(8,128)(2,1)S(1)}, bf16[384,512]{1,0:T(8,128)(2,1)S(1)}, u32[]{:S(2)}, u32[]{:S(2)}) %collective-permute-start.4) | collective-permute-done | bytes 393248 | tf_op jit(solution)/shard_map/ppermute | solution.py:51
  30.0 3.7 %collective-permute-start.5 = (bf16[384,512]{1,0:T(8,128)(2,1)S(1)}, bf16[384,512]{1,0:T(8,128)(2,1)S(1)}, u32[]{:S(2)}, u32[]{:S(2)}) collective-permute-start(bf16[384,512]{1,0:T(8,128)(2,1)S(1)} %collective-permute-done.4), channel_id=1, source_target_pairs={{0,24},{2,26},{4,28},{6,30},{8,32},{10,34},{12,36},{14,38},{16,40}... | collective-permute-start | bytes 1179656 | tf_op jit(solution)/shard_map/ppermute | solution.py:61
  33.7 2.6 %copy-done.2 = bf16[2688,1024]{1,0:T(8,128)(2,1)S(1)} copy-done((bf16[2688,1024]{1,0:T(8,128)(2,1)S(1)}, bf16[2688,1024]{1,0:T(8,128)(2,1)}, u32[]{:S(2)}) %copy-start.2) | copy-done | bytes 5505048
  40.0 2.5 %collective-permute-start.8 = (bf16[2,128,256]{2,1,0:T(8,128)(2,1)S(1)}, bf16[2,128,256]{2,1,0:T(8,128)(2,1)S(1)}, u32[]{:S(2)}, u32[]{:S(2)}) collective-permute-start(bf16[2,128,256]{2,1,0:T(8,128)(2,1)S(1)} %get-tuple-element.61), channel_id=1, source_target_pairs={{0,4},{2,6},{4,0},{6,2},{8,12},{10,14},{12,8},{14,10},{16,20},{18,... | collective-permute-start | bytes 393224 | tf_op jit(solution)/shard_map/ppermute | solution.py:28
  47.5 6.6 %collective-permute-done.3.low = bf16[128,512]{1,0:T(8,128)(2,1)S(1)} collective-permute-done((bf16[128,512]{1,0:T(8,128)(2,1)S(1)}, bf16[128,512]{1,0:T(8,128)(2,1)S(1)}, u32[]{:S(2)}, u32[]{:S(2)}) %collective-permute-start.3) | collective-permute-done | bytes 131104 | tf_op jit(solution)/shard_map/ppermute | solution.py:42
  54.1 5.3 %shard_map.80 = (bf16[128,256]{1,0:T(8,128)(2,1)S(1)}, bf16[128,256]{1,0:T(8,128)(2,1)S(1)}, bf16[128,256]{1,0:T(8,128)(2,1)S(1)}, bf16[128,256]{1,0:T(8,128)(2,...) custom-call(s32[4]{0:T(128)S(1)} %pad_add_fusion.pos, ...), custom_call_target="tpu_custom_call" | custom-call | flops 1509949440 | bytes 8388608 | tf_op jit(solution)/shard_map/pallas_call | solution.py:108
  62.9 2.4 %collective-permute-start.12 = (bf16[128,256]{1,0:T(8,128)(2,1)S(1)}, bf16[128,256]{1,0:T(8,128)(2,1)S(1)}, u32[]{:S(2)}, u32[]{:S(2)}) collective-permute-start(bf16[128,256]{1,0:T(8,128)(2,1)S(1)} %get-tuple-element.66), channel_id=1, source_target_pairs={{0,6},{2,0},{4,2},{6,4},{8,14},{10,8},{12,10},{14,12},{16,22},{18,... | collective-permute-start | bytes 196616 | tf_op jit(solution)/shard_map/ppermute | solution.py:28
  72.3 3.0 %collective-permute-start.29 = (bf16[1344,128]{1,0:T(8,128)(2,1)S(1)}, bf16[1344,128]{1,0:T(8,128)(2,1)S(1)}, u32[]{:S(2)}, u32[]{:S(2)}) collective-permute-start(bf16[1344,128]{1,0:T(8,128)(2,1)S(1)} %dynamic-slice_bitcast_fusion), channel_id=1, source_target_pairs={{0,4},{2,6},{4,0},{6,2},{8,12},{10,14},{12,8},{14,10},{16,20},{18,... | collective-permute-start | bytes 1032200 | tf_op jit(solution)/shard_map/ppermute | solution.py:28
  75.4 7.3 %collective-permute-done.28.r1 = bf16[1344,128]{1,0:T(8,128)(2,1)S(1)} collective-permute-done((bf16[1344,128]{1,0:T(8,128)(2,1)S(1)}, bf16[1344,128]{1,0:T(8,128)(2,1)S(1)}, u32[]{:S(2)}, u32[]{:S(2)}) %collective-permute-start.28) | collective-permute-done | bytes 344096 | tf_op jit(solution)/shard_map/ppermute | solution.py:28
  82.7 2.6 %copy-done.1 = bf16[1024,2688]{1,0:T(8,128)(2,1)S(1)} copy-done((bf16[1024,2688]{1,0:T(8,128)(2,1)S(1)}, bf16[1024,2688]{1,0:T(8,128)(2,1)}, u32[]{:S(2)}) %copy-start.1) | copy-done | bytes 5505048
  86.6 2.5 %shard_map.83 = (bf16[128,256]{1,0:T(8,128)(2,1)S(1)}, bf16[128,256]{1,0:T(8,128)(2,1)S(1)}, bf16[128,256]{1,0:T(8,128)(2,1)S(1)}, bf16[128,256]{1,0:T(8,128)(2,1)S(1)}) custom-call(s32[4]{0:T(128)S(1)} %pad_add_fusion.pos, f32[128,2688]{1,0:T(8,128)S(1)} %copy-done.9, bf16[128,2688]{1,0:T(8,128)(2,1)S(1)} %collective-permute-done.13.other, ...), custom_call_target="tpu_custom_call" | custom-call | flops 704643072 | bytes 5505024 | tf_op jit(solution)/shard_map/pallas_call | solution.py:108
  89.7 3.0 %collective-permute-start.15 = (bf16[128,256]{1,0:T(8,128)(2,1)S(1)}, bf16[128,256]{1,0:T(8,128)(2,1)S(1)}, u32[]{:S(2)}, u32[]{:S(2)}) collective-permute-start(bf16[128,256]{1,0:T(8,128)(2,1)S(1)} %get-tuple-element.71), channel_id=1, source_target_pairs={{0,4},{2,6},{4,0},{6,2},{8,12},{10,14},{12,8},{14,10},{16,20},{18,... | collective-permute-start | bytes 196616 | tf_op jit(solution)/shard_map/ppermute | solution.py:28
  97.0 5.0 %shard_map.84 = (bf16[128,256]{1,0:T(8,128)(2,1)S(1)}, bf16[128,256]{1,0:T(8,128)(2,1)S(1)}, bf16[128,256]{1,0:T(8,128)(2,1)S(1)}, bf16[128,256]{1,0:T(8,128)(2,...) custom-call(s32[4]{0:T(128)S(1)} %pad_add_fusion.pos, ...), custom_call_target="tpu_custom_call" | custom-call | flops 1207959552 | bytes 6291456 | tf_op jit(solution)/shard_map/pallas_call | solution.py:108
  104.2 5.8 %collective-permute-done.19 = bf16[256,256]{1,0:T(8,128)(2,1)S(1)} collective-permute-done((bf16[256,256]{1,0:T(8,128)(2,1)S(1)}, bf16[256,256]{1,0:T(8,128)(2,1)S(1)}, u32[]{:S(2)}, u32[]{:S(2)}) %collective-permute-start.19) | collective-permute-done | bytes 131104 | tf_op jit(solution)/shard_map/ppermute | solution.py:65
  112.2 4.4 %collective-permute-start.25 = (bf16[128,256]{1,0:T(8,128)(2,1)S(1)}, bf16[128,256]{1,0:T(8,128)(2,1)S(1)}, u32[]{:S(2)}, u32[]{:S(2)}) collective-permute-start(bf16[128,256]{1,0:T(8,128)(2,1)S(1)} %get-tuple-element.85), channel_id=1, source_target_pairs={{0,4},{2,6},{4,0},{6,2},{8,12},{10,14},{12,8},{14,10},{16,20},{18,... | collective-permute-start | bytes 196616 | tf_op jit(solution)/shard_map/ppermute | solution.py:28
  119.4 2.9 %collective-permute-start.22 = (bf16[128,256]{1,0:T(8,128)(2,1)S(1)}, bf16[128,256]{1,0:T(8,128)(2,1)S(1)}, u32[]{:S(2)}, u32[]{:S(2)}) collective-permute-start(bf16[128,256]{1,0:T(8,128)(2,1)S(1)} %get-tuple-element.81.c2), channel_id=1, source_target_pairs={{0,4},{2,6},{4,0},{6,2},{8,12},{10,14},{12,8},{14,10},{16,20},{18,... | collective-permute-start | bytes 196616 | tf_op jit(solution)/shard_map/ppermute | solution.py:28
  124.4 2.7 %collective-permute-start.35 = (bf16[672,256]{1,0:T(8,128)(2,1)S(1)}, bf16[672,256]{1,0:T(8,128)(2,1)S(1)}, u32[]{:S(2)}, u32[]{:S(2)}) collective-permute-start(bf16[672,256]{1,0:T(8,128)(2,1)S(1)} %get-tuple-element.92), channel_id=1, source_target_pairs={{0,64},{2,66},{4,68},{6,70},{8,72},{10,74},{12,76},{14,78},{16,80}... | collective-permute-start | bytes 1032200 | tf_op jit(solution)/shard_map/ppermute | solution.py:38
  135.6 4.3 %collective-permute-done.35.refs_2_ = bf16[672,256]{1,0:T(8,128)(2,1)S(1)} collective-permute-done((bf16[672,256]{1,0:T(8,128)(2,1)S(1)}, bf16[672,256]{1,0:T(8,128)(2,1)S(1)}, u32[]{:S(2)}, u32[]{:S(2)}) %collective-permute-start.35) | collective-permute-done | bytes 344096 | tf_op jit(solution)/shard_map/ppermute | solution.py:38
  141.8 3.5 %collective-permute-start.38 = (bf16[168,256]{1,0:T(8,128)(2,1)S(1)}, bf16[168,256]{1,0:T(8,128)(2,1)S(1)}, u32[]{:S(2)}, u32[]{:S(2)}) collective-permute-start(bf16[168,256]{1,0:T(8,128)(2,1)S(1)} %get-tuple-element.96), channel_id=1, source_target_pairs={{0,16},{2,18},{4,20},{6,22},{8,24},{10,26},{12,28},{14,30},{16,0},... | collective-permute-start | bytes 258056 | tf_op jit(solution)/shard_map/ppermute | solution.py:32
  150.7 2.3 %collective-permute-start.41 = (f32[42,256]{1,0:T(8,128)S(1)}, f32[42,256]{1,0:T(8,128)S(1)}, u32[]{:S(2)}, u32[]{:S(2)}) collective-permute-start(f32[42,256]{1,0:T(8,128)S(1)} %get-tuple-element.100), channel_id=1, source_target_pairs={{0,4},{2,6},{4,0},{6,2},{8,12},{10,14},{12,8},{14,10},{16,20},{18,... | collective-permute-start | bytes 129032 | tf_op jit(solution)/shard_map/ppermute | solution.py:28
  (125 shorter events, 61.5 us)
Async XLA Ops:
  7.6 9.1 %collective-permute-start.1 = (bf16[4,128,128]{2,1,0:T(8,128)(2,1)}, bf16[4,128,128]{2,1,0:T(8,128)(2,1)S(1)}, u32[]{:S(2)}, u32[]{:S(2)}) collective-permute-start(bf16[4,128,128]{2,1,0:T(8,128)(2,1)} %get-tuple-element.54), channel_id=1, source_target_pairs={{0,4},{2,6},{4,0},{6,2},{8,12},{10,14},{12,8},{14,10},{16,20},{18,... | collective-permute-start | bytes 393224 | tf_op jit(solution)/shard_map/ppermute | solution.py:28
  18.4 11.6 %collective-permute-start.4 = (bf16[384,512]{1,0:T(8,128)(2,1)S(1)}, bf16[384,512]{1,0:T(8,128)(2,1)S(1)}, u32[]{:S(2)}, u32[]{:S(2)}) collective-permute-start(bf16[384,512]{1,0:T(8,128)(2,1)S(1)} %get-tuple-element.57), channel_id=1, source_target_pairs={{0,24},{2,26},{4,28},{6,30},{8,0},{10,2},{12,4},{14,6},{16,8},{18,... | collective-permute-start | bytes 1179656 | tf_op jit(solution)/shard_map/ppermute | solution.py:51
  22.5 31.6 %collective-permute-start.6 = (bf16[512,512]{1,0:T(8,128)(2,1)S(1)}, bf16[512,512]{1,0:T(8,128)(2,1)S(1)}, u32[]{:S(2)}, u32[]{:S(2)}) collective-permute-start(bf16[512,512]{1,0:T(8,128)(2,1)S(1)} %get-tuple-element.58.own.own_kv), channel_id=1, source_target_pairs={{0,8},{2,10},{4,12},{6,14},{8,16},{10,18},{12,20},{14,22},{16,24},... | collective-permute-start | bytes 1572872 | tf_op jit(solution)/shard_map/ppermute | solution.py:42
  30.0 24.1 %collective-permute-start.5 = (bf16[384,512]{1,0:T(8,128)(2,1)S(1)}, bf16[384,512]{1,0:T(8,128)(2,1)S(1)}, u32[]{:S(2)}, u32[]{:S(2)}) collective-permute-start(bf16[384,512]{1,0:T(8,128)(2,1)S(1)} %collective-permute-done.4), channel_id=1, source_target_pairs={{0,24},{2,26},{4,28},{6,30},{8,32},{10,34},{12,36},{14,38},{16,40}... | collective-permute-start | bytes 1179656 | tf_op jit(solution)/shard_map/ppermute | solution.py:61
  45.5 8.6 %collective-permute-start.3 = (bf16[128,512]{1,0:T(8,128)(2,1)S(1)}, bf16[128,512]{1,0:T(8,128)(2,1)S(1)}, u32[]{:S(2)}, u32[]{:S(2)}) collective-permute-start(bf16[128,512]{1,0:T(8,128)(2,1)S(1)} %get-tuple-element.56), channel_id=1, source_target_pairs={{0,16},{2,18},{4,20},{6,22},{8,24},{10,26},{12,28},{14,30},{16,32}... | collective-permute-start | bytes 393224 | tf_op jit(solution)/shard_map/ppermute | solution.py:42
  70.5 12.2 %collective-permute-start.13 = (bf16[128,2688]{1,0:T(8,128)(2,1)S(1)}, bf16[128,2688]{1,0:T(8,128)(2,1)S(1)}, u32[]{:S(2)}, u32[]{:S(2)}) collective-permute-start(bf16[128,2688]{1,0:T(8,128)(2,1)S(1)} %get-tuple-element.68), channel_id=1, source_target_pairs={{0,1},{1,0},{2,3},{3,2},{4,5},{5,4},{6,7},{7,6},{8,9},{9,8},{10,11... | collective-permute-start | bytes 2064392 | tf_op jit(solution)/shard_map/ppermute | solution.py:79
  70.9 11.8 %collective-permute-start.28 = (bf16[1344,128]{1,0:T(8,128)(2,1)S(1)}, bf16[1344,128]{1,0:T(8,128)(2,1)S(1)}, u32[]{:S(2)}, u32[]{:S(2)}) collective-permute-start(bf16[1344,128]{1,0:T(8,128)(2,1)S(1)} %dynamic-slice_bitcast_fusion), channel_id=1, source_target_pairs={{0,2},{2,4},{4,6},{6,0},{8,10},{10,12},{12,14},{14,8},{16,18},{18,... | collective-permute-start | bytes 1032200 | tf_op jit(solution)/shard_map/ppermute | solution.py:28
  72.3 20.4 %collective-permute-start.29 = (bf16[1344,128]{1,0:T(8,128)(2,1)S(1)}, bf16[1344,128]{1,0:T(8,128)(2,1)S(1)}, u32[]{:S(2)}, u32[]{:S(2)}) collective-permute-start(bf16[1344,128]{1,0:T(8,128)(2,1)S(1)} %dynamic-slice_bitcast_fusion), channel_id=1, source_target_pairs={{0,4},{2,6},{4,0},{6,2},{8,12},{10,14},{12,8},{14,10},{16,20},{18,... | collective-permute-start | bytes 1032200 | tf_op jit(solution)/shard_map/ppermute | solution.py:28
  75.3 17.6 %collective-permute-start.30 = (bf16[1344,128]{1,0:T(8,128)(2,1)S(1)}, bf16[1344,128]{1,0:T(8,128)(2,1)S(1)}, u32[]{:S(2)}, u32[]{:S(2)}) collective-permute-start(bf16[1344,128]{1,0:T(8,128)(2,1)S(1)} %dynamic-slice_bitcast_fusion), channel_id=1, source_target_pairs={{0,6},{2,0},{4,2},{6,4},{8,14},{10,8},{12,10},{14,12},{16,22},{18,... | collective-permute-start | bytes 1032200 | tf_op jit(solution)/shard_map/ppermute | solution.py:28
  82.6 21.5 %collective-permute-start.31 = (bf16[1344,128]{1,0:T(8,128)(2,1)S(1)}, bf16[1344,128]{1,0:T(8,128)(2,1)S(1)}, u32[]{:S(2)}, u32[]{:S(2)}) collective-permute-start(bf16[1344,128]{1,0:T(8,128)(2,1)S(1)} %collective-permute-done.28.r1), channel_id=1, source_target_pairs={{0,1},{1,0},{2,3},{3,2},{4,5},{5,4},{6,7},{7,6},{8,9},{9,8},{10,11... | collective-permute-start | bytes 1032200 | tf_op jit(solution)/shard_map/ppermute | solution.py:79
  92.9 17.3 %collective-permute-start.32 = (bf16[1344,128]{1,0:T(8,128)(2,1)S(1)}, bf16[1344,128]{1,0:T(8,128)(2,1)S(1)}, u32[]{:S(2)}, u32[]{:S(2)}) collective-permute-start(bf16[1344,128]{1,0:T(8,128)(2,1)S(1)} %collective-permute-done.29.r2), channel_id=1, source_target_pairs={{0,1},{1,0},{2,3},{3,2},{4,5},{5,4},{6,7},{7,6},{8,9},{9,8},{10,11... | collective-permute-start | bytes 1032200 | tf_op jit(solution)/shard_map/ppermute | solution.py:79
  95.0 15.2 %collective-permute-start.33 = (bf16[1344,128]{1,0:T(8,128)(2,1)S(1)}, bf16[1344,128]{1,0:T(8,128)(2,1)S(1)}, u32[]{:S(2)}, u32[]{:S(2)}) collective-permute-start(bf16[1344,128]{1,0:T(8,128)(2,1)S(1)} %collective-permute-done.30.r3), channel_id=1, source_target_pairs={{0,1},{1,0},{2,3},{3,2},{4,5},{5,4},{6,7},{7,6},{8,9},{9,8},{10,11... | collective-permute-start | bytes 1032200 | tf_op jit(solution)/shard_map/ppermute | solution.py:79
  102.0 15.3 %collective-permute-start.17 = (bf16[512,256]{1,0:T(8,128)(2,1)S(1)}, bf16[512,256]{1,0:T(8,128)(2,1)S(1)}, u32[]{:S(2)}, u32[]{:S(2)}) collective-permute-start(bf16[512,256]{1,0:T(8,128)(2,1)S(1)} %get-tuple-element.76), channel_id=1, source_target_pairs={{0,120},{2,122},{4,124},{6,126},{8,0},{10,2},{12,4},{14,6},{16,8},... | collective-permute-start | bytes 786440 | tf_op jit(solution)/shard_map/ppermute | solution.py:42
  102.4 7.7 %collective-permute-start.19 = (bf16[256,256]{1,0:T(8,128)(2,1)S(1)}, bf16[256,256]{1,0:T(8,128)(2,1)S(1)}, u32[]{:S(2)}, u32[]{:S(2)}) collective-permute-start(bf16[256,256]{1,0:T(8,128)(2,1)S(1)} %get-tuple-element.78), channel_id=1, source_target_pairs={{0,8},{2,10},{4,12},{6,14},{8,16},{10,18},{12,20},{14,22},{16,24},... | collective-permute-start | bytes 393224 | tf_op jit(solution)/shard_map/ppermute | solution.py:65
  104.1 12.5 %collective-permute-start.18 = (bf16[256,256]{1,0:T(8,128)(2,1)S(1)}, bf16[256,256]{1,0:T(8,128)(2,1)S(1)}, u32[]{:S(2)}, u32[]{:S(2)}) collective-permute-start(bf16[256,256]{1,0:T(8,128)(2,1)S(1)} %get-tuple-element.77), channel_id=1, source_target_pairs={{0,112},{2,114},{4,116},{6,118},{8,120},{10,122},{12,124},{14,126}... | collective-permute-start | bytes 393224 | tf_op jit(solution)/shard_map/ppermute | solution.py:42
  111.2 12.5 %collective-permute-start.24 = (bf16[128,256]{1,0:T(8,128)(2,1)S(1)}, bf16[128,256]{1,0:T(8,128)(2,1)S(1)}, u32[]{:S(2)}, u32[]{:S(2)}) collective-permute-start(bf16[128,256]{1,0:T(8,128)(2,1)S(1)} %get-tuple-element.84), channel_id=1, source_target_pairs={{0,2},{2,4},{4,6},{6,0},{8,10},{10,12},{12,14},{14,8},{16,18},{18,... | collective-permute-start | bytes 196616 | tf_op jit(solution)/shard_map/ppermute | solution.py:28
  112.2 11.6 %collective-permute-start.25 = (bf16[128,256]{1,0:T(8,128)(2,1)S(1)}, bf16[128,256]{1,0:T(8,128)(2,1)S(1)}, u32[]{:S(2)}, u32[]{:S(2)}) collective-permute-start(bf16[128,256]{1,0:T(8,128)(2,1)S(1)} %get-tuple-element.85), channel_id=1, source_target_pairs={{0,4},{2,6},{4,0},{6,2},{8,12},{10,14},{12,8},{14,10},{16,20},{18,... | collective-permute-start | bytes 196616 | tf_op jit(solution)/shard_map/ppermute | solution.py:28
  116.6 7.8 %collective-permute-start.26 = (bf16[128,256]{1,0:T(8,128)(2,1)S(1)}, bf16[128,256]{1,0:T(8,128)(2,1)S(1)}, u32[]{:S(2)}, u32[]{:S(2)}) collective-permute-start(bf16[128,256]{1,0:T(8,128)(2,1)S(1)} %get-tuple-element.86), channel_id=1, source_target_pairs={{0,6},{2,0},{4,2},{6,4},{8,14},{10,8},{12,10},{14,12},{16,22},{18,... | collective-permute-start | bytes 196616 | tf_op jit(solution)/shard_map/ppermute | solution.py:28
  118.1 9.1 %collective-permute-start.21 = (bf16[128,256]{1,0:T(8,128)(2,1)S(1)}, bf16[128,256]{1,0:T(8,128)(2,1)S(1)}, u32[]{:S(2)}, u32[]{:S(2)}) collective-permute-start(bf16[128,256]{1,0:T(8,128)(2,1)S(1)} %get-tuple-element.80.c1), channel_id=1, source_target_pairs={{0,2},{2,4},{4,6},{6,0},{8,10},{10,12},{12,14},{14,8},{16,18},{18,... | collective-permute-start | bytes 196616 | tf_op jit(solution)/shard_map/ppermute | solution.py:28
  119.4 11.4 %collective-permute-start.22 = (bf16[128,256]{1,0:T(8,128)(2,1)S(1)}, bf16[128,256]{1,0:T(8,128)(2,1)S(1)}, u32[]{:S(2)}, u32[]{:S(2)}) collective-permute-start(bf16[128,256]{1,0:T(8,128)(2,1)S(1)} %get-tuple-element.81.c2), channel_id=1, source_target_pairs={{0,4},{2,6},{4,0},{6,2},{8,12},{10,14},{12,8},{14,10},{16,20},{18,... | collective-permute-start | bytes 196616 | tf_op jit(solution)/shard_map/ppermute | solution.py:28
  123.9 11.8 %collective-permute-start.34 = (bf16[672,256]{1,0:T(8,128)(2,1)S(1)}, bf16[672,256]{1,0:T(8,128)(2,1)S(1)}, u32[]{:S(2)}, u32[]{:S(2)}) collective-permute-start(bf16[672,256]{1,0:T(8,128)(2,1)S(1)} %get-tuple-element.91), channel_id=1, source_target_pairs={{0,32},{2,34},{4,36},{6,38},{8,40},{10,42},{12,44},{14,46},{16,48}... | collective-permute-start | bytes 1032200 | tf_op jit(solution)/shard_map/ppermute | solution.py:38
  124.4 15.6 %collective-permute-start.35 = (bf16[672,256]{1,0:T(8,128)(2,1)S(1)}, bf16[672,256]{1,0:T(8,128)(2,1)S(1)}, u32[]{:S(2)}, u32[]{:S(2)}) collective-permute-start(bf16[672,256]{1,0:T(8,128)(2,1)S(1)} %get-tuple-element.92), channel_id=1, source_target_pairs={{0,64},{2,66},{4,68},{6,70},{8,72},{10,74},{12,76},{14,78},{16,80}... | collective-permute-start | bytes 1032200 | tf_op jit(solution)/shard_map/ppermute | solution.py:38
  127.2 12.8 %collective-permute-start.36 = (bf16[672,256]{1,0:T(8,128)(2,1)S(1)}, bf16[672,256]{1,0:T(8,128)(2,1)S(1)}, u32[]{:S(2)}, u32[]{:S(2)}) collective-permute-start(bf16[672,256]{1,0:T(8,128)(2,1)S(1)} %get-tuple-element.93), channel_id=1, source_target_pairs={{0,96},{2,98},{4,100},{6,102},{8,104},{10,106},{12,108},{14,110},{... | collective-permute-start | bytes 1032200 | tf_op jit(solution)/shard_map/ppermute | solution.py:38
  133.4 21.1 %collective-permute-start.27 = (bf16[1344,128]{1,0:T(8,128)(2,1)S(1)}, bf16[1344,128]{1,0:T(8,128)(2,1)S(1)}, u32[]{:S(2)}, u32[]{:S(2)}) collective-permute-start(bf16[1344,128]{1,0:T(8,128)(2,1)S(1)} %get-tuple-element.88), channel_id=1, source_target_pairs={{0,1},{1,0},{2,3},{3,2},{4,5},{5,4},{6,7},{7,6},{8,9},{9,8},{10,11... | collective-permute-start | bytes 1032200 | tf_op jit(solution)/shard_map/ppermute | solution.py:79
  (40 other events, 314.8 us)
